TPU v7x, 32 devices: a whole 2x2x4 slice. The times are simulated.
32 devices in a mesh: grp: 4 (over y, x), edge: 8 (over z, core).
Axes of the slice: x: 2, y: 2, z: 4, core: 2. Of those that a mesh axis runs over, the one named last changes fastest.
Arguments:
- edge_embed: bfloat16 [65536, 512], P(('grp', 'edge')), may hold values from -6 to 6
- atom_embed: bfloat16 [4096, 256], P(('grp', 'edge')), may hold values from -6 to 6
- radial_basis: bfloat16 [65536, 128], P(('grp', 'edge')), may hold values from 0 to 1
- triplet_basis: bfloat16 [65536, 256], P(('grp', 'edge')), may hold values from -6 to 6
- quadruplet_basis: bfloat16 [65536, 256], P(('grp', 'edge')), may hold values from -6 to 6
- triplet_source_row: int32 [65536, 16], P(('grp', 'edge')), may hold values from 0 to 2175, as said below
- triplet_mask: int32 [65536, 16], P(('grp', 'edge')), may hold values 0 or 1
- quadruplet_source_row: int32 [65536, 8], P(('grp', 'edge')), may hold values from 0 to 2175, as said below
- quadruplet_mask: int32 [65536, 8], P(('grp', 'edge')), may hold values 0 or 1
- edge_target_atom: int32 [32, 2048], P(('grp', 'edge')), may hold values from 0 to 127, never falling along the last dimension, each value on 1 to 30 neighbouring positions
- borrowed_edges: int32 [32, 8, 16], P(('grp', 'edge')), may hold values from 0 to 16383, as said below
- w_source_trip: bfloat16 [512, 512], replicated, may hold values from -0.25 to 0.25
- w_rbf_trip: bfloat16 [128, 512], replicated, may hold values from -0.5 to 0.5
- w_down_trip: bfloat16 [512, 64], replicated, may hold values from -0.25 to 0.25
- w_source_quad: bfloat16 [512, 512], replicated, may hold values from -0.25 to 0.25
- w_rbf_quad: bfloat16 [128, 512], replicated, may hold values from -0.5 to 0.5
- w_down_quad: bfloat16 [512, 32], replicated, may hold values from -0.25 to 0.25
- triplet_bilinear_weight: bfloat16 [1024, 64], replicated, may hold values from -0.1875 to 0.1875
- w_up_trip: bfloat16 [64, 512], replicated, may hold values from -0.75 to 0.75
- w_bilinear_quad: bfloat16 [1024, 32], replicated, may hold values from -0.1875 to 0.1875
- w_up_quad: bfloat16 [32, 512], replicated, may hold values from -1 to 1
- w_skip: bfloat16 [512, 512], replicated, may hold values from -0.25 to 0.25
- w_res_first: bfloat16 [512, 512], replicated, may hold values from -0.25 to 0.25
- w_res_second: bfloat16 [512, 512], replicated, may hold values from -0.25 to 0.25
- w_rbf_atom: bfloat16 [128, 512], replicated, may hold values from -0.5 to 0.5
- w_atom: bfloat16 [512, 256], replicated, may hold values from -0.25 to 0.25
- w_concat: bfloat16 [768, 512], replicated, may hold values from -0.21875 to 0.21875
- w_rbf_out: bfloat16 [128, 512], replicated, may hold values from -0.5 to 0.5
- w_out: bfloat16 [512, 256], replicated, may hold values from -0.25 to 0.25
- edge_cotangent: bfloat16 [65536, 512], P(('grp', 'edge')), may hold values from -6 to 6
- atom_cotangent: bfloat16 [4096, 256], P(('grp', 'edge')), may hold values from -6 to 6
- output_cotangent: bfloat16 [4096, 256], P(('grp', 'edge')), may hold values from -6 to 6
Outputs:
- edge_update: bfloat16 [65536, 512], P(('grp', 'edge'))
- atom_update: bfloat16 [4096, 256], P(('grp', 'edge'))
- atom_output: bfloat16 [4096, 256], P(('grp', 'edge'))
- grad_edge_embed: bfloat16 [65536, 512], P(('grp', 'edge'))
- grad_atom_embed: bfloat16 [4096, 256], P(('grp', 'edge'))
- grad_w_source_trip: float32 [512, 512], P('edge')
- grad_w_rbf_trip: float32 [128, 512], P('edge')
- grad_w_down_trip: float32 [512, 64], P('edge')
- grad_w_source_quad: float32 [512, 512], P('edge')
- grad_w_rbf_quad: float32 [128, 512], P('edge')
- grad_w_down_quad: float32 [512, 32], P('edge')
- grad_w_bilinear_trip: float32 [1024, 64], P('edge')
- grad_w_up_trip: float32 [64, 512], P(None, 'edge')
- grad_w_bilinear_quad: float32 [1024, 32], P('edge')
- grad_w_up_quad: float32 [32, 512], P(None, 'edge')
- grad_w_skip: float32 [512, 512], P('edge')
- grad_w_res_first: float32 [512, 512], P('edge')
- grad_w_res_second: float32 [512, 512], P('edge')
- grad_w_rbf_atom: float32 [128, 512], P('edge')
- grad_w_atom: float32 [512, 256], P('edge')
- grad_w_concat: float32 [768, 512], P('edge')
- grad_w_rbf_out: float32 [128, 512], P('edge')
- grad_w_out: float32 [512, 256], P('edge')
Inputs may be any that keep to these rules, and one draw needn't show every extreme that they name: `borrowed_edges`: entry (b, p, j) is the id, within the structure group of block b, of an edge of that group's block p: it lies in [p * 2048, (p + 1) * 2048); the 16 entries of one (b, p) are distinct. `triplet_source_row`: A value v below 2048 is row v of the own block; a value 2048 + p * 16 + j reads entry (p, j) of the block's borrowed_edges, with p never the block's own index within its group. `quadruplet_source_row`: as for triplet_source_row.
All inputs are finite; a program needn't handle non-finite values. No bound on the sum of `triplet_mask` or of `quadruplet_mask` on one device may be relied on, other than what follows from the above.
Results may differ from a plain program's by a relative error of at most 0.02.
Values may be sent and summed in bfloat16 or wider, within the bound.
No kernel may reach another device: no remote copies, remote signals or barrier semaphores. Data moves between devices by JAX's collectives and lax.ppermute only.
A program may use at most 320 MiB of HBM per device.

v0:
```python
import math

import jax
import jax.numpy as jnp
from jax import lax
from jax.sharding import PartitionSpec as P

HALF_ROOT = 1.0 / math.sqrt(2.0)
THIRD_ROOT = 1.0 / math.sqrt(3.0)


def silu_slope(value):
    sigma = jax.nn.sigmoid(value)
    return sigma * (1.0 + value * (1.0 - sigma))


def product(operand, weight):
    return jnp.dot(operand, weight, preferred_element_type=jnp.float32)


def outer_sum(operand, gradient):
    return lax.dot_general(
        operand, gradient, (((0,), (0,)), ((), ())), preferred_element_type=jnp.float32
    )


def against(gradient, weight):
    return lax.dot_general(
        gradient, weight, (((1,), (1,)), ((), ())), preferred_element_type=jnp.float32
    )


def exact_rows(onehot, values):
    return jnp.dot(onehot, values, precision=lax.Precision.HIGHEST)


def exact_cols(onehot, values):
    return lax.dot_general(
        onehot, values, (((0,), (0,)), ((), ())), precision=lax.Precision.HIGHEST
    )


def source_forward(edge_rows, radial, weights):
    w_source_trip, w_rbf_trip, w_down_trip, w_source_quad, w_rbf_quad, w_down_quad = weights
    pre_trip = product(edge_rows, w_source_trip)
    radial_trip = product(radial, w_rbf_trip)
    mix_trip = (jax.nn.silu(pre_trip) * radial_trip).astype(jnp.bfloat16)
    down_trip = product(mix_trip, w_down_trip)
    pre_quad = product(edge_rows, w_source_quad)
    radial_quad = product(radial, w_rbf_quad)
    mix_quad = (jax.nn.silu(pre_quad) * radial_quad).astype(jnp.bfloat16)
    down_quad = product(mix_quad, w_down_quad)
    source_table = jnp.concatenate(
        [jax.nn.silu(down_trip).astype(jnp.bfloat16), jax.nn.silu(down_quad).astype(jnp.bfloat16)],
        axis=1,
    )
    return (
        source_table,
        (pre_trip, radial_trip, mix_trip, down_trip, pre_quad, radial_quad, mix_quad, down_quad),
    )


def branch_backward(
    edge_rows, radial, w_source, w_down, pre_source, radial_part, mixed_part, down_part, grad_down
):
    rounded_down = (grad_down * silu_slope(down_part)).astype(jnp.bfloat16)
    grad_w_down = outer_sum(mixed_part, rounded_down)
    grad_mix = against(rounded_down, w_down)
    rounded_source = (grad_mix * radial_part * silu_slope(pre_source)).astype(jnp.bfloat16)
    rounded_radial = (grad_mix * jax.nn.silu(pre_source)).astype(jnp.bfloat16)
    return (
        against(rounded_source, w_source),
        outer_sum(edge_rows, rounded_source),
        outer_sum(radial, rounded_radial),
        grad_w_down,
    )


def bilinear_sum(source_table, sources, slot_mask, coefficients):
    edge_count, slots = sources.shape
    coefficient = coefficients.reshape(edge_count, slots, -1)
    picked = jnp.take(source_table, sources.reshape(-1), axis=0).reshape(edge_count, slots, -1)
    picked = picked * slot_mask[:, :, None].astype(jnp.bfloat16)
    summed = jnp.einsum("ekc,eki->eci", coefficient, picked, preferred_element_type=jnp.float32)
    return summed.reshape(edge_count, -1).astype(jnp.bfloat16)


def bilinear_back(rounded_sum, sources, slot_mask, coefficients, table_rows):
    edge_count, slots = sources.shape
    coefficient = coefficients.reshape(edge_count, slots, -1)
    grad_sum = rounded_sum.reshape(edge_count, coefficient.shape[2], -1)
    picked_grad = jnp.einsum(
        "ekc,eci->eki", coefficient, grad_sum, preferred_element_type=jnp.float32
    )
    picked_grad = picked_grad * slot_mask[:, :, None].astype(jnp.float32)
    column_count = picked_grad.shape[2]
    zeroed = jnp.zeros((table_rows, column_count), jnp.float32)
    return zeroed.at[sources.reshape(-1)].add(picked_grad.reshape(-1, column_count))


def per_device(
    edge_embed,
    atom_embed,
    radial_basis,
    triplet_basis,
    quadruplet_basis,
    triplet_source_row,
    triplet_mask,
    quadruplet_source_row,
    quadruplet_mask,
    edge_target_atom,
    borrowed_edges,
    w_source_trip,
    w_rbf_trip,
    w_down_trip,
    w_source_quad,
    w_rbf_quad,
    w_down_quad,
    triplet_bilinear_weight,
    w_up_trip,
    w_bilinear_quad,
    w_up_quad,
    w_skip,
    w_res_first,
    w_res_second,
    w_rbf_atom,
    w_atom,
    w_concat,
    w_rbf_out,
    w_out,
    edge_cotangent,
    atom_cotangent,
    output_cotangent,
):
    edge_count = edge_embed.shape[0]
    atom_count = atom_embed.shape[0]
    peer_count = lax.axis_size("edge")
    capacity = borrowed_edges.shape[2]
    source_weights = (
        w_source_trip,
        w_rbf_trip,
        w_down_trip,
        w_source_quad,
        w_rbf_quad,
        w_down_quad,
    )
    wanted = borrowed_edges[0] - (jnp.arange(peer_count, dtype=jnp.int32) * edge_count)[:, None]
    asked = lax.all_to_all(wanted, "edge", split_axis=0, concat_axis=0, tiled=True)
    asked_flat = asked.reshape(-1)
    local_table, kept = source_forward(edge_embed, radial_basis, source_weights)
    outgoing = jnp.take(local_table, asked_flat, axis=0).reshape(peer_count, -1)
    ghost_table = lax.all_to_all(outgoing, "edge", split_axis=0, concat_axis=0, tiled=True)
    source_table = jnp.concatenate(
        [local_table, ghost_table.reshape(peer_count * capacity, -1)], axis=0
    )
    table_rows = source_table.shape[0]
    trip_width = w_down_trip.shape[1]
    trip_sum = bilinear_sum(
        source_table[:, :trip_width], triplet_source_row, triplet_mask, triplet_basis
    )
    quad_sum = bilinear_sum(
        source_table[:, trip_width:], quadruplet_source_row, quadruplet_mask, quadruplet_basis
    )
    pre_bil_trip = product(trip_sum, triplet_bilinear_weight)
    pre_bil_quad = product(quad_sum, w_bilinear_quad)
    hidden_trip = jax.nn.silu(pre_bil_trip).astype(jnp.bfloat16)
    hidden_quad = jax.nn.silu(pre_bil_quad).astype(jnp.bfloat16)
    pre_up_trip = product(hidden_trip, w_up_trip)
    pre_up_quad = product(hidden_quad, w_up_quad)
    pre_skip = product(edge_embed, w_skip)
    mixed = (
        jax.nn.silu(pre_skip) + jax.nn.silu(pre_up_trip) + jax.nn.silu(pre_up_quad)
    ) * THIRD_ROOT
    mixed_low = mixed.astype(jnp.bfloat16)
    pre_res = product(mixed_low, w_res_first)
    res_hidden = jax.nn.silu(pre_res).astype(jnp.bfloat16)
    pre_res_second = product(res_hidden, w_res_second)
    merged = (
        edge_embed.astype(jnp.float32) + (mixed + jax.nn.silu(pre_res_second)) * HALF_ROOT
    ) * HALF_ROOT
    onehot_float = (
        edge_target_atom[0][:, None] == jnp.arange(atom_count, dtype=jnp.int32)[None, :]
    ).astype(jnp.float32)
    onehot_low = onehot_float.astype(jnp.bfloat16)
    radial_atom = product(radial_basis, w_rbf_atom)
    weighted = (merged * radial_atom).astype(jnp.bfloat16)
    gathered_low = outer_sum(onehot_low, weighted).astype(jnp.bfloat16)
    pre_atom = product(gathered_low, w_atom)
    atom_new = (atom_embed.astype(jnp.float32) + jax.nn.silu(pre_atom)) * HALF_ROOT
    atom_low = atom_new.astype(jnp.bfloat16)
    concat_rows = jnp.concatenate(
        [product(onehot_low, atom_low).astype(jnp.bfloat16), merged.astype(jnp.bfloat16)], axis=1
    )
    pre_concat = product(concat_rows, w_concat)
    edge_new = (merged + jax.nn.silu(pre_concat)) * HALF_ROOT
    radial_out = product(radial_basis, w_rbf_out)
    out_weighted = (edge_new * radial_out).astype(jnp.bfloat16)
    out_low = outer_sum(onehot_low, out_weighted).astype(jnp.bfloat16)
    atom_output = product(out_low, w_out)
    grad_w_out = outer_sum(out_low, output_cotangent)
    grad_out_weighted = exact_rows(onehot_float, against(output_cotangent, w_out))
    grad_edge_new = edge_cotangent.astype(jnp.float32) + grad_out_weighted * radial_out
    rounded_radial_out = (grad_out_weighted * edge_new).astype(jnp.bfloat16)
    grad_w_rbf_out = outer_sum(radial_basis, rounded_radial_out)
    rounded_concat = (grad_edge_new * HALF_ROOT * silu_slope(pre_concat)).astype(jnp.bfloat16)
    grad_w_concat = outer_sum(concat_rows, rounded_concat)
    grad_concat = against(rounded_concat, w_concat)
    atom_width = atom_embed.shape[1]
    grad_merged = grad_edge_new * HALF_ROOT + grad_concat[:, atom_width:]
    grad_atom_new = atom_cotangent.astype(jnp.float32) + exact_cols(
        onehot_float, grad_concat[:, :atom_width]
    )
    rounded_atom = (grad_atom_new * HALF_ROOT * silu_slope(pre_atom)).astype(jnp.bfloat16)
    grad_w_atom = outer_sum(gathered_low, rounded_atom)
    grad_weighted = exact_rows(onehot_float, against(rounded_atom, w_atom))
    grad_merged = grad_merged + grad_weighted * radial_atom
    rounded_radial_atom = (grad_weighted * merged).astype(jnp.bfloat16)
    grad_w_rbf_atom = outer_sum(radial_basis, rounded_radial_atom)
    rounded_res_second = (grad_merged * 0.5 * silu_slope(pre_res_second)).astype(jnp.bfloat16)
    grad_w_res_second = outer_sum(res_hidden, rounded_res_second)
    rounded_res = (against(rounded_res_second, w_res_second) * silu_slope(pre_res)).astype(
        jnp.bfloat16
    )
    grad_w_res_first = outer_sum(mixed_low, rounded_res)
    grad_mixed = (grad_merged * 0.5 + against(rounded_res, w_res_first)) * THIRD_ROOT
    rounded_skip = (grad_mixed * silu_slope(pre_skip)).astype(jnp.bfloat16)
    rounded_up_trip = (grad_mixed * silu_slope(pre_up_trip)).astype(jnp.bfloat16)
    rounded_up_quad = (grad_mixed * silu_slope(pre_up_quad)).astype(jnp.bfloat16)
    grad_w_skip = outer_sum(edge_embed, rounded_skip)
    grad_w_up_trip = outer_sum(hidden_trip, rounded_up_trip)
    grad_w_up_quad = outer_sum(hidden_quad, rounded_up_quad)
    rounded_bil_trip = (against(rounded_up_trip, w_up_trip) * silu_slope(pre_bil_trip)).astype(
        jnp.bfloat16
    )
    rounded_bil_quad = (against(rounded_up_quad, w_up_quad) * silu_slope(pre_bil_quad)).astype(
        jnp.bfloat16
    )
    grad_w_bilinear_trip = outer_sum(trip_sum, rounded_bil_trip)
    grad_w_bilinear_quad = outer_sum(quad_sum, rounded_bil_quad)
    rounded_trip_sum = against(rounded_bil_trip, triplet_bilinear_weight).astype(jnp.bfloat16)
    rounded_quad_sum = against(rounded_bil_quad, w_bilinear_quad).astype(jnp.bfloat16)
    grad_table = jnp.concatenate(
        [
            bilinear_back(
                rounded_trip_sum, triplet_source_row, triplet_mask, triplet_basis, table_rows
            ),
            bilinear_back(
                rounded_quad_sum,
                quadruplet_source_row,
                quadruplet_mask,
                quadruplet_basis,
                table_rows,
            ),
        ],
        axis=1,
    )
    returned = lax.all_to_all(
        grad_table[edge_count:].reshape(peer_count, -1).astype(jnp.bfloat16),
        "edge",
        split_axis=0,
        concat_axis=0,
        tiled=True,
    ).astype(jnp.float32)
    grad_local = (
        grad_table[:edge_count].at[asked_flat].add(returned.reshape(peer_count * capacity, -1))
    )
    pre_trip, radial_trip, mix_trip, down_trip, pre_quad, radial_quad, mix_quad, down_quad = kept
    back_trip = branch_backward(
        edge_embed,
        radial_basis,
        w_source_trip,
        w_down_trip,
        pre_trip,
        radial_trip,
        mix_trip,
        down_trip,
        grad_local[:, :trip_width],
    )
    back_quad = branch_backward(
        edge_embed,
        radial_basis,
        w_source_quad,
        w_down_quad,
        pre_quad,
        radial_quad,
        mix_quad,
        down_quad,
        grad_local[:, trip_width:],
    )
    grad_edge = (
        grad_merged * HALF_ROOT + against(rounded_skip, w_skip) + back_trip[0] + back_quad[0]
    )
    pieces = (
        lax.psum_scatter(back_trip[1], "edge", scatter_dimension=0, tiled=True),
        lax.psum_scatter(back_trip[2], "edge", scatter_dimension=0, tiled=True),
        lax.psum_scatter(back_trip[3], "edge", scatter_dimension=0, tiled=True),
        lax.psum_scatter(back_quad[1], "edge", scatter_dimension=0, tiled=True),
        lax.psum_scatter(back_quad[2], "edge", scatter_dimension=0, tiled=True),
        lax.psum_scatter(back_quad[3], "edge", scatter_dimension=0, tiled=True),
        lax.psum_scatter(grad_w_bilinear_trip, "edge", scatter_dimension=0, tiled=True),
        lax.psum_scatter(grad_w_up_trip, "edge", scatter_dimension=1, tiled=True),
        lax.psum_scatter(grad_w_bilinear_quad, "edge", scatter_dimension=0, tiled=True),
        lax.psum_scatter(grad_w_up_quad, "edge", scatter_dimension=1, tiled=True),
        lax.psum_scatter(grad_w_skip, "edge", scatter_dimension=0, tiled=True),
        lax.psum_scatter(grad_w_res_first, "edge", scatter_dimension=0, tiled=True),
        lax.psum_scatter(grad_w_res_second, "edge", scatter_dimension=0, tiled=True),
        lax.psum_scatter(grad_w_rbf_atom, "edge", scatter_dimension=0, tiled=True),
        lax.psum_scatter(grad_w_atom, "edge", scatter_dimension=0, tiled=True),
        lax.psum_scatter(grad_w_concat, "edge", scatter_dimension=0, tiled=True),
        lax.psum_scatter(grad_w_rbf_out, "edge", scatter_dimension=0, tiled=True),
        lax.psum_scatter(grad_w_out, "edge", scatter_dimension=0, tiled=True),
    )
    shares = (
        lax.psum(pieces[0].astype(jnp.bfloat16), "grp").astype(jnp.float32),
        lax.psum(pieces[1].astype(jnp.bfloat16), "grp").astype(jnp.float32),
        lax.psum(pieces[2].astype(jnp.bfloat16), "grp").astype(jnp.float32),
        lax.psum(pieces[3].astype(jnp.bfloat16), "grp").astype(jnp.float32),
        lax.psum(pieces[4].astype(jnp.bfloat16), "grp").astype(jnp.float32),
        lax.psum(pieces[5].astype(jnp.bfloat16), "grp").astype(jnp.float32),
        lax.psum(pieces[6].astype(jnp.bfloat16), "grp").astype(jnp.float32),
        lax.psum(pieces[7].astype(jnp.bfloat16), "grp").astype(jnp.float32),
        lax.psum(pieces[8].astype(jnp.bfloat16), "grp").astype(jnp.float32),
        lax.psum(pieces[9].astype(jnp.bfloat16), "grp").astype(jnp.float32),
        lax.psum(pieces[10].astype(jnp.bfloat16), "grp").astype(jnp.float32),
        lax.psum(pieces[11].astype(jnp.bfloat16), "grp").astype(jnp.float32),
        lax.psum(pieces[12].astype(jnp.bfloat16), "grp").astype(jnp.float32),
        lax.psum(pieces[13].astype(jnp.bfloat16), "grp").astype(jnp.float32),
        lax.psum(pieces[14].astype(jnp.bfloat16), "grp").astype(jnp.float32),
        lax.psum(pieces[15].astype(jnp.bfloat16), "grp").astype(jnp.float32),
        lax.psum(pieces[16].astype(jnp.bfloat16), "grp").astype(jnp.float32),
        lax.psum(pieces[17].astype(jnp.bfloat16), "grp").astype(jnp.float32),
    )
    return (
        edge_new.astype(jnp.bfloat16),
        atom_new.astype(jnp.bfloat16),
        atom_output.astype(jnp.bfloat16),
        grad_edge.astype(jnp.bfloat16),
        (grad_atom_new * HALF_ROOT).astype(jnp.bfloat16),
        shares[0],
        shares[1],
        shares[2],
        shares[3],
        shares[4],
        shares[5],
        shares[6],
        shares[7],
        shares[8],
        shares[9],
        shares[10],
        shares[11],
        shares[12],
        shares[13],
        shares[14],
        shares[15],
        shares[16],
        shares[17],
    )


def solution(mesh):
    placed = (
        P(("grp", "edge"), None),
        P(("grp", "edge"), None),
        P(("grp", "edge"), None),
        P(("grp", "edge"), None),
        P(("grp", "edge"), None),
        P(("grp", "edge"), None),
        P(("grp", "edge"), None),
        P(("grp", "edge"), None),
        P(("grp", "edge"), None),
        P(("grp", "edge"), None),
        P(("grp", "edge"), None, None),
        P(),
        P(),
        P(),
        P(),
        P(),
        P(),
        P(),
        P(),
        P(),
        P(),
        P(),
        P(),
        P(),
        P(),
        P(),
        P(),
        P(),
        P(),
        P(("grp", "edge"), None),
        P(("grp", "edge"), None),
        P(("grp", "edge"), None),
    )
    return jax.shard_map(
        per_device,
        mesh=mesh,
        in_specs=placed,
        out_specs=(
            P(("grp", "edge"), None),
            P(("grp", "edge"), None),
            P(("grp", "edge"), None),
            P(("grp", "edge"), None),
            P(("grp", "edge"), None),
            P("edge", None),
            P("edge", None),
            P("edge", None),
            P("edge", None),
            P("edge", None),
            P("edge", None),
            P("edge", None),
            P(None, "edge"),
            P("edge", None),
            P(None, "edge"),
            P("edge", None),
            P("edge", None),
            P("edge", None),
            P("edge", None),
            P("edge", None),
            P("edge", None),
            P("edge", None),
            P("edge", None),
        ),
        check_vma=False,
    )
```

profile of v0, /device:TPU:0, one launch (start us, length us, event | category | flops | bytes accessed | tf_op | source)
XLA Modules:
  0.0 1469.7 jit_solution(3962303661131372811)
XLA Ops:
  8.7 6.4 all-to-all-start
  71.9 5.6 all-to-all-start.1
  103.0 8.5 copy.226
  113.4 114.2 %gather_fusion.1 = bf16[32768,64]{1,0:T(8,128)(2,1)} fusion(bf16[2176,64]{1,0:T(8,128)(2,1)S(1)} %copy.196, s32[32768]{0:T(1024)S(1)} %copy-done.43), kind=kCustom, calls=%fused_computation.1 | custom fusion | bytes 8519680 | tf_op jit(solution)/shard_map/jit(_take)/gather | solution.py:82
  227.5 17.2 %convert_bitcast_fusion.1 = bf16[2048,16,64]{2,1,0:T(8,128)(2,1)} fusion(bf16[2048,16,16]{2,1,0:T(8,128)(2,1)} %copy.226, bf16[2048,16,64]{2,1,0:T(8,128)(2,1)} %bitcast.169, pred[2048,16]{1,0:T(8,128)(4,1)S(1)} %copy-done.58, bf16[2048,16]{1,0:T(8,128)(2,1)S(1)} %copy-done.47), kind=kOutput, calls=%fused_computation.11 | convolution fusion | flops 79691776 | bytes 9535488 | tf_op jit(solution)/shard_map/ekc,eki->eci/dot_general | solution.py:84
  244.7 9.8 copy.200
  254.6 57.4 %gather_fusion.2 = bf16[16384,32]{1,0:T(8,128)(2,1)} fusion(bf16[2176,32]{1,0:T(8,128)(2,1)S(1)} %copy.203, s32[16384]{0:T(1024)S(1)} %copy-done.53), kind=kCustom, calls=%fused_computation.2 | custom fusion | bytes 2162688 | tf_op jit(solution)/shard_map/jit(_take)/gather | solution.py:82
  312.0 13.9 convert_bitcast_fusion
  325.8 20.0 %copy.207 = bf16[2048,32,32]{0,2,1:T(8,128)(2,1)} copy(bf16[2048,32,32]{1,2,0:T(8,128)(2,1)} %convert_bitcast_fusion) | data formatting | bytes 8388608 | tf_op jit(solution)/shard_map/convert_element_type | solution.py:85
  352.3 4.8 add_multiply_fusion.4
  371.2 7.0 fusion.71
  385.4 5.5 copy.292
  394.9 10.7 multiply_convert_fusion.10
  412.1 9.1 multiply_convert_fusion.8
  431.8 10.9 copy.225
  442.7 23.0 %copy.228 = bf16[2048,32,32]{2,1,0:T(8,128)(2,1)} copy(bf16[2048,32,32]{0,2,1:T(8,128)(2,1)} %bitcast.165) | data formatting | bytes 8388608 | tf_op jit(solution)/shard_map/reshape | solution.py:91
  465.8 11.3 fusion.84
  477.1 15.0 %convolution_multiply_fusion = f32[2048,64,16]{1,2,0:T(8,128)} fusion(bf16[2048,16,16]{2,1,0:T(8,128)(2,1)} %copy.226, bf16[2048,16,64]{2,1,0:T(8,128)(2,1)} %copy.225, f32[2048,16]{1,0:T(8,128)S(1)} %copy-done.20), kind=kOutput, calls=%fused_computation.7 | convolution fusion | flops 69206016 | bytes 13762560 | tf_op jit(solution)/shard_map/ekc,eci->eki/dot_general | solution.py:92
  492.1 174.5 %scatter_custom_fusion = f32[2176,64]{1,0:T(8,128)S(1)} fusion(s32[32768]{0:T(1024)} %bitcast.173, f32[32768,64]{1,0:T(8,128)} %bitcast.167, f32[]{:T(128)} %constant.82.clone.1), kind=kCustom, calls=%fused_computation.103 | custom fusion | flops 2097152 | bytes 557568 | tf_op jit(solution)/shard_map/scatter-add | solution.py:98
  666.6 93.0 %scatter_custom_fusion.1 = f32[2176,32]{1,0:T(8,128)} fusion(s32[16384]{0:T(1024)} %bitcast.181, f32[2048,32,8]{1,2,0:T(8,128)} %fusion.84, f32[2048,8]{1,0:T(8,128)S(1)} %copy-done.23, f32[]{:T(128)} %constant.82.clone.1), kind=kCustom, calls=%fused_computation.8 | custom fusion | flops 1048576 | bytes 8733184 | tf_op jit(solution)/shard_map/scatter-add | solution.py:98
  762.0 5.2 all-to-all-start.2
  801.6 4.3 fusion.87
  806.0 5.8 multiply_convert_fusion.5
  814.0 6.0 multiply_convert_fusion.4
  820.1 4.7 fusion.33
  825.8 4.4 fusion.35
  836.4 5.3 fusion.46
  861.4 5.7 fusion.29
  870.5 5.0 fusion.94
  879.9 16.5 %reduce-scatter.43.cloned.1.call-done = f32[128,32]{0,1:T(8,128)} async-done(((f32[1024,32]{0,1:T(8,128)}), f32[128,32]{0,1:T(8,128)}) %reduce-scatter.43.cloned.1.call-update) | async-done | bytes 16400 | tf_op jit(solution)/shard_map/reduce_scatter | solution.py:302
  897.7 29.7 %reduce-scatter.39.cloned.1.call-done = f32[64,64]{1,0:T(8,128)} async-done(((f32[512,64]{1,0:T(8,128)}), f32[64,64]{1,0:T(8,128)}) %reduce-scatter.39.cloned.1.call-update) | async-done | bytes 16400 | tf_op jit(solution)/shard_map/reduce_scatter | solution.py:296
  928.8 29.7 %reduce-scatter.73.cloned.1.call-done = f32[16,512]{1,0:T(8,128)} async-done(((f32[128,512]{1,0:T(8,128)}), f32[16,512]{1,0:T(8,128)}) %reduce-scatter.73.cloned.1.call-update) | async-done | bytes 32784
  960.0 29.7 %reduce-scatter.71.cloned.1.call-done = f32[16,512]{1,0:T(8,128)} async-done(((f32[128,512]{1,0:T(8,128)}), f32[16,512]{1,0:T(8,128)}) %reduce-scatter.71.cloned.1.call-update) | async-done | bytes 32784
  991.3 29.7 %reduce-scatter.41.cloned.1.call-done = f32[128,64]{0,1:T(8,128)} async-done(((f32[1024,64]{0,1:T(8,128)}), f32[128,64]{0,1:T(8,128)}) %reduce-scatter.41.cloned.1.call-update) | async-done | bytes 32784 | tf_op jit(solution)/shard_map/reduce_scatter | solution.py:300
  1022.3 29.8 %reduce-scatter.57.cloned.1.call-done = f32[16,512]{1,0:T(8,128)} async-done(((f32[128,512]{1,0:T(8,128)}), f32[16,512]{1,0:T(8,128)}) %reduce-scatter.57.cloned.1.call-update) | async-done | bytes 32784
  1053.6 29.5 %reduce-scatter.61.cloned.1.call-done = f32[16,512]{1,0:T(8,128)} async-done(((f32[128,512]{1,0:T(8,128)}), f32[16,512]{1,0:T(8,128)}) %reduce-scatter.61.cloned.1.call-update) | async-done | bytes 32784
  1084.7 30.2 %reduce-scatter.53.cloned.1.call-done = f32[64,256]{1,0:T(8,128)} async-done(((f32[512,256]{1,0:T(8,128)}), f32[64,256]{1,0:T(8,128)}) %reduce-scatter.53.cloned.1.call-update) | async-done | bytes 65552 | tf_op jit(solution)/shard_map/reduce_scatter | solution.py:311
  1116.4 30.1 %reduce-scatter.49.cloned.1.call-done = f32[64,256]{1,0:T(8,128)} async-done(((f32[512,256]{1,0:T(8,128)}), f32[64,256]{1,0:T(8,128)}) %reduce-scatter.49.cloned.1.call-update) | async-done | bytes 65552 | tf_op jit(solution)/shard_map/reduce_scatter | solution.py:308
  1148.1 4.4 fusion.95
  1152.4 27.1 %reduce-scatter.47.cloned.1.call-done = f32[64,512]{1,0:T(8,128)} async-done(((f32[512,512]{1,0:T(8,128)}), f32[64,512]{1,0:T(8,128)}) %reduce-scatter.47.cloned.1.call-update) | async-done | bytes 131088 | tf_op jit(solution)/shard_map/reduce_scatter | solution.py:306
  1181.0 31.6 %reduce-scatter.45.cloned.1.call-done = f32[64,512]{1,0:T(8,128)} async-done(((f32[512,512]{1,0:T(8,128)}), f32[64,512]{1,0:T(8,128)}) %reduce-scatter.45.cloned.1.call-update) | async-done | bytes 131088 | tf_op jit(solution)/shard_map/reduce_scatter | solution.py:305
  1214.1 31.6 %reduce-scatter.69.cloned.1.call-done = f32[64,512]{1,0:T(8,128)} async-done(((f32[512,512]{1,0:T(8,128)}), f32[64,512]{1,0:T(8,128)}) %reduce-scatter.69.cloned.1.call-update) | async-done | bytes 131088
  1247.4 31.1 %reduce-scatter.55.cloned.1.call-done = f32[64,512]{1,0:T(8,128)} async-done(((f32[512,512]{1,0:T(8,128)}), f32[64,512]{1,0:T(8,128)}) %reduce-scatter.55.cloned.1.call-update) | async-done | bytes 131088
  1280.1 31.5 %reduce-scatter.59.cloned.1.call-done = f32[64,512]{1,0:T(8,128)} async-done(((f32[512,512]{1,0:T(8,128)}), f32[64,512]{1,0:T(8,128)}) %reduce-scatter.59.cloned.1.call-update) | async-done | bytes 131088
  1313.3 32.7 %reduce-scatter.51.cloned.1.call-done = f32[96,512]{1,0:T(8,128)} async-done(((f32[768,512]{1,0:T(8,128)}), f32[96,512]{1,0:T(8,128)}) %reduce-scatter.51.cloned.1.call-update) | async-done | bytes 196624 | tf_op jit(solution)/shard_map/reduce_scatter | solution.py:309
  1347.7 6.7 add_convert_fusion
  1356.8 43.7 %all-reduce.5.cloned.1.call-done = (bf16[16,512]{0,1:T(8,128)(2,1)}, bf16[16,512]{0,1:T(8,128)(2,1)}, bf16[16,512]{0,1:T(8,128)(2,1)}, bf16[16,512]{0,1:T(8,128)...) async-done(((bf16[16,512]{0,1:T(8,128)(2,1)}, ...) | async-done | bytes 180240 | tf_op jit(solution)/shard_map/psum | solution.py:315
  1417.6 35.3 %all-reduce.7.cloned.1.call-done = (bf16[64,512]{0,1:T(8,128)(2,1)}, bf16[64,512]{0,1:T(8,128)(2,1)}, bf16[64,512]{0,1:T(8,128)(2,1)}, bf16[64,512]{1,0:T(8,128)...) async-done(((bf16[64,512]{0,1:T(8,128)(2,1)}, bf16[64,512]{0,1:T(8,128)(2,1)}, bf16[64,512]{0,1:T(8,128)(2,1)}, bf16[64,512]{1,0:T(8,128)(2,1)}, ...) | async-done | bytes 426000 | tf_op jit(solution)/shard_map/psum | solution.py:314
  (380 shorter events, 259.1 us)
Async XLA Ops:
  7.2 361.4 %copy-start = (bf16[768,512]{1,0:T(8,128)(2,1)S(1)}, bf16[768,512]{1,0:T(8,128)(2,1)}, u32[]{:S(2)}) copy-start(bf16[768,512]{1,0:T(8,128)(2,1)} %param.58) | copy-start | bytes 2359300
  7.2 24.7 %copy-start.2 = (bf16[2048,512]{1,0:T(8,128)(2,1)S(1)}, bf16[2048,512]{1,0:T(8,128)(2,1)}, u32[]{:S(2)}) copy-start(bf16[2048,512]{1,0:T(8,128)(2,1)} %param.32) | copy-start | bytes 6291460
  7.2 24.7 %copy-start.35 = (bf16[512,512]{1,0:T(8,128)(2,1)S(1)}, bf16[512,512]{1,0:T(8,128)(2,1)}, u32[]{:S(2)}) copy-start(bf16[512,512]{1,0:T(8,128)(2,1)} %param.43) | copy-start | bytes 1572868
  8.7 48.9 %all-to-all-start = ((s32[8,1,16]{2,1,0:T(1,128)}), s32[8,1,16]{2,1,0:T(1,128)S(1)}, u32[]{:S(2)}, u32[]{:S(2)}) async-start(s32[8,1,16]{2,1,0:T(1,128)} %bitcast.1), calls=%async_computation | async-start | bytes 8192 | tf_op jit(solution)/shard_map/all_to_all | solution.py:148
  33.2 15.8 %copy-start.12 = (f32[2048,512]{0,1:T(8,128)}, f32[2048,512]{0,1:T(8,128)S(1)}, u32[]{:S(2)}) copy-start(f32[2048,512]{0,1:T(8,128)S(1)} %fusion.77) | copy-start | bytes 12582916
  52.2 25.2 %copy-start.51 = (s32[1,2048]{1,0:T(1,128)S(1)}, s32[1,2048]{1,0:T(1,128)}, u32[]{:S(2)}) copy-start(s32[1,2048]{1,0:T(1,128)} %param.41) | copy-start | bytes 24580
  71.9 39.6 %all-to-all-start.1 = ((bf16[8,2,768]{2,1,0:T(2,128)(2,1)}), bf16[8,2,768]{2,1,0:T(2,128)(2,1)}, u32[]{:S(2)}, u32[]{:S(2)}) async-start(bf16[8,2,768]{2,1,0:T(2,128)(2,1)} %reshape.383), calls=%async_computation.1 | async-start | bytes 49152 | tf_op jit(solution)/shard_map/all_to_all | solution.py:152
  81.2 10.1 copy-start.57
  103.0 10.4 copy-start.43
  113.4 114.2 %copy-start.47 = (bf16[2048,16]{1,0:T(8,128)(2,1)S(1)}, bf16[2048,16]{1,0:T(8,128)(2,1)}, u32[]{:S(2)}) copy-start(bf16[2048,16]{1,0:T(8,128)(2,1)} %copy.197) | copy-start | bytes 196612
  113.4 114.2 %copy-start.58 = (pred[2048,16]{1,0:T(8,128)(4,1)S(1)}, pred[2048,16]{1,0:T(8,128)(4,1)}, u32[]{:S(2)}) copy-start(pred[2048,16]{1,0:T(8,128)(4,1)} %copy.184) | copy-start | bytes 98308
  244.7 9.8 copy-start.53
  254.6 57.4 %copy-start.49 = (bf16[2048,8]{1,0:T(8,128)(2,1)S(1)}, bf16[2048,8]{1,0:T(8,128)(2,1)}, u32[]{:S(2)}) copy-start(bf16[2048,8]{1,0:T(8,128)(2,1)} %copy.204) | copy-start | bytes 98308
  254.6 57.4 %copy-start.61 = (pred[2048,8]{1,0:T(8,128)(4,1)S(1)}, pred[2048,8]{1,0:T(8,128)(4,1)}, u32[]{:S(2)}) copy-start(pred[2048,8]{1,0:T(8,128)(4,1)} %copy.201) | copy-start | bytes 49156
  325.8 20.0 %copy-start.41 = (bf16[1024,64]{0,1:T(8,128)(2,1)S(1)}, bf16[1024,64]{0,1:T(8,128)(2,1)}, u32[]{:S(2)}) copy-start(bf16[1024,64]{0,1:T(8,128)(2,1)} %param.49) | copy-start | bytes 393220
  367.9 10.2 copy-start.71
  368.5 9.6 copy-start.40
  394.9 10.8 copy-start.77
  394.9 10.8 copy-start.90
  407.6 13.6 copy-start.88
  465.8 11.3 copy-start.20
  477.1 189.5 %copy-start.23 = (f32[2048,8]{1,0:T(8,128)S(1)}, f32[2048,8]{1,0:T(8,128)}, u32[]{:S(2)}) copy-start(f32[2048,8]{1,0:T(8,128)} %copy.230) | copy-start | bytes 196612
  759.5 13.6 copy-start.75
  762.0 14.2 copy-start.36
  762.0 10.9 all-to-all-start.2
  767.2 108.3 %reduce-scatter.67.cloned.1.call-start = ((), (), s32[]{:S(2)}) async-start(), calls=%async_computation.35 | async-start | bytes 294912
  768.9 108.1 %reduce-scatter.63.cloned.1.call-start = ((), (), s32[]{:S(2)}) async-start(), calls=%async_computation.33 | async-start | bytes 294912
  780.3 98.1 %reduce-scatter.65.cloned.1.call-start = ((), (), s32[]{:S(2)}) async-start(), calls=%async_computation.34 | async-start | bytes 294912
  783.4 113.0 %reduce-scatter.43.cloned.1.call-start = ((), (), s32[]{:S(2)}) async-start(), calls=%async_computation.23 | async-start | bytes 147456 | tf_op jit(solution)/shard_map/reduce_scatter | solution.py:302
  787.7 139.7 %reduce-scatter.39.cloned.1.call-start = ((), (), s32[]{:S(2)}) async-start(), calls=%async_computation.21 | async-start | bytes 294912 | tf_op jit(solution)/shard_map/reduce_scatter | solution.py:296
  791.3 167.2 %reduce-scatter.73.cloned.1.call-start = ((), (), s32[]{:S(2)}) async-start(), calls=%async_computation.38 | async-start | bytes 294912
  796.5 193.3 %reduce-scatter.71.cloned.1.call-start = ((), (), s32[]{:S(2)}) async-start(), calls=%async_computation.37 | async-start | bytes 294912
  801.6 219.3 %reduce-scatter.41.cloned.1.call-start = ((), (), s32[]{:S(2)}) async-start(), calls=%async_computation.22 | async-start | bytes 294912 | tf_op jit(solution)/shard_map/reduce_scatter | solution.py:300
  806.0 246.2 %reduce-scatter.57.cloned.1.call-start = ((), (), s32[]{:S(2)}) async-start(), calls=%async_computation.30 | async-start | bytes 294912
  820.0 263.1 %reduce-scatter.61.cloned.1.call-start = ((), (), s32[]{:S(2)}) async-start(), calls=%async_computation.32 | async-start | bytes 294912
  825.7 289.2 %reduce-scatter.53.cloned.1.call-start = ((), (), s32[]{:S(2)}) async-start(), calls=%async_computation.28 | async-start | bytes 589824 | tf_op jit(solution)/shard_map/reduce_scatter | solution.py:311
  831.3 315.2 %reduce-scatter.49.cloned.1.call-start = ((), (), s32[]{:S(2)}) async-start(), calls=%async_computation.26 | async-start | bytes 589824 | tf_op jit(solution)/shard_map/reduce_scatter | solution.py:308
  832.4 347.1 %reduce-scatter.47.cloned.1.call-start = ((), (), s32[]{:S(2)}) async-start(), calls=%async_computation.25 | async-start | bytes 1179648 | tf_op jit(solution)/shard_map/reduce_scatter | solution.py:306
  836.4 376.2 %reduce-scatter.45.cloned.1.call-start = ((), (), s32[]{:S(2)}) async-start(), calls=%async_computation.24 | async-start | bytes 1179648 | tf_op jit(solution)/shard_map/reduce_scatter | solution.py:305
  841.7 404.0 %reduce-scatter.69.cloned.1.call-start = ((), (), s32[]{:S(2)}) async-start(), calls=%async_computation.36 | async-start | bytes 1179648
  848.2 430.3 %reduce-scatter.55.cloned.1.call-start = ((), (), s32[]{:S(2)}) async-start(), calls=%async_computation.29 | async-start | bytes 1179648
  854.7 457.0 %reduce-scatter.59.cloned.1.call-start = ((), (), s32[]{:S(2)}) async-start(), calls=%async_computation.31 | async-start | bytes 1179648
  861.1 484.9 %reduce-scatter.51.cloned.1.call-start = ((), (), s32[]{:S(2)}) async-start(), calls=%async_computation.27 | async-start | bytes 1769472 | tf_op jit(solution)/shard_map/reduce_scatter | solution.py:309
  867.1 533.4 %all-reduce.5.cloned.1.call-start = ((), (), s32[]{:S(2)}) async-start(), calls=%async_computation.39 | async-start | bytes 1327104 | tf_op jit(solution)/shard_map/psum | solution.py:315
  870.5 277.5 %copy-start.31 = (bf16[2048,512]{0,1:T(8,128)(2,1)S(1)}, bf16[2048,512]{0,1:T(8,128)(2,1)}, u32[]{:S(2)}) copy-start(bf16[2048,512]{0,1:T(8,128)(2,1)} %get-tuple-element.142) | copy-start | bytes 6291460
  1148.0 199.7 %copy-start.28 = (bf16[512,512]{1,0:T(8,128)(2,1)S(1)}, bf16[512,512]{1,0:T(8,128)(2,1)}, u32[]{:S(2)}) copy-start(bf16[512,512]{1,0:T(8,128)(2,1)} %param.46) | copy-start | bytes 1572868
  1148.0 304.9 %all-reduce.7.cloned.1.call-start = ((), (), s32[]{:S(2)}) async-start(), calls=%async_computation.40 | async-start | bytes 1245184 | tf_op jit(solution)/shard_map/psum | solution.py:314
  1347.6 114.8 %copy-start.1 = (bf16[768,512]{1,0:T(8,128)(2,1)S(1)}, bf16[768,512]{1,0:T(8,128)(2,1)}, u32[]{:S(2)}) copy-start(bf16[768,512]{1,0:T(8,128)(2,1)} %param.58) | copy-start | bytes 2359300
  (66 other events, 291.0 us)
Sparse Core Ops, SparseCore 0:
  770.3 32.2 reduce-scatter.66
  804.8 28.9 reduce-scatter.62
  836.0 28.9 reduce-scatter.64
  867.7 28.7 reduce-scatter.42
  898.5 28.9 reduce-scatter.38
  929.6 28.9 reduce-scatter.72
  960.8 28.9 reduce-scatter.70
  992.0 28.8 reduce-scatter.40
  1023.2 28.9 reduce-scatter.56
  1054.2 28.9 reduce-scatter.60
  1085.4 29.4 reduce-scatter.52
  1117.0 29.4 reduce-scatter.48
  1148.8 30.6 reduce-scatter.46
  1181.6 30.9 reduce-scatter.44
  1214.7 30.9 reduce-scatter.68
  1247.9 30.5 reduce-scatter.54
  1280.6 30.9 reduce-scatter.58
  1313.8 32.1 reduce-scatter.50
  1352.1 48.3 all-reduce.4
  1405.2 47.6 all-reduce.6
where the time goes:
time: 1480 us; the launch traced here: 1470 us
  waiting for transfers between devices  524 us (35%)
  local copies, waits for them, and re-layouts  355 us (24%)
  other arithmetic  315 us (21%)
  matrix products  241 us (16%)
  starting transfers between devices  18.3 us (1%)
  between operations  15.9 us (1%)
    scatter-add x2, other arithmetic, bilinear_back(): zeroed.at[sources.reshape(-1)].add(picked_grad.reshape(-1, column_count))  267 us
    unnamed x30, waiting for transfers between devices  213 us
    gather x2, local copies, waits for them, and re-layouts, bilinear_sum(): jnp.take(source_table, sources.reshape(-1), axis=0)  172 us
    unnamed x221, local copies, waits for them, and re-layouts  80.7 us
    dot_general x17, matrix products, outer_sum(): lax.dot_general(operand, gradient, (((0,), (0,)), ((), ())), preferred_el...  60.1 us
    dot_general x14, matrix products, against(): lax.dot_general(gradient, weight, (((1,), (1,)), ((), ())), preferred_ele...  50.4 us
    dot_general x19, matrix products, product(): return jnp.dot(operand, weight, preferred_element_type=jnp.float32)  47.8 us
    psum x1, waiting for transfers between devices, per_device(): lax.psum(pieces[1].astype(jnp.bfloat16), 'grp').astype(jnp.float32)  43.7 us
  transfers between devices with their start and end apart: 23, of which 18 were waited for; matrix products, arithmetic and copies ran while one was open for 16% of the time, Pallas kernels for 0%

commit v1 on v0

v1 whole, which is shorter than its diff:
```python
import math

import jax
import jax.numpy as jnp
from jax import lax
from jax.experimental import pallas as pl
from jax.experimental.pallas import tpu as pltpu
from jax.sharding import PartitionSpec as P

HALF_ROOT = 1.0 / math.sqrt(2.0)
THIRD_ROOT = 1.0 / math.sqrt(3.0)
LOW = jnp.bfloat16
WIDE = jnp.float32
TILE = 256
VMEM_BYTES = 60 * 1024 * 1024


def sigma(v):
    return 0.5 * jnp.tanh(0.5 * v) + 0.5


def slope_of(v, s):
    return s * (1.0 + v * (1.0 - s))


def nn(a, b):
    return jnp.dot(a, b, preferred_element_type=WIDE)


def nt(a, b):
    return lax.dot_general(a, b, (((1,), (1,)), ((), ())), preferred_element_type=WIDE)


def tn(a, b):
    return lax.dot_general(a, b, (((0,), (0,)), ((), ())), preferred_element_type=WIDE)


def split_pair(v):
    high = v.astype(LOW)
    rest = (v - high.astype(WIDE)).astype(LOW)
    return jnp.concatenate([high, rest], axis=0)


def whole(array):
    rank = len(array.shape)
    return pl.BlockSpec(array.shape, lambda i: (0,) * rank)


def rows(width):
    return pl.BlockSpec((TILE, width), lambda i: (i, 0))


def cols(height):
    return pl.BlockSpec((height, TILE), lambda i: (0, i))


def fixed(*shape):
    return pl.BlockSpec(shape, lambda i: (0,) * len(shape))


def call(body, name, steps, ins, in_specs, outs, out_specs, scratch):
    return pl.pallas_call(
        body,
        name=name,
        out_shape=[jax.ShapeDtypeStruct(s, t) for s, t in outs],
        grid_spec=pltpu.PrefetchScalarGridSpec(
            num_scalar_prefetch=0,
            grid=(steps,),
            in_specs=in_specs,
            out_specs=out_specs,
            scratch_shapes=scratch,
        ),
        compiler_params=pltpu.CompilerParams(
            dimension_semantics=("arbitrary",), vmem_limit_bytes=VMEM_BYTES
        ),
    )(*ins)


def source_body(edge, radial, ws3, wr3, wd3, ws4, wr4, wd4, table, down):
    e = edge[...]
    r = radial[...]
    pre3 = nn(e, ws3[...])
    mix3 = (pre3 * sigma(pre3) * nn(r, wr3[...])).astype(LOW)
    down3 = nt(wd3[...], mix3)
    pre4 = nn(e, ws4[...])
    mix4 = (pre4 * sigma(pre4) * nn(r, wr4[...])).astype(LOW)
    down4 = nt(wd4[...], mix4)
    both = jnp.concatenate([down3, down4], axis=0)
    down[...] = both
    table[...] = (both * sigma(both)).astype(LOW)


def fill_slabs(tab, ghost, t3, t4, n3, n4):
    local = tab.shape[1] // TILE
    for s in range(local):
        t3[s * n3 : (s + 1) * n3, :] = tab[0:n3, s * TILE : (s + 1) * TILE]
        t4[s * n4 : (s + 1) * n4, :] = tab[n3 : n3 + n4, s * TILE : (s + 1) * TILE]
    for g in range(ghost.shape[1] // TILE):
        s = local + g
        t3[s * n3 : (s + 1) * n3, :] = ghost[0:n3, g * TILE : (g + 1) * TILE]
        t4[s * n4 : (s + 1) * n4, :] = ghost[n3 : n3 + n4, g * TILE : (g + 1) * TILE]


def pick(tab, index_row, width):
    slabs = tab.shape[0] // width
    low_part = index_row & (TILE - 1)
    slab = index_row >> 8
    hot = (lax.broadcasted_iota(jnp.int32, (TILE, TILE), 0) == low_part).astype(LOW)
    found = nn(tab[...], hot)
    got = jnp.zeros((width, TILE), WIDE)
    for s in range(slabs):
        got = jnp.where(slab == s, found[s * width : (s + 1) * width, :], got)
    return got


def weigh(coef, picked, out, slots, basis, width):
    chunk = 32
    for h in range(width // chunk):
        for cb in range(basis // 4):
            acc = [None] * 4
            for k in range(slots):
                g = picked[k, h * chunk : (h + 1) * chunk, :]
                for j in range(4):
                    row = k * basis + cb * 4 + j
                    term = coef[row : row + 1, :] * g
                    acc[j] = term if acc[j] is None else acc[j] + term
            for j in range(4):
                at = (cb * 4 + j) * width + h * chunk
                out[at : at + chunk, :] = acc[j].astype(LOW)


def gather_body(
    tab, ghost, i3, i4, b3, b4, w3t, w4t, s3, s4, p3, p4, t3, t4, g3, g4, c3, c4
):
    n3, n4 = w3t.shape[0], w4t.shape[0]
    k3, k4 = i3.shape[0], i4.shape[0]

    @pl.when(pl.program_id(0) == 0)
    def _():
        fill_slabs(tab, ghost, t3, t4, n3, n4)

    c3[...] = b3[...].astype(WIDE).T
    c4[...] = b4[...].astype(WIDE).T

    def step3(k, carry):
        g3[k] = pick(t3, i3[pl.ds(k, 1), :], n3)
        return carry

    lax.fori_loop(0, k3, step3, 0, unroll=4)

    def step4(k, carry):
        g4[k] = pick(t4, i4[pl.ds(k, 1), :], n4)
        return carry

    lax.fori_loop(0, k4, step4, 0, unroll=4)
    weigh(c3, g3, s3, k3, c3.shape[0] // k3, n3)
    weigh(c4, g4, s4, k4, c4.shape[0] // k4, n4)
    p3[...] = nn(w3t[...], s3[...])
    p4[...] = nn(w4t[...], s4[...])


def mix_body(
    edge, radial, p3, p4, trow, wu3, wu4, wsk, wr1, wr2, wra, wat, atom,
    merged, mixlow, reshid, dsk, du3, du4, dr1, dr2, gath, anew, aslope, acc,
):
    step = pl.program_id(0)
    atoms = acc.shape[0]
    v3 = p3[...]
    v4 = p4[...]
    h3 = (v3 * sigma(v3)).T.astype(LOW)
    h4 = (v4 * sigma(v4)).T.astype(LOW)
    up3 = nn(h3, wu3[...])
    s = sigma(up3)
    du3[...] = slope_of(up3, s).astype(LOW)
    total = up3 * s
    up4 = nn(h4, wu4[...])
    s = sigma(up4)
    du4[...] = slope_of(up4, s).astype(LOW)
    total = total + up4 * s
    skip = nn(edge[...], wsk[...])
    s = sigma(skip)
    dsk[...] = slope_of(skip, s).astype(LOW)
    mixed = (total + skip * s) * THIRD_ROOT
    low_mixed = mixed.astype(LOW)
    mixlow[...] = low_mixed
    res = nn(low_mixed, wr1[...])
    s = sigma(res)
    dr1[...] = slope_of(res, s).astype(LOW)
    hid = (res * s).astype(LOW)
    reshid[...] = hid
    res2 = nn(hid, wr2[...])
    s = sigma(res2)
    dr2[...] = (0.5 * slope_of(res2, s)).astype(LOW)
    out = (edge[...].astype(WIDE) + (mixed + res2 * s) * HALF_ROOT) * HALF_ROOT
    merged[...] = out
    weighted = (out * nn(radial[...], wra[...])).astype(LOW)
    hot_t = (lax.broadcasted_iota(jnp.int32, (atoms, TILE), 0) == trow[...]).astype(LOW)
    part = nn(hot_t, weighted)

    @pl.when(step == 0)
    def _():
        acc[...] = part

    @pl.when(step > 0)
    def _():
        acc[...] += part

    @pl.when(step == pl.num_programs(0) - 1)
    def _():
        g = acc[...].astype(LOW)
        gath[...] = g
        pre = nn(g, wat[...])
        sa = sigma(pre)
        aslope[...] = HALF_ROOT * slope_of(pre, sa)
        anew[...] = ((atom[...].astype(WIDE) + pre * sa) * HALF_ROOT).astype(LOW)


def out_body(
    merged, radial, trow, tcol, anew, cot, wc, wro, wout, ocot, acot, aslope, gath, wat,
    enew, gmer, gwc, gro, goa, aout, gatom, gw2, ogat, seg, both, awc, aro,
):
    step = pl.program_id(0)
    atoms, wide = ogat.shape
    aw = anew.shape[1]

    @pl.when(step == 0)
    def _():
        both[:, 0:wide] = split_pair(nt(ocot[...], wout[...]))
        both[:, wide : 2 * wide] = split_pair(nn(anew[...], wc[0:aw, :]))
        ogat[...] = jnp.zeros_like(ogat)
        seg[...] = jnp.zeros_like(seg)
        awc[...] = jnp.zeros_like(awc)
        aro[...] = jnp.zeros_like(aro)

    hot_t = (lax.broadcasted_iota(jnp.int32, (atoms, TILE), 0) == trow[...]).astype(LOW)
    lane = lax.broadcasted_iota(jnp.int32, (TILE, 2 * atoms), 1)
    hot = ((lane & (atoms - 1)) == tcol[...]).astype(LOW)
    spread = nn(hot, both[...])
    gow = spread[:, 0:wide]
    m = merged[...]
    ml = m.astype(LOW)
    wcm = wc[aw:, :]
    pre = spread[:, wide:] + nn(ml, wcm)
    s = sigma(pre)
    new = (m + pre * s) * HALF_ROOT
    enew[...] = new.astype(LOW)
    rout = nn(radial[...], wro[...])
    ogat[...] += nn(hot_t, (new * rout).astype(LOW))
    gnew = cot[...].astype(WIDE) + gow * rout
    aro[...] += tn(radial[...], (gow * new).astype(LOW))
    lc = (gnew * (HALF_ROOT * slope_of(pre, s))).astype(LOW)
    awc[...] += tn(ml, lc)
    seg[...] += nn(hot_t, lc)
    gmer[...] = gnew * HALF_ROOT + nt(lc, wcm)

    @pl.when(step == pl.num_programs(0) - 1)
    def _():
        ol = ogat[...].astype(LOW)
        aout[...] = nn(ol, wout[...]).astype(LOW)
        goa[:, 0:aw] = tn(ol, ocot[...]).astype(LOW)
        gwc[aw:, :] = awc[...].astype(LOW)
        gro[...] = aro[...].astype(LOW)
        pair = split_pair(seg[...])
        hi = pair[0:atoms, :]
        lo = pair[atoms:, :]
        gwc[0:aw, :] = (tn(anew[...], hi) + tn(anew[...], lo)).astype(LOW)
        wca = wc[0:aw, :]
        ga = acot[...].astype(WIDE) + nt(hi, wca) + nt(lo, wca)
        gatom[...] = (ga * HALF_ROOT).astype(LOW)
        la = (ga * aslope[...]).astype(LOW)
        goa[:, aw : 2 * aw] = tn(gath[...], la).astype(LOW)
        gw2[...] = split_pair(nt(la, wat[...]))


def back_body(
    edge, radial, tcol, merged, gmer, gw2, p3, p4, mixlow, reshid, dsk, du3, du4, dr1, dr2,
    wu3, wu4, wsk, wr1, wr2, wra,
    gpart, lb3, lb4, gsk, gr1, gr2, gra, gup, ask, ar1, ar2, ara, aup,
):
    step = pl.program_id(0)
    pair = gw2.shape[0]
    n3 = wu3.shape[0]

    @pl.when(step == 0)
    def _():
        ask[...] = jnp.zeros_like(ask)
        ar1[...] = jnp.zeros_like(ar1)
        ar2[...] = jnp.zeros_like(ar2)
        ara[...] = jnp.zeros_like(ara)
        aup[...] = jnp.zeros_like(aup)

    lane = lax.broadcasted_iota(jnp.int32, (TILE, pair), 1)
    hot = ((lane & (pair // 2 - 1)) == tcol[...]).astype(LOW)
    gw = nn(hot, gw2[...])
    gm = gmer[...] + gw * nn(radial[...], wra[...])
    ara[...] += tn(radial[...], (gw * merged[...]).astype(LOW))
    l2 = (gm * dr2[...].astype(WIDE)).astype(LOW)
    ar2[...] += tn(reshid[...], l2)
    l1 = (nt(l2, wr2[...]) * dr1[...].astype(WIDE)).astype(LOW)
    ar1[...] += tn(mixlow[...], l1)
    gmix = (gm * 0.5 + nt(l1, wr1[...])) * THIRD_ROOT
    ls = (gmix * dsk[...].astype(WIDE)).astype(LOW)
    l3 = (gmix * du3[...].astype(WIDE)).astype(LOW)
    l4 = (gmix * du4[...].astype(WIDE)).astype(LOW)
    ask[...] += tn(edge[...], ls)
    gpart[...] = gm * HALF_ROOT + nt(ls, wsk[...])
    v3 = p3[...]
    s3 = sigma(v3)
    v4 = p4[...]
    s4 = sigma(v4)
    aup[0:n3, :] += nn((v3 * s3).astype(LOW), l3)
    aup[n3:, :] += nn((v4 * s4).astype(LOW), l4)
    lb3[...] = (nt(wu3[...], l3) * slope_of(v3, s3)).astype(LOW)
    lb4[...] = (nt(wu4[...], l4) * slope_of(v4, s4)).astype(LOW)

    @pl.when(step == pl.num_programs(0) - 1)
    def _():
        gsk[...] = ask[...].astype(LOW)
        gr1[...] = ar1[...].astype(LOW)
        gr2[...] = ar2[...].astype(LOW)
        gra[...] = ara[...].astype(LOW)
        gup[...] = aup[...].T.astype(LOW)


def unweigh(coef, dsum, index, spread, hots, slots, basis, width):
    chunk = 32
    slabs = spread.shape[0] // width
    for k in range(slots):
        low_part = index[k : k + 1, :] & (TILE - 1)
        hot = (lax.broadcasted_iota(jnp.int32, (TILE, TILE), 0) == low_part).astype(LOW)
        hots[:, k * TILE : (k + 1) * TILE] = hot
    for h in range(width // chunk):
        for kb in range(slots // 4):
            acc = [None] * 4
            for c in range(basis):
                at = c * width + h * chunk
                d = dsum[at : at + chunk, :]
                for j in range(4):
                    row = (kb * 4 + j) * basis + c
                    term = coef[row : row + 1, :] * d
                    acc[j] = term if acc[j] is None else acc[j] + term
            for j in range(4):
                k = kb * 4 + j
                slab = index[k : k + 1, :] >> 8
                for s in range(slabs):
                    at = s * width + h * chunk
                    spread[at : at + chunk, k * TILE : (k + 1) * TILE] = jnp.where(
                        slab == s, acc[j], 0.0
                    ).astype(LOW)


def scatter_body(
    lb3, lb4, i3, i4, b3, b4, w3, w4, s3, s4, grad, gbil, a3, a4, abil, c3, c4, d3, d4, v3, v4, h3, h4
):
    step = pl.program_id(0)
    n3, n4 = w3.shape[1], w4.shape[1]
    k3, k4 = i3.shape[0], i4.shape[0]

    @pl.when(step == 0)
    def _():
        a3[...] = jnp.zeros_like(a3)
        a4[...] = jnp.zeros_like(a4)
        abil[...] = jnp.zeros_like(abil)

    c3[...] = b3[...].astype(WIDE).T
    c4[...] = b4[...].astype(WIDE).T
    d3[...] = nn(w3[...], lb3[...])
    d4[...] = nn(w4[...], lb4[...])
    abil[:, 0:n3] += nt(s3[...], lb3[...])
    abil[:, n3 : n3 + n4] += nt(s4[...], lb4[...])
    unweigh(c3, d3, i3, v3, h3, k3, c3.shape[0] // k3, n3)
    a3[...] += nt(v3[...], h3[...])
    unweigh(c4, d4, i4, v4, h4, k4, c4.shape[0] // k4, n4)
    a4[...] += nt(v4[...], h4[...])

    @pl.when(step == pl.num_programs(0) - 1)
    def _():
        for s in range(a3.shape[0] // n3):
            grad[0:n3, s * TILE : (s + 1) * TILE] = a3[s * n3 : (s + 1) * n3, :]
            grad[n3 : n3 + n4, s * TILE : (s + 1) * TILE] = a4[s * n4 : (s + 1) * n4, :]
        gbil[...] = abil[...].astype(LOW)


def source_back_body(
    edge, radial, gpart, grad, down, ret, ask, ws3, wr3, wd3, ws4, wr4, wd4,
    gedge, gs3, gs4, gr3, gr4, gdn, as3, as4, ar3, ar4, adn,
):
    step = pl.program_id(0)
    n3 = wd3.shape[0]

    @pl.when(step == 0)
    def _():
        as3[...] = jnp.zeros_like(as3)
        as4[...] = jnp.zeros_like(as4)
        ar3[...] = jnp.zeros_like(ar3)
        ar4[...] = jnp.zeros_like(ar4)
        adn[...] = jnp.zeros_like(adn)

    lane = lax.broadcasted_iota(jnp.int32, (ask.shape[0], TILE), 1) + step * TILE
    back = nn(ret[...], (lane == ask[...]).astype(LOW))
    v = down[...]
    ld = (grad[...] + back) * slope_of(v, sigma(v))
    ldt = ld.astype(LOW)
    low_rows = ld.T.astype(LOW)
    e = edge[...]
    r = radial[...]
    pre = nn(e, ws3[...])
    rad = nn(r, wr3[...])
    s = sigma(pre)
    act = pre * s
    adn[0:n3, :] += nn(ldt[0:n3, :], (act * rad).astype(LOW))
    gm = nn(low_rows[:, 0:n3], wd3[...])
    l3 = (gm * rad * slope_of(pre, s)).astype(LOW)
    ar3[...] += tn(r, (gm * act).astype(LOW))
    as3[...] += tn(e, l3)
    pre = nn(e, ws4[...])
    rad = nn(r, wr4[...])
    s = sigma(pre)
    act = pre * s
    adn[n3:, :] += nn(ldt[n3:, :], (act * rad).astype(LOW))
    gm = nn(low_rows[:, n3:], wd4[...])
    l4 = (gm * rad * slope_of(pre, s)).astype(LOW)
    ar4[...] += tn(r, (gm * act).astype(LOW))
    as4[...] += tn(e, l4)
    gedge[...] = (gpart[...] + nt(l3, ws3[...]) + nt(l4, ws4[...])).astype(LOW)

    @pl.when(step == pl.num_programs(0) - 1)
    def _():
        gs3[...] = as3[...].astype(LOW)
        gs4[...] = as4[...].astype(LOW)
        gr3[...] = ar3[...].astype(LOW)
        gr4[...] = ar4[...].astype(LOW)
        gdn[...] = adn[...].T.astype(LOW)


def swap(v, axis, bit):
    count = lax.axis_size(axis)
    return lax.ppermute(v, axis, [(j, j ^ (1 << bit)) for j in range(count)])


def bits_of(axis):
    return range(lax.axis_size(axis).bit_length() - 1)


def reduce_shares(packed):
    v = packed
    place = lax.axis_index("edge")
    for bit in bits_of("edge"):
        side = (place >> bit) & 1
        v = v.reshape(v.shape[0] // 2, 2, *v.shape[1:])
        kept = lax.dynamic_index_in_dim(v, side, 1, keepdims=False)
        sent = lax.dynamic_index_in_dim(v, 1 - side, 1, keepdims=False)
        got = swap(sent, "edge", bit)
        v = (kept.astype(WIDE) + got.astype(WIDE)).astype(LOW)
    v = v[0]
    last = bits_of("grp")[-1]
    for bit in bits_of("grp"):
        v = v.astype(WIDE) + swap(v, "grp", bit).astype(WIDE)
        if bit != last:
            v = v.astype(LOW)
    return v


def by_rows(g, count):
    return g.reshape(count, g.shape[0] // count, g.shape[1])


def fold(g, count):
    parts = g.reshape(count, 4, g.shape[0] // count // 4, g.shape[1])
    parts = jnp.pad(parts, ((0, 0), (0, 0), (0, 0), (0, 128 - g.shape[1])))
    return jnp.concatenate([parts[:, q] for q in range(4)], axis=2)


def unfold(g):
    return jnp.concatenate([g[:, q * 128 : q * 128 + 96] for q in range(4)], axis=0)


def per_device(
    edge_embed, atom_embed, radial_basis, triplet_basis, quadruplet_basis,
    triplet_source_row, triplet_mask, quadruplet_source_row, quadruplet_mask,
    edge_target_atom, borrowed_edges,
    w_source_trip, w_rbf_trip, w_down_trip, w_source_quad, w_rbf_quad, w_down_quad,
    triplet_bilinear_weight, w_up_trip, w_bilinear_quad, w_up_quad, w_skip,
    w_res_first, w_res_second, w_rbf_atom, w_atom, w_concat, w_rbf_out, w_out,
    edge_cotangent, atom_cotangent, output_cotangent,
):
    edges, wide = edge_embed.shape
    atoms, aw = atom_embed.shape
    rbf = radial_basis.shape[1]
    peers = lax.axis_size("edge")
    cap = borrowed_edges.shape[2]
    steps = edges // TILE
    n3, n4 = w_down_trip.shape[1], w_down_quad.shape[1]
    nb = n3 + n4
    k3, k4 = triplet_mask.shape[1], quadruplet_mask.shape[1]
    f3, f4 = triplet_bilinear_weight.shape[0], w_bilinear_quad.shape[0]
    q3, q4 = triplet_basis.shape[1], quadruplet_basis.shape[1]
    ghosts = peers * cap
    ghosts_up = -(-ghosts // TILE) * TILE
    slabs = (edges + ghosts_up) // TILE

    wanted = borrowed_edges[0] - (jnp.arange(peers, dtype=jnp.int32) * edges)[:, None]
    asked = lax.all_to_all(wanted, "edge", split_axis=0, concat_axis=0, tiled=True).reshape(-1)

    wd3t, wd4t = w_down_trip.T, w_down_quad.T
    w3t, w4t = triplet_bilinear_weight.T, w_bilinear_quad.T
    i3 = jnp.where(triplet_mask > 0, triplet_source_row, -1).T
    i4 = jnp.where(quadruplet_mask > 0, quadruplet_source_row, -1).T
    trow = edge_target_atom
    tcol = edge_target_atom.reshape(edges, 1)

    src_ins = (edge_embed, radial_basis, w_source_trip, w_rbf_trip, wd3t, w_source_quad, w_rbf_quad, wd4t)
    table, down = call(
        source_body, "source_rows", steps, src_ins,
        [rows(wide), rows(rbf)] + [whole(w) for w in src_ins[2:]],
        [((nb, edges), LOW), ((nb, edges), WIDE)],
        [cols(nb), cols(nb)],
        [],
    )

    hot_out = (asked[:, None] == jnp.arange(edges, dtype=jnp.int32)[None, :]).astype(LOW)
    outgoing = nt(hot_out, table).astype(LOW).reshape(peers, -1)
    ghost = lax.all_to_all(outgoing, "edge", split_axis=0, concat_axis=0, tiled=True)
    ghost = jnp.pad(ghost.reshape(ghosts, nb).T, ((0, 0), (0, ghosts_up - ghosts)))

    s3, s4, p3, p4 = call(
        gather_body, "gather_sums", steps,
        (table, ghost, i3, i4, triplet_basis, quadruplet_basis, w3t, w4t),
        [whole(table), whole(ghost), cols(k3), cols(k4), rows(q3), rows(q4), whole(w3t), whole(w4t)],
        [((f3, edges), LOW), ((f4, edges), LOW), ((n3, edges), WIDE), ((n4, edges), WIDE)],
        [cols(f3), cols(f4), cols(n3), cols(n4)],
        [
            pltpu.VMEM((slabs * n3, TILE), LOW), pltpu.VMEM((slabs * n4, TILE), LOW),
            pltpu.VMEM((k3, n3, TILE), WIDE), pltpu.VMEM((k4, n4, TILE), WIDE),
            pltpu.VMEM((q3, TILE), WIDE), pltpu.VMEM((q4, TILE), WIDE),
        ],
    )

    act = ((edges, wide), LOW)
    merged, mixlow, reshid, dsk, du3, du4, dr1, dr2, gath, anew, aslope = call(
        mix_body, "edge_update", steps,
        (edge_embed, radial_basis, p3, p4, trow, w_up_trip, w_up_quad, w_skip, w_res_first,
         w_res_second, w_rbf_atom, w_atom, atom_embed),
        [rows(wide), rows(rbf), cols(n3), cols(n4), cols(1)]
        + [whole(w) for w in (w_up_trip, w_up_quad, w_skip, w_res_first, w_res_second, w_rbf_atom, w_atom, atom_embed)],
        [((edges, wide), WIDE), act, act, act, act, act, act, act,
         ((atoms, wide), LOW), ((atoms, aw), LOW), ((atoms, aw), WIDE)],
        [rows(wide)] * 8 + [fixed(atoms, wide), fixed(atoms, aw), fixed(atoms, aw)],
        [pltpu.VMEM((atoms, wide), WIDE)],
    )

    enew, gmer, gwc, gro, goa, aout, gatom, gw2 = call(
        out_body, "output_block", steps,
        (merged, radial_basis, trow, tcol, anew, edge_cotangent, w_concat, w_rbf_out, w_out,
         output_cotangent, atom_cotangent, aslope, gath, w_atom),
        [rows(wide), rows(rbf), cols(1), rows(1), whole(anew), rows(wide)]
        + [whole(w) for w in (w_concat, w_rbf_out, w_out, output_cotangent, atom_cotangent, aslope, gath, w_atom)],
        [act, ((edges, wide), WIDE), (w_concat.shape, LOW), (w_rbf_out.shape, LOW),
         ((wide, 2 * aw), LOW), ((atoms, aw), LOW), ((atoms, aw), LOW), ((2 * atoms, wide), LOW)],
        [rows(wide), rows(wide), whole(w_concat), whole(w_rbf_out), fixed(wide, 2 * aw),
         fixed(atoms, aw), fixed(atoms, aw), fixed(2 * atoms, wide)],
        [
            pltpu.VMEM((atoms, wide), WIDE), pltpu.VMEM((atoms, wide), WIDE),
            pltpu.VMEM((2 * atoms, 2 * wide), LOW),
            pltpu.VMEM((w_concat.shape[0] - aw, wide), WIDE), pltpu.VMEM(w_rbf_out.shape, WIDE),
        ],
    )
    first = jnp.concatenate([by_rows(gwc, peers), by_rows(goa, peers), by_rows(gro, peers)], axis=1)
    first = reduce_shares(first)

    gpart, lb3, lb4, gsk, gr1, gr2, gra, gup = call(
        back_body, "edge_update_back", steps,
        (edge_embed, radial_basis, tcol, merged, gmer, gw2, p3, p4, mixlow, reshid, dsk, du3, du4,
         dr1, dr2, w_up_trip, w_up_quad, w_skip, w_res_first, w_res_second, w_rbf_atom),
        [rows(wide), rows(rbf), rows(1), rows(wide), rows(wide), whole(gw2), cols(n3), cols(n4)]
        + [rows(wide)] * 7
        + [whole(w) for w in (w_up_trip, w_up_quad, w_skip, w_res_first, w_res_second, w_rbf_atom)],
        [((edges, wide), WIDE), ((n3, edges), LOW), ((n4, edges), LOW), (w_skip.shape, LOW),
         (w_skip.shape, LOW), (w_skip.shape, LOW), (w_rbf_atom.shape, LOW), ((wide, nb), LOW)],
        [rows(wide), cols(n3), cols(n4), whole(w_skip), whole(w_skip), whole(w_skip),
         whole(w_rbf_atom), fixed(wide, nb)],
        [pltpu.VMEM(w_skip.shape, WIDE)] * 3
        + [pltpu.VMEM(w_rbf_atom.shape, WIDE), pltpu.VMEM((nb, wide), WIDE)],
    )

    grad, gbil = call(
        scatter_body, "scatter_sums", steps,
        (lb3, lb4, i3, i4, triplet_basis, quadruplet_basis, triplet_bilinear_weight, w_bilinear_quad, s3, s4),
        [cols(n3), cols(n4), cols(k3), cols(k4), rows(q3), rows(q4), whole(triplet_bilinear_weight),
         whole(w_bilinear_quad), cols(f3), cols(f4)],
        [((nb, slabs * TILE), WIDE), ((f3, nb), LOW)],
        [fixed(nb, slabs * TILE), fixed(f3, nb)],
        [
            pltpu.VMEM((slabs * n3, TILE), WIDE), pltpu.VMEM((slabs * n4, TILE), WIDE),
            pltpu.VMEM((f3, nb), WIDE),
            pltpu.VMEM((q3, TILE), WIDE), pltpu.VMEM((q4, TILE), WIDE),
            pltpu.VMEM((f3, TILE), WIDE), pltpu.VMEM((f4, TILE), WIDE),
            pltpu.VMEM((slabs * n3, k3 * TILE), LOW), pltpu.VMEM((slabs * n4, k4 * TILE), LOW),
            pltpu.VMEM((TILE, k3 * TILE), LOW), pltpu.VMEM((TILE, k4 * TILE), LOW),
        ],
    )
    second = jnp.concatenate(
        [by_rows(gsk, peers), by_rows(gr1, peers), by_rows(gr2, peers), by_rows(gra, peers),
         fold(gup, peers), fold(gbil, peers)],
        axis=1,
    )
    second = reduce_shares(second)

    back = grad[:, edges : edges + ghosts].astype(LOW).T.reshape(peers, -1)
    back = lax.all_to_all(back, "edge", split_axis=0, concat_axis=0, tiled=True)
    back = back.reshape(ghosts, nb).T
    askcol = asked.reshape(ghosts, 1)

    sb_ins = (edge_embed, radial_basis, gpart, grad, down, back, askcol) + src_ins[2:]
    gedge, gs3, gs4, gr3, gr4, gdn = call(
        source_back_body, "source_rows_back", steps, sb_ins,
        [rows(wide), rows(rbf), rows(wide), cols(nb), cols(nb), whole(back), whole(askcol)]
        + [whole(w) for w in src_ins[2:]],
        [act, (w_skip.shape, LOW), (w_skip.shape, LOW), (w_rbf_trip.shape, LOW),
         (w_rbf_trip.shape, LOW), ((wide, nb), LOW)],
        [rows(wide), whole(w_skip), whole(w_skip), whole(w_rbf_trip), whole(w_rbf_trip), fixed(wide, nb)],
        [pltpu.VMEM(w_skip.shape, WIDE)] * 2
        + [pltpu.VMEM(w_rbf_trip.shape, WIDE)] * 2
        + [pltpu.VMEM((nb, wide), WIDE)],
    )
    third = jnp.concatenate(
        [by_rows(gs3, peers), by_rows(gs4, peers), by_rows(gr3, peers), by_rows(gr4, peers), fold(gdn, peers)],
        axis=1,
    )
    third = reduce_shares(third)

    a = wide // peers
    b = rbf // peers
    c = w_concat.shape[0] // peers
    r_concat = first[0:c]
    r_oa = first[c : c + a]
    r_out = first[c + a : c + a + b]
    r_sk = second[0:a]
    r_r1 = second[a : 2 * a]
    r_r2 = second[2 * a : 3 * a]
    r_ra = second[3 * a : 3 * a + b]
    at = 3 * a + b
    r_up = unfold(second[at : at + a // 4]).T
    r_bil = unfold(second[at + a // 4 :])
    r_s3 = third[0:a]
    r_s4 = third[a : 2 * a]
    r_r3 = third[2 * a : 2 * a + b]
    r_r4 = third[2 * a + b : 2 * a + 2 * b]
    r_dn = unfold(third[2 * a + 2 * b :])
    return (
        enew, anew, aout, gedge, gatom,
        r_s3, r_r3, r_dn[:, 0:n3], r_s4, r_r4, r_dn[:, n3:],
        r_bil[:, 0:n3], r_up[0:n3], r_bil[:, n3:], r_up[n3:],
        r_sk, r_r1, r_r2, r_ra, r_oa[:, aw:], r_concat, r_out, r_oa[:, 0:aw],
    )


def solution(mesh):
    both = P(("grp", "edge"), None)
    placed = (both,) * 10 + (P(("grp", "edge"), None, None),) + (P(),) * 18 + (both,) * 3
    shares = [P("edge", None)] * 18
    shares[7] = P(None, "edge")
    shares[9] = P(None, "edge")
    return jax.shard_map(
        per_device, mesh=mesh, in_specs=placed, out_specs=(both,) * 5 + tuple(shares), check_vma=False
    )
```

time: 1480 us -> 298 us (0.20)
  waiting for transfers between devices: 524 us -> 53.9 us
  local copies, waits for them, and re-layouts: 355 us -> 38.9 us
  other arithmetic: 315 us -> 15.6 us
  matrix products: 241 us -> 1.4 us
  Pallas kernels: 0 us -> 155 us
    scatter-add x3 -> x0, other arithmetic: 269 us -> none  [the longest x2 267 us: bilinear_back(): zeroed.at[sources.reshape(-1)].add(picked_grad.reshape(-1, column_count))]
    dot_general x57 -> x1, matrix products: 234 us -> 1.4 us  [nt(): lax.dot_general(a, b, (((1,), (1,)), ((), ())), preferred_element_type=WIDE)]
    reduce_scatter x8 -> x0, waiting for transfers between devices: 228 us -> none  [the longest x1 32.7 us: per_device(): lax.psum_scatter(grad_w_concat, 'edge', scatter_dimension=0, tiled=True)]
    unnamed x30 -> x0, waiting for transfers between devices: 213 us -> none
    gather x4 -> x0, local copies, waits for them, and re-layouts: 175 us -> none  [the longest x2 172 us: bilinear_sum(): jnp.take(source_table, sources.reshape(-1), axis=0)]
    pallas_call x0 -> x7, Pallas kernels: none -> 155 us  [call(): pl.pallas_call(body, name=name, out_shape=[jax.ShapeDtypeStruct(s, t) for...]
    psum x2 -> x0, waiting for transfers between devices: 79 us -> none  [the longest x1 43.7 us: per_device(): lax.psum(pieces[1].astype(jnp.bfloat16), 'grp').astype(jnp.float32)]
    unnamed x221 -> x57, local copies, waits for them, and re-layouts: 80.7 us -> 15.4 us
  transfers between devices with their start and end apart: 23 -> 18, of which waited for: 18 -> 10; matrix products, arithmetic and copies ran while one was open for 16% -> 13% of each run, Pallas kernels for 0% -> 27%
where the time goes in v1:
time: 298 us; the launch traced here: 296 us
  Pallas kernels  155 us (52%)
  waiting for transfers between devices  53.9 us (18%)
  local copies, waits for them, and re-layouts  38.9 us (13%)
  starting transfers between devices  30.2 us (10%)
  other arithmetic  15.6 us (5%)
    pallas_call x7, Pallas kernels, call(): pl.pallas_call(body, name=name, out_shape=[jax.ShapeDtypeStruct(s, t) for...  155 us
    ppermute x15, waiting for transfers between devices, swap(): return lax.ppermute(v, axis, [(j, j ^ 1 << bit) for j in range(count)])  49.5 us
    unnamed x57, local copies, waits for them, and re-layouts  15.4 us
    ppermute x15, starting transfers between devices, swap(): return lax.ppermute(v, axis, [(j, j ^ 1 << bit) for j in range(count)])  14.8 us
    all_to_all x1, starting transfers between devices, per_device(): lax.all_to_all(wanted, 'edge', split_axis=0, concat_axis=0, tiled=True)  6.35 us
  transfers between devices with their start and end apart: 18, of which 10 were waited for; matrix products, arithmetic and copies ran while one was open for 13% of the time, Pallas kernels for 27%

profile of v1, /device:TPU:0, one launch (start us, length us, event | category | flops | bytes accessed | tf_op | source)
XLA Modules:
  0.0 296.0 jit_solution(13982061806087778083)
XLA Ops:
  0.7 1.4 bitcast_subtract_fusion
  2.0 6.4 %all-to-all-start = ((s32[8,1,16]{2,1,0:T(1,128)}), s32[8,1,16]{2,1,0:T(1,128)S(1)}, u32[]{:S(2)}, u32[]{:S(2)}) async-start(s32[8,1,16]{2,1,0:T(1,128)} %bitcast.3), calls=%async_computation | async-start | bytes 8192 | tf_op jit(solution)/shard_map/all_to_all | solution.py:503
  8.4 1.6 select_bitcast_fusion.i3
  10.0 9.8 %source_rows.1 = (bf16[96,2048]{1,0:T(8,128)(2,1)}, f32[96,2048]{1,0:T(8,128)}) custom-call(bf16[2048,512]{1,0:T(8,128)(2,1)} %edge.7, bf16[2048,128]{1,0:T(8,128)(2,1)} %radial.9, bf16[512,512]{1,0:T(8,128)(2,1)} %ws3.3, bf16[128,512]{1,0:T(8,128)(2,1)} %wr3.3, bf16[64,512]{1,0:T(8,128)(2,1)} %bitcast.116, bf16[512,512]{1,0:T(8,128)(2,1)} %ws4.3, ...), custom_call_target="tpu_custom_call" | custom-call | tf_op jit(solution)/shard_map/source_rows/pallas_call | solution.py:62
  21.1 1.4 convolution_convert_fusion
  24.7 5.1 %all-to-all-start.1 = ((bf16[8,2,768]{2,1,0:T(2,128)(2,1)}), bf16[8,2,768]{2,1,0:T(2,128)(2,1)S(1)}, u32[]{:S(2)}, u32[]{:S(2)}) async-start(bf16[8,2,768]{2,1,0:T(2,128)(2,1)} %reshape.244), calls=%async_computation.1 | async-start | bytes 49152 | tf_op jit(solution)/shard_map/all_to_all | solution.py:523
  30.4 1.4 copy.127.tcol
  34.2 1.3 all-to-all-done.1
  36.5 38.8 %gather_sums.1 = (bf16[1024,2048]{1,0:T(8,128)(2,1)}, bf16[1024,2048]{1,0:T(8,128)(2,1)}, f32[64,2048]{1,0:T(8,128)}, f32[32,2048]{1,0:T(8,128)}) custom-call(bf16[96,2048]{1,0:T(8,128)(2,1)} %get-tuple-element.64.tab, bf16[96,256]{1,0:T(8,128)(2,1)} %pad.15.ghost, s32[16,2048]{1,0:T(8,128)} %select_bitcast_fusion.i3, s32[8,2048]{1,0:T(8,128)} %select_bitcast_fusion.1.i4, ...), custom_call_target="tpu_custom_call" | custom-call | tf_op jit(solution)/shard_map/gather_sums/pallas_call | solution.py:62
  75.3 18.9 %edge_update.1 = (f32[2048,512]{1,0:T(8,128)}, bf16[2048,512]{1,0:T(8,128)(2,1)}, bf16[2048,512]{1,0:T(8,128)(2,1)}, bf16[2048,512]{1,0:T(8,128)(2,1)}, bf16[204...) custom-call(bf16[2048,512]{1,0:T(8,128)(2,1)} %edge.7, ...), custom_call_target="tpu_custom_call" | custom-call | tf_op jit(solution)/shard_map/edge_update/pallas_call | solution.py:62
  94.2 16.2 %output_block.1 = (bf16[2048,512]{1,0:T(8,128)(2,1)}, f32[2048,512]{1,0:T(8,128)}, bf16[768,512]{1,0:T(8,128)(2,1)}, bf16[128,512]{1,0:T(8,128)(2,1)}, bf16[512,...) custom-call(f32[2048,512]{1,0:T(8,128)} %get-tuple-element.67.merged, ...), custom_call_target="tpu_custom_call" | custom-call | tf_op jit(solution)/shard_map/output_block/pallas_call | solution.py:62
  110.5 1.5 pad_maximum_fusion
  113.0 20.5 %edge_update_back.1 = (f32[2048,512]{1,0:T(8,128)}, bf16[64,2048]{1,0:T(8,128)(2,1)}, bf16[32,2048]{1,0:T(8,128)(2,1)}, bf16[512,512]{1,0:T(8,128)(2,1)}, bf16[5...) custom-call(bf16[2048,512]{1,0:T(8,128)(2,1)} %edge.7, ...), custom_call_target="tpu_custom_call" | custom-call | tf_op jit(solution)/shard_map/edge_update_back/pallas_call | solution.py:62
  134.6 1.5 pad_slice_fusion.7
  136.1 31.4 %scatter_sums.1 = (f32[96,2304]{1,0:T(8,128)}, bf16[1024,96]{1,0:T(8,128)(2,1)}) custom-call(bf16[64,2048]{1,0:T(8,128)(2,1)} %get-tuple-element.83.lb3, bf16[32,2048]{1,0:T(8,128)(2,1)} %get-tuple-element.84.lb4, s32[16,2048]{1,0:T(8,128)} %select_bitcast_fusion.i3, s32[8,2048]{1,0:T(8,128)} %select_bitcast_fusion.1.i4, bf16[2048,256]{1,0:T(8,128)(2,1)} %b3.3, ...), custom_call_target="tpu_custom_call" | custom-call | tf_op jit(solution)/shard_map/scatter_sums/pallas_call | solution.py:62
  167.4 1.7 pad_slice_fusion.3
  169.1 1.4 fusion.10
  170.5 1.5 copy.131
  172.0 1.5 all_to_all.22
  173.4 2.2 reduce.9
  175.6 1.4 reshape.246
  177.0 4.0 %all-to-all-start.2 = ((bf16[8,2,768]{2,1,0:T(2,128)(2,1)}), bf16[8,2,768]{2,1,0:T(2,128)(2,1)}, u32[]{:S(2)}, u32[]{:S(2)}) async-start(bf16[8,2,768]{2,1,0:T(2,128)(2,1)} %reshape.246), calls=%async_computation.2 | async-start | bytes 49152 | tf_op jit(solution)/shard_map/all_to_all | solution.py:610
  181.1 1.2 constant_dynamic-update-slice_fusion.6
  183.6 3.2 %all-to-all-done.2 = bf16[8,2,768]{2,1,0:T(2,128)(2,1)} async-done(((bf16[8,2,768]{2,1,0:T(2,128)(2,1)}), bf16[8,2,768]{2,1,0:T(2,128)(2,1)}, u32[]{:S(2)}, u32[]{:S(2)}) %all-to-all-start.2) | async-done | bytes 24608 | tf_op jit(solution)/shard_map/all_to_all | solution.py:610
  186.7 1.4 reshape.247
  188.1 1.5 reduce.2
  189.7 1.4 reshape.217
  191.1 1.5 copy.133
  192.6 19.0 %source_rows_back.1 = (bf16[2048,512]{1,0:T(8,128)(2,1)}, bf16[512,512]{1,0:T(8,128)(2,1)}, bf16[512,512]{1,0:T(8,128)(2,1)}, bf16[128,512]{1,0:T(8,128)(2,1)}, ...) custom-call(bf16[2048,512]{1,0:T(8,128)(2,1)} %edge.7, bf16[2048,128]{1,0:T(8,128)(2,1)} %radial.9, ...), custom_call_target="tpu_custom_call" | custom-call | tf_op jit(solution)/shard_map/source_rows_back/pallas_call | solution.py:62
  214.8 1.1 copy-done
  218.4 1.4 fusion.1
  220.6 1.3 fusion.2
  221.9 1.5 collective-permute-start.1
  223.4 1.5 fusion
  225.7 5.6 %collective-permute-done.11 = bf16[2,176,512]{2,1,0:T(8,128)(2,1)S(1)} collective-permute-done((bf16[2,176,512]{2,1,0:T(8,128)(2,1)S(1)}, bf16[2,176,512]{2,1,0:T(8,128)(2,1)S(1)}, u32[]{:S(2)}, u32[]{:S(2)}) %collective-permute-start.11) | collective-permute-done | bytes 360480 | tf_op jit(solution)/shard_map/ppermute | solution.py:438
  232.0 10.8 %collective-permute-done.1 = bf16[2,176,512]{2,1,0:T(8,128)(2,1)S(1)} collective-permute-done((bf16[2,176,512]{2,1,0:T(8,128)(2,1)S(1)}, bf16[2,176,512]{2,1,0:T(8,128)(2,1)S(1)}, u32[]{:S(2)}, u32[]{:S(2)}) %collective-permute-start.1) | collective-permute-done | bytes 360480 | tf_op jit(solution)/shard_map/ppermute | solution.py:438
  243.1 9.2 %collective-permute-done.12 = bf16[1,176,512]{2,1,0:T(8,128)(2,1)S(1)} collective-permute-done((bf16[1,176,512]{2,1,0:T(8,128)(2,1)S(1)}, bf16[1,176,512]{2,1,0:T(8,128)(2,1)S(1)}, u32[]{:S(2)}, u32[]{:S(2)}) %collective-permute-start.12) | collective-permute-done | bytes 180256 | tf_op jit(solution)/shard_map/ppermute | solution.py:438
  252.3 1.5 collective-permute-start.13
  253.8 3.3 %collective-permute-done.2 = bf16[1,176,512]{2,1,0:T(8,128)(2,1)S(1)} collective-permute-done((bf16[1,176,512]{2,1,0:T(8,128)(2,1)S(1)}, bf16[1,176,512]{2,1,0:T(8,128)(2,1)S(1)}, u32[]{:S(2)}, u32[]{:S(2)}) %collective-permute-start.2) | collective-permute-done | bytes 180256 | tf_op jit(solution)/shard_map/ppermute | solution.py:438
  257.2 1.5 collective-permute-start.3
  258.8 1.6 collective-permute-start.14
  260.4 2.4 collective-permute-done.3
  262.8 1.6 collective-permute-start.4
  264.6 2.4 collective-permute-start.7
  269.0 8.9 %collective-permute-done.7 = bf16[1,256,512]{2,1,0:T(8,128)(2,1)S(1)} collective-permute-done((bf16[1,256,512]{2,1,0:T(8,128)(2,1)S(1)}, bf16[1,256,512]{2,1,0:T(8,128)(2,1)S(1)}, u32[]{:S(2)}, u32[]{:S(2)}) %collective-permute-start.7) | collective-permute-done | bytes 262176 | tf_op jit(solution)/shard_map/ppermute | solution.py:438
  278.0 1.6 collective-permute-start.8
  280.2 4.9 %collective-permute-done.8 = bf16[256,512]{1,0:T(8,128)(2,1)S(1)} collective-permute-done((bf16[256,512]{1,0:T(8,128)(2,1)S(1)}, bf16[256,512]{1,0:T(8,128)(2,1)S(1)}, u32[]{:S(2)}, u32[]{:S(2)}) %collective-permute-start.8) | collective-permute-done | bytes 262176 | tf_op jit(solution)/shard_map/ppermute | solution.py:438
  287.2 4.4 %collective-permute-done.9 = bf16[256,512]{1,0:T(8,128)(2,1)S(1)} collective-permute-done((bf16[256,512]{1,0:T(8,128)(2,1)S(1)}, bf16[256,512]{1,0:T(8,128)(2,1)S(1)}, u32[]{:S(2)}, u32[]{:S(2)}) %collective-permute-start.9) | collective-permute-done | bytes 262176 | tf_op jit(solution)/shard_map/ppermute | solution.py:438
  (124 shorter events, 28.4 us)
Async XLA Ops:
  2.0 17.8 %all-to-all-start = ((s32[8,1,16]{2,1,0:T(1,128)}), s32[8,1,16]{2,1,0:T(1,128)S(1)}, u32[]{:S(2)}, u32[]{:S(2)}) async-start(s32[8,1,16]{2,1,0:T(1,128)} %bitcast.3), calls=%async_computation | async-start | bytes 8192 | tf_op jit(solution)/shard_map/all_to_all | solution.py:503
  10.0 19.8 %copy-start.17 = (s32[2048,8]{0,1:T(8,128)S(1)}, s32[2048,8]{0,1:T(8,128)}, u32[]{:S(2)}) copy-start(s32[2048,8]{0,1:T(8,128)} %param.39) | copy-start | bytes 196612
  10.0 19.8 %copy-start.18 = (s32[2048,8]{0,1:T(8,128)S(1)}, s32[2048,8]{0,1:T(8,128)}, u32[]{:S(2)}) copy-start(s32[2048,8]{0,1:T(8,128)} %param.40) | copy-start | bytes 196612
  10.0 20.4 %copy-start.16 = (s32[1,2048]{1,0:T(1,128)S(1)}, s32[1,2048]{1,0:T(1,128)}, u32[]{:S(2)}) copy-start(s32[1,2048]{1,0:T(1,128)} %trow.3) | copy-start | bytes 24580
  19.8 12.0 %copy-start.2 = (bf16[1024,64]{0,1:T(8,128)(2,1)S(1)}, bf16[1024,64]{0,1:T(8,128)(2,1)}, u32[]{:S(2)}) copy-start(bf16[1024,64]{0,1:T(8,128)(2,1)} %param.49) | copy-start | bytes 393220
  19.8 12.8 %copy-start.3 = (bf16[1024,32]{0,1:T(8,128)(2,1)S(1)}, bf16[1024,32]{0,1:T(8,128)(2,1)}, u32[]{:S(2)}) copy-start(bf16[1024,32]{0,1:T(8,128)(2,1)} %param.51) | copy-start | bytes 196612
  24.7 10.8 %all-to-all-start.1 = ((bf16[8,2,768]{2,1,0:T(2,128)(2,1)}), bf16[8,2,768]{2,1,0:T(2,128)(2,1)S(1)}, u32[]{:S(2)}, u32[]{:S(2)}) async-start(bf16[8,2,768]{2,1,0:T(2,128)(2,1)} %reshape.244), calls=%async_computation.1 | async-start | bytes 49152 | tf_op jit(solution)/shard_map/all_to_all | solution.py:523
  112.9 105.5 %collective-permute-start.10 = (bf16[4,176,512]{2,1,0:T(8,128)(2,1)}, bf16[4,176,512]{2,1,0:T(8,128)(2,1)}, u32[]{:S(2)}, u32[]{:S(2)}) collective-permute-start(bf16[4,176,512]{2,1,0:T(8,128)(2,1)} %dynamic-slice_bitcast_fusion.1), channel_id=1, source_target_pairs={{0,1},{1,0},{2,3},{3,2},{4,5},{5,4},{6,7},{7,6},{8,9},{9,8},{10,11... | collective-permute-start | bytes 2162696 | tf_op jit(solution)/shard_map/ppermute | solution.py:438
  177.0 9.8 %all-to-all-start.2 = ((bf16[8,2,768]{2,1,0:T(2,128)(2,1)}), bf16[8,2,768]{2,1,0:T(2,128)(2,1)}, u32[]{:S(2)}, u32[]{:S(2)}) async-start(bf16[8,2,768]{2,1,0:T(2,128)(2,1)} %reshape.246), calls=%async_computation.2 | async-start | bytes 49152 | tf_op jit(solution)/shard_map/all_to_all | solution.py:610
  181.0 2.4 copy-start.8
  181.0 2.4 copy-start.12
  181.0 2.4 copy-start.13
  181.0 2.4 copy-start.14
  181.0 2.4 copy-start.15
  181.0 2.5 copy-start.4
  181.0 2.5 copy-start.5
  181.0 2.5 copy-start.6
  181.1 2.5 copy-start.7
  211.6 3.1 %copy-start.10 = (bf16[128,512]{1,0:T(8,128)(2,1)S(1)}, bf16[128,512]{1,0:T(8,128)(2,1)}, u32[]{:S(2)}) copy-start(bf16[128,512]{1,0:T(8,128)(2,1)} %get-tuple-element.93) | copy-start | bytes 393220
  211.6 3.1 %copy-start.9 = (bf16[128,512]{1,0:T(8,128)(2,1)S(1)}, bf16[128,512]{1,0:T(8,128)(2,1)}, u32[]{:S(2)}) copy-start(bf16[128,512]{1,0:T(8,128)(2,1)} %get-tuple-element.94) | copy-start | bytes 393220
  214.8 1.1 copy-start
  216.9 3.7 %collective-permute-start = (bf16[4,176,512]{2,1,0:T(8,128)(2,1)}, bf16[4,176,512]{2,1,0:T(8,128)(2,1)}, u32[]{:S(2)}, u32[]{:S(2)}) collective-permute-start(bf16[4,176,512]{2,1,0:T(8,128)(2,1)} %dynamic-slice_bitcast_fusion.2), channel_id=1, source_target_pairs={{0,1},{1,0},{2,3},{3,2},{4,5},{5,4},{6,7},{7,6},{8,9},{9,8},{10,11... | collective-permute-start | bytes 2162696 | tf_op jit(solution)/shard_map/ppermute | solution.py:438
  217.9 5.5 %collective-permute-start.5 = (bf16[4,256,512]{2,1,0:T(8,128)(2,1)}, bf16[4,256,512]{2,1,0:T(8,128)(2,1)}, u32[]{:S(2)}, u32[]{:S(2)}) collective-permute-start(bf16[4,256,512]{2,1,0:T(8,128)(2,1)} %dynamic-slice_bitcast_fusion), channel_id=1, source_target_pairs={{0,1},{1,0},{2,3},{3,2},{4,5},{5,4},{6,7},{7,6},{8,9},{9,8},{10,11... | collective-permute-start | bytes 3145736 | tf_op jit(solution)/shard_map/ppermute | solution.py:438
  218.4 2.2 copy-start.1
  219.9 11.4 %collective-permute-start.11 = (bf16[2,176,512]{2,1,0:T(8,128)(2,1)S(1)}, bf16[2,176,512]{2,1,0:T(8,128)(2,1)S(1)}, u32[]{:S(2)}, u32[]{:S(2)}) collective-permute-start(bf16[2,176,512]{2,1,0:T(8,128)(2,1)S(1)} %dynamic-slice_bitcast_fusion.4), channel_id=1, source_target_pairs={{0,2},{1,3},{2,0},{3,1},{4,6},{5,7},{6,4},{7,5},{8,10},{9,11},{10,... | collective-permute-start | bytes 1081352 | tf_op jit(solution)/shard_map/ppermute | solution.py:438
  221.9 20.9 %collective-permute-start.1 = (bf16[2,176,512]{2,1,0:T(8,128)(2,1)S(1)}, bf16[2,176,512]{2,1,0:T(8,128)(2,1)S(1)}, u32[]{:S(2)}, u32[]{:S(2)}) collective-permute-start(bf16[2,176,512]{2,1,0:T(8,128)(2,1)S(1)} %dynamic-slice_bitcast_fusion.5), channel_id=1, source_target_pairs={{0,2},{1,3},{2,0},{3,1},{4,6},{5,7},{6,4},{7,5},{8,10},{9,11},{10,... | collective-permute-start | bytes 1081352 | tf_op jit(solution)/shard_map/ppermute | solution.py:438
  225.0 39.4 %collective-permute-start.6 = (bf16[2,256,512]{2,1,0:T(8,128)(2,1)S(1)}, bf16[2,256,512]{2,1,0:T(8,128)(2,1)S(1)}, u32[]{:S(2)}, u32[]{:S(2)}) collective-permute-start(bf16[2,256,512]{2,1,0:T(8,128)(2,1)S(1)} %dynamic-slice_bitcast_fusion.3), channel_id=1, source_target_pairs={{0,2},{1,3},{2,0},{3,1},{4,6},{5,7},{6,4},{7,5},{8,10},{9,11},{10,... | collective-permute-start | bytes 1572872 | tf_op jit(solution)/shard_map/ppermute | solution.py:438
  231.4 20.8 %collective-permute-start.12 = (bf16[1,176,512]{2,1,0:T(8,128)(2,1)S(1)}, bf16[1,176,512]{2,1,0:T(8,128)(2,1)S(1)}, u32[]{:S(2)}, u32[]{:S(2)}) collective-permute-start(bf16[1,176,512]{2,1,0:T(8,128)(2,1)S(1)} %constant_dynamic-slice_fusion), channel_id=1, source_target_pairs={{0,4},{1,5},{2,6},{3,7},{4,0},{5,1},{6,2},{7,3},{8,12},{9,13},{10,... | collective-permute-start | bytes 540680 | tf_op jit(solution)/shard_map/ppermute | solution.py:438
  243.0 14.2 %collective-permute-start.2 = (bf16[1,176,512]{2,1,0:T(8,128)(2,1)S(1)}, bf16[1,176,512]{2,1,0:T(8,128)(2,1)S(1)}, u32[]{:S(2)}, u32[]{:S(2)}) collective-permute-start(bf16[1,176,512]{2,1,0:T(8,128)(2,1)S(1)} %constant_dynamic-slice_fusion.2), channel_id=1, source_target_pairs={{0,4},{1,5},{2,6},{3,7},{4,0},{5,1},{6,2},{7,3},{8,12},{9,13},{10,... | collective-permute-start | bytes 540680 | tf_op jit(solution)/shard_map/ppermute | solution.py:438
  252.3 6.5 %collective-permute-start.13 = (bf16[176,512]{1,0:T(8,128)(2,1)S(1)}, bf16[176,512]{1,0:T(8,128)(2,1)S(1)}, u32[]{:S(2)}, u32[]{:S(2)}) collective-permute-start(bf16[176,512]{1,0:T(8,128)(2,1)S(1)} %fusion.9), channel_id=1, source_target_pairs={{0,8},{8,0},{16,24},{24,16},{1,9},{9,1},{17,25},{25,17},{2,10},{10... | collective-permute-start | bytes 540680 | tf_op jit(solution)/shard_map/ppermute | solution.py:438
  257.2 5.6 %collective-permute-start.3 = (bf16[176,512]{1,0:T(8,128)(2,1)S(1)}, bf16[176,512]{1,0:T(8,128)(2,1)S(1)}, u32[]{:S(2)}, u32[]{:S(2)}) collective-permute-start(bf16[176,512]{1,0:T(8,128)(2,1)S(1)} %fusion.8), channel_id=1, source_target_pairs={{0,8},{8,0},{16,24},{24,16},{1,9},{9,1},{17,25},{25,17},{2,10},{10... | collective-permute-start | bytes 540680 | tf_op jit(solution)/shard_map/ppermute | solution.py:438
  258.8 8.1 %collective-permute-start.14 = (bf16[176,512]{1,0:T(8,128)(2,1)S(1)}, bf16[176,512]{1,0:T(8,128)(2,1)S(1)}, u32[]{:S(2)}, u32[]{:S(2)}) collective-permute-start(bf16[176,512]{1,0:T(8,128)(2,1)S(1)} %add_convert_fusion.2), channel_id=1, source_target_pairs={{0,16},{8,24},{16,0},{24,8},{1,17},{9,25},{17,1},{25,9},{2,18},{10... | collective-permute-start | bytes 540680 | tf_op jit(solution)/shard_map/ppermute | solution.py:438
  262.8 6.1 %collective-permute-start.4 = (bf16[176,512]{1,0:T(8,128)(2,1)S(1)}, bf16[176,512]{1,0:T(8,128)(2,1)S(1)}, u32[]{:S(2)}, u32[]{:S(2)}) collective-permute-start(bf16[176,512]{1,0:T(8,128)(2,1)S(1)} %add_convert_fusion.4), channel_id=1, source_target_pairs={{0,16},{8,24},{16,0},{24,8},{1,17},{9,25},{17,1},{25,9},{2,18},{10... | collective-permute-start | bytes 540680 | tf_op jit(solution)/shard_map/ppermute | solution.py:438
  264.6 13.3 %collective-permute-start.7 = (bf16[1,256,512]{2,1,0:T(8,128)(2,1)S(1)}, bf16[1,256,512]{2,1,0:T(8,128)(2,1)S(1)}, u32[]{:S(2)}, u32[]{:S(2)}) collective-permute-start(bf16[1,256,512]{2,1,0:T(8,128)(2,1)S(1)} %constant_dynamic-slice_fusion.1), channel_id=1, source_target_pairs={{0,4},{1,5},{2,6},{3,7},{4,0},{5,1},{6,2},{7,3},{8,12},{9,13},{10,... | collective-permute-start | bytes 786440 | tf_op jit(solution)/shard_map/ppermute | solution.py:438
  278.0 7.1 %collective-permute-start.8 = (bf16[256,512]{1,0:T(8,128)(2,1)S(1)}, bf16[256,512]{1,0:T(8,128)(2,1)S(1)}, u32[]{:S(2)}, u32[]{:S(2)}) collective-permute-start(bf16[256,512]{1,0:T(8,128)(2,1)S(1)} %fusion.7), channel_id=1, source_target_pairs={{0,8},{8,0},{16,24},{24,16},{1,9},{9,1},{17,25},{25,17},{2,10},{10... | collective-permute-start | bytes 786440 | tf_op jit(solution)/shard_map/ppermute | solution.py:438
  285.2 6.4 %collective-permute-start.9 = (bf16[256,512]{1,0:T(8,128)(2,1)S(1)}, bf16[256,512]{1,0:T(8,128)(2,1)S(1)}, u32[]{:S(2)}, u32[]{:S(2)}) collective-permute-start(bf16[256,512]{1,0:T(8,128)(2,1)S(1)} %add_convert_fusion), channel_id=1, source_target_pairs={{0,16},{8,24},{16,0},{24,8},{1,17},{9,25},{17,1},{25,9},{2,18},{10... | collective-permute-start | bytes 786440 | tf_op jit(solution)/shard_map/ppermute | solution.py:438
  285.8 10.3 %copy-start.11 = (f32[64,96]{1,0:T(8,128)}, f32[64,96]{1,0:T(8,128)S(1)}, u32[]{:S(2)}) copy-start(f32[64,96]{1,0:T(8,128)S(1)} %pad_maximum_fusion.2) | copy-start | bytes 73732

commit v2 on v1

v2 whole, which is shorter than its diff:
```python
import functools
import math

import jax
import jax.numpy as jnp
from jax import lax
from jax.experimental import pallas as pl
from jax.experimental.pallas import tpu as pltpu
from jax.sharding import PartitionSpec as P

HALF_ROOT = 1.0 / math.sqrt(2.0)
THIRD_ROOT = 1.0 / math.sqrt(3.0)
LOW = jnp.bfloat16
WIDE = jnp.float32
TILE = 256
LANES = 128
VMEM_BYTES = 60 * 1024 * 1024


def sigma(v):
    return 0.5 * jnp.tanh(0.5 * v) + 0.5


def slope_of(v, s):
    return s * (1.0 + v * (1.0 - s))


def nn(a, b):
    return jnp.dot(a, b, preferred_element_type=WIDE)


def nt(a, b):
    return lax.dot_general(a, b, (((1,), (1,)), ((), ())), preferred_element_type=WIDE)


def tn(a, b):
    return lax.dot_general(a, b, (((0,), (0,)), ((), ())), preferred_element_type=WIDE)


def split_pair(v):
    high = v.astype(LOW)
    rest = (v - high.astype(WIDE)).astype(LOW)
    return jnp.concatenate([high, rest], axis=0)


def whole(array):
    rank = len(array.shape)
    return pl.BlockSpec(array.shape, lambda i: (0,) * rank)


def rows(width):
    return pl.BlockSpec((TILE, width), lambda i: (i, 0))


def cols(height):
    return pl.BlockSpec((height, TILE), lambda i: (0, i))


def fixed(*shape):
    return pl.BlockSpec(shape, lambda i: (0,) * len(shape))


def call(body, name, steps, micros, ins, in_specs, outs, out_specs, scratch):
    return pl.pallas_call(
        body,
        name=name,
        out_shape=[jax.ShapeDtypeStruct(s, t) for s, t in outs],
        grid_spec=pltpu.PrefetchScalarGridSpec(
            num_scalar_prefetch=0,
            grid=(steps,),
            in_specs=in_specs,
            out_specs=out_specs,
            scratch_shapes=scratch,
        ),
        compiler_params=pltpu.CompilerParams(
            dimension_semantics=("arbitrary",), vmem_limit_bytes=VMEM_BYTES
        ),
        cost_estimate=pl.CostEstimate(
            flops=int(micros * 1.1e9), transcendentals=0, bytes_accessed=1 << 22
        ),
    )(*ins)


def source_body(
    edge, radial, asked, ws3, wr3, wd3, ws4, wr4, wd4, table, down, sent, t3, t4, acc
):
    step = pl.program_id(0)
    ghosts = asked.shape[1]

    @pl.when(step == 0)
    def _():
        t3[...] = wd3[...].astype(WIDE).T.astype(LOW)
        t4[...] = wd4[...].astype(WIDE).T.astype(LOW)
        acc[...] = jnp.zeros_like(acc)

    e = edge[...]
    r = radial[...]
    pre3 = nn(e, ws3[...])
    mix3 = (pre3 * sigma(pre3) * nn(r, wr3[...])).astype(LOW)
    down3 = nt(t3[...], mix3)
    pre4 = nn(e, ws4[...])
    mix4 = (pre4 * sigma(pre4) * nn(r, wr4[...])).astype(LOW)
    down4 = nt(t4[...], mix4)
    both = jnp.concatenate([down3, down4], axis=0)
    down[...] = both
    found = (both * sigma(both)).astype(LOW)
    table[...] = found
    place = lax.broadcasted_iota(jnp.int32, (TILE, ghosts), 0) + step * TILE
    acc[0 : found.shape[0], :] += nn(found, (place == asked[...]).astype(LOW))

    @pl.when(step == pl.num_programs(0) - 1)
    def _():
        sent[...] = acc[...].T.astype(LOW)


def fill_slabs(tab, ghost, t3, t4, n3, n4):
    local = tab.shape[1] // TILE
    for s in range(local):
        t3[s * n3 : (s + 1) * n3, :] = tab[0:n3, s * TILE : (s + 1) * TILE]
        t4[s * n4 : (s + 1) * n4, :] = tab[n3 : n3 + n4, s * TILE : (s + 1) * TILE]
    for g in range(0, ghost.shape[0], TILE):
        s = local + g // TILE
        size = min(TILE, ghost.shape[0] - g)
        part = ghost[g : g + size, :].astype(WIDE).T
        if size < TILE:
            part = jnp.concatenate([part, jnp.zeros((LANES, TILE - size), WIDE)], axis=1)
        t3[s * n3 : (s + 1) * n3, :] = part[0:n3, :].astype(LOW)
        t4[s * n4 : (s + 1) * n4, :] = part[n3 : n3 + n4, :].astype(LOW)


def pick(tab, index_row, width):
    slabs = tab.shape[0] // width
    low_part = index_row & (TILE - 1)
    slab = index_row >> 8
    hot = (lax.broadcasted_iota(jnp.int32, (TILE, TILE), 0) == low_part).astype(LOW)
    found = nn(tab[...], hot)
    got = jnp.zeros((width, TILE), WIDE)
    for s in range(slabs):
        got = jnp.where(slab == s, found[s * width : (s + 1) * width, :], got)
    return got


def weigh(coef, picked, out, slots, basis, width):
    chunk = 32
    for h in range(width // chunk):
        for cb in range(basis // 4):
            acc = [None] * 4
            for k in range(slots):
                g = picked[k, h * chunk : (h + 1) * chunk, :]
                for j in range(4):
                    row = k * basis + cb * 4 + j
                    term = coef[row : row + 1, :] * g
                    acc[j] = term if acc[j] is None else acc[j] + term
            for j in range(4):
                at = (cb * 4 + j) * width + h * chunk
                out[at : at + chunk, :] = acc[j].astype(LOW)


def gather_body(
    tab, ghost, i3, i4, b3, b4, w3, w4, s3, s4, p3, p4, t3, t4, g3, g4, c3, c4, w3t, w4t
):
    n3, n4 = w3t.shape[0], w4t.shape[0]
    k3, k4 = i3.shape[0], i4.shape[0]

    @pl.when(pl.program_id(0) == 0)
    def _():
        w3t[...] = w3[...].astype(WIDE).T.astype(LOW)
        w4t[...] = w4[...].astype(WIDE).T.astype(LOW)
        fill_slabs(tab, ghost, t3, t4, n3, n4)

    c3[...] = b3[...].astype(WIDE).T
    c4[...] = b4[...].astype(WIDE).T

    def step3(k, carry):
        g3[k] = pick(t3, i3[pl.ds(k, 1), :], n3)
        return carry

    lax.fori_loop(0, k3, step3, 0, unroll=4)

    def step4(k, carry):
        g4[k] = pick(t4, i4[pl.ds(k, 1), :], n4)
        return carry

    lax.fori_loop(0, k4, step4, 0, unroll=4)
    weigh(c3, g3, s3, k3, c3.shape[0] // k3, n3)
    weigh(c4, g4, s4, k4, c4.shape[0] // k4, n4)
    p3[...] = nn(w3t[...], s3[...])
    p4[...] = nn(w4t[...], s4[...])


def mix_body(
    edge, radial, p3, p4, trow, wu3, wu4, wsk, wr1, wr2, wra, wat, atom,
    merged, mixlow, reshid, dsk, du3, du4, dr1, dr2, gath, anew, aslope, acc,
):
    step = pl.program_id(0)
    atoms = acc.shape[0]
    v3 = p3[...]
    v4 = p4[...]
    h3 = (v3 * sigma(v3)).T.astype(LOW)
    h4 = (v4 * sigma(v4)).T.astype(LOW)
    up3 = nn(h3, wu3[...])
    s = sigma(up3)
    du3[...] = slope_of(up3, s).astype(LOW)
    total = up3 * s
    up4 = nn(h4, wu4[...])
    s = sigma(up4)
    du4[...] = slope_of(up4, s).astype(LOW)
    total = total + up4 * s
    skip = nn(edge[...], wsk[...])
    s = sigma(skip)
    dsk[...] = slope_of(skip, s).astype(LOW)
    mixed = (total + skip * s) * THIRD_ROOT
    low_mixed = mixed.astype(LOW)
    mixlow[...] = low_mixed
    res = nn(low_mixed, wr1[...])
    s = sigma(res)
    dr1[...] = slope_of(res, s).astype(LOW)
    hid = (res * s).astype(LOW)
    reshid[...] = hid
    res2 = nn(hid, wr2[...])
    s = sigma(res2)
    dr2[...] = (0.5 * slope_of(res2, s)).astype(LOW)
    out = (edge[...].astype(WIDE) + (mixed + res2 * s) * HALF_ROOT) * HALF_ROOT
    merged[...] = out
    weighted = (out * nn(radial[...], wra[...])).astype(LOW)
    hot_t = (lax.broadcasted_iota(jnp.int32, (atoms, TILE), 0) == trow[...]).astype(LOW)
    part = nn(hot_t, weighted)

    @pl.when(step == 0)
    def _():
        acc[...] = part

    @pl.when(step > 0)
    def _():
        acc[...] += part

    @pl.when(step == pl.num_programs(0) - 1)
    def _():
        g = acc[...].astype(LOW)
        gath[...] = g
        pre = nn(g, wat[...])
        sa = sigma(pre)
        aslope[...] = HALF_ROOT * slope_of(pre, sa)
        anew[...] = ((atom[...].astype(WIDE) + pre * sa) * HALF_ROOT).astype(LOW)


def out_body(
    merged, radial, trow, anew, cot, wc, wro, wout, ocot, acot, aslope, gath, wat,
    enew, gmer, gwc, gro, goa, aout, gatom, gw2, ogat, seg, both, awc, aro,
):
    step = pl.program_id(0)
    atoms, wide = ogat.shape
    aw = anew.shape[1]

    @pl.when(step == 0)
    def _():
        both[:, 0:wide] = split_pair(nt(ocot[...], wout[...]))
        both[:, wide : 2 * wide] = split_pair(nn(anew[...], wc[0:aw, :]))
        ogat[...] = jnp.zeros_like(ogat)
        seg[...] = jnp.zeros_like(seg)
        awc[...] = jnp.zeros_like(awc)
        aro[...] = jnp.zeros_like(aro)

    hot_t = (lax.broadcasted_iota(jnp.int32, (atoms, TILE), 0) == trow[...]).astype(LOW)
    spread = tn(jnp.concatenate([hot_t, hot_t], axis=0), both[...])
    gow = spread[:, 0:wide]
    m = merged[...]
    ml = m.astype(LOW)
    wcm = wc[aw:, :]
    pre = spread[:, wide:] + nn(ml, wcm)
    s = sigma(pre)
    new = (m + pre * s) * HALF_ROOT
    enew[...] = new.astype(LOW)
    rout = nn(radial[...], wro[...])
    ogat[...] += nn(hot_t, (new * rout).astype(LOW))
    gnew = cot[...].astype(WIDE) + gow * rout
    aro[...] += tn(radial[...], (gow * new).astype(LOW))
    lc = (gnew * (HALF_ROOT * slope_of(pre, s))).astype(LOW)
    awc[...] += tn(ml, lc)
    seg[...] += nn(hot_t, lc)
    gmer[...] = gnew * HALF_ROOT + nt(lc, wcm)

    @pl.when(step == pl.num_programs(0) - 1)
    def _():
        ol = ogat[...].astype(LOW)
        aout[...] = nn(ol, wout[...]).astype(LOW)
        goa[:, 0:aw] = tn(ol, ocot[...]).astype(LOW)
        gwc[aw:, :] = awc[...].astype(LOW)
        gro[...] = aro[...].astype(LOW)
        pair = split_pair(seg[...])
        hi = pair[0:atoms, :]
        lo = pair[atoms:, :]
        gwc[0:aw, :] = (tn(anew[...], hi) + tn(anew[...], lo)).astype(LOW)
        wca = wc[0:aw, :]
        ga = acot[...].astype(WIDE) + nt(hi, wca) + nt(lo, wca)
        gatom[...] = (ga * HALF_ROOT).astype(LOW)
        la = (ga * aslope[...]).astype(LOW)
        goa[:, aw : 2 * aw] = tn(gath[...], la).astype(LOW)
        gw2[...] = split_pair(nt(la, wat[...]))


def back_body(
    edge, radial, trow, s3, s4, merged, gmer, gw2, p3, p4, mixlow, reshid, dsk, du3, du4, dr1, dr2,
    wu3, wu4, wsk, wr1, wr2, wra,
    gpart, lb3, lb4, gsk, gr1, gr2, gra, gup, gbil, ask, ar1, ar2, ara, aup, abil,
):
    step = pl.program_id(0)
    pair = gw2.shape[0]
    n3 = wu3.shape[0]

    @pl.when(step == 0)
    def _():
        ask[...] = jnp.zeros_like(ask)
        ar1[...] = jnp.zeros_like(ar1)
        ar2[...] = jnp.zeros_like(ar2)
        ara[...] = jnp.zeros_like(ara)
        aup[...] = jnp.zeros_like(aup)
        abil[...] = jnp.zeros_like(abil)

    hot_t = (lax.broadcasted_iota(jnp.int32, (pair // 2, TILE), 0) == trow[...]).astype(LOW)
    gw = tn(jnp.concatenate([hot_t, hot_t], axis=0), gw2[...])
    gm = gmer[...] + gw * nn(radial[...], wra[...])
    ara[...] += tn(radial[...], (gw * merged[...]).astype(LOW))
    l2 = (gm * dr2[...].astype(WIDE)).astype(LOW)
    ar2[...] += tn(reshid[...], l2)
    l1 = (nt(l2, wr2[...]) * dr1[...].astype(WIDE)).astype(LOW)
    ar1[...] += tn(mixlow[...], l1)
    gmix = (gm * 0.5 + nt(l1, wr1[...])) * THIRD_ROOT
    ls = (gmix * dsk[...].astype(WIDE)).astype(LOW)
    l3 = (gmix * du3[...].astype(WIDE)).astype(LOW)
    l4 = (gmix * du4[...].astype(WIDE)).astype(LOW)
    ask[...] += tn(edge[...], ls)
    gpart[...] = gm * HALF_ROOT + nt(ls, wsk[...])
    v3 = p3[...]
    g3 = sigma(v3)
    v4 = p4[...]
    g4 = sigma(v4)
    aup[0:n3, :] += nn((v3 * g3).astype(LOW), l3)
    aup[n3:, :] += nn((v4 * g4).astype(LOW), l4)
    low3 = (nt(wu3[...], l3) * slope_of(v3, g3)).astype(LOW)
    low4 = (nt(wu4[...], l4) * slope_of(v4, g4)).astype(LOW)
    lb3[...] = low3
    lb4[...] = low4
    abil[:, 0:n3] += nt(s3[...], low3)
    abil[:, n3:] += nt(s4[...], low4)

    @pl.when(step == pl.num_programs(0) - 1)
    def _():
        gsk[...] = ask[...].astype(LOW)
        gr1[...] = ar1[...].astype(LOW)
        gr2[...] = ar2[...].astype(LOW)
        gra[...] = ara[...].astype(LOW)
        gup[...] = aup[...].T.astype(LOW)
        gbil[...] = abil[...].astype(LOW)


def unweigh(coef, dsum, index, spread, hots, slots, basis, width):
    chunk = 32
    slabs = spread.shape[0] // width
    for k in range(slots):
        low_part = index[k : k + 1, :] & (TILE - 1)
        hot = (lax.broadcasted_iota(jnp.int32, (TILE, TILE), 0) == low_part).astype(LOW)
        hots[:, k * TILE : (k + 1) * TILE] = hot
    for h in range(width // chunk):
        for kb in range(slots // 4):
            acc = [None] * 4
            for c in range(basis):
                at = c * width + h * chunk
                d = dsum[at : at + chunk, :]
                for j in range(4):
                    row = (kb * 4 + j) * basis + c
                    term = coef[row : row + 1, :] * d
                    acc[j] = term if acc[j] is None else acc[j] + term
            for j in range(4):
                k = kb * 4 + j
                slab = index[k : k + 1, :] >> 8
                for s in range(slabs):
                    at = s * width + h * chunk
                    spread[at : at + chunk, k * TILE : (k + 1) * TILE] = jnp.where(
                        slab == s, acc[j], 0.0
                    ).astype(LOW)


def scatter_body(lb, idx, basis, w, *rest, edges, other):
    if other:
        beside, grad, far, acc, coef, dsum, spread, hots = rest
    else:
        grad, far, acc, coef, dsum, spread, hots = rest
    step = pl.program_id(0)
    n = w.shape[1]
    slots = idx.shape[0]

    @pl.when(step == 0)
    def _():
        acc[...] = jnp.zeros_like(acc)

    coef[...] = basis[...].astype(WIDE).T
    dsum[...] = nn(w[...], lb[...])
    unweigh(coef, dsum, idx, spread, hots, slots, coef.shape[0] // slots, n)
    acc[...] += nt(spread[...], hots[...])

    @pl.when(step == pl.num_programs(0) - 1)
    def _():
        local = edges // TILE
        for s in range(local):
            grad[:, s * TILE : (s + 1) * TILE] = acc[s * n : (s + 1) * n, :]
        for s in range(local, acc.shape[0] // n):
            part = acc[s * n : (s + 1) * n, :]
            if other:
                more = beside[:, (s - local) * TILE : (s - local + 1) * TILE]
                filler = jnp.zeros((LANES - n - more.shape[0], TILE), WIDE)
                part = jnp.concatenate([part, more, filler], axis=0).T.astype(LOW)
                size = min(TILE, far.shape[0] - (s - local) * TILE)
                far[(s - local) * TILE : (s - local) * TILE + size, :] = part[0:size, :]
            else:
                far[:, (s - local) * TILE : (s - local + 1) * TILE] = part


def source_back_body(
    edge, radial, gpart, grad3, grad4, down, ret, asked, ws3, wr3, wd3, ws4, wr4, wd4,
    gedge, gs3, gs4, gr3, gr4, gdn, as3, as4, ar3, ar4, adn, t3, t4, rt,
):
    step = pl.program_id(0)
    n3, n4 = grad3.shape[0], grad4.shape[0]

    @pl.when(step == 0)
    def _():
        t3[...] = wd3[...].astype(WIDE).T.astype(LOW)
        t4[...] = wd4[...].astype(WIDE).T.astype(LOW)
        rt[...] = ret[...].astype(WIDE).T.astype(LOW)
        as3[...] = jnp.zeros_like(as3)
        as4[...] = jnp.zeros_like(as4)
        ar3[...] = jnp.zeros_like(ar3)
        ar4[...] = jnp.zeros_like(ar4)
        adn[...] = jnp.zeros_like(adn)

    place = lax.broadcasted_iota(jnp.int32, (TILE, asked.shape[1]), 0) + step * TILE
    back = nt(rt[...], (place == asked[...]).astype(LOW))
    v = down[...]
    ld = jnp.concatenate([grad3[...], grad4[...]], axis=0) + back[0 : n3 + n4, :]
    ld = ld * slope_of(v, sigma(v))
    ldt = ld.astype(LOW)
    low_rows = ld.T.astype(LOW)
    e = edge[...]
    r = radial[...]
    pre = nn(e, ws3[...])
    rad = nn(r, wr3[...])
    s = sigma(pre)
    act = pre * s
    adn[0:n3, :] += nn(ldt[0:n3, :], (act * rad).astype(LOW))
    gm = nn(low_rows[:, 0:n3], t3[...])
    l3 = (gm * rad * slope_of(pre, s)).astype(LOW)
    ar3[...] += tn(r, (gm * act).astype(LOW))
    as3[...] += tn(e, l3)
    pre = nn(e, ws4[...])
    rad = nn(r, wr4[...])
    s = sigma(pre)
    act = pre * s
    adn[n3:, :] += nn(ldt[n3:, :], (act * rad).astype(LOW))
    gm = nn(low_rows[:, n3:], t4[...])
    l4 = (gm * rad * slope_of(pre, s)).astype(LOW)
    ar4[...] += tn(r, (gm * act).astype(LOW))
    as4[...] += tn(e, l4)
    gedge[...] = (gpart[...] + nt(l3, ws3[...]) + nt(l4, ws4[...])).astype(LOW)

    @pl.when(step == pl.num_programs(0) - 1)
    def _():
        gs3[...] = as3[...].astype(LOW)
        gs4[...] = as4[...].astype(LOW)
        gr3[...] = ar3[...].astype(LOW)
        gr4[...] = ar4[...].astype(LOW)
        gdn[...] = adn[...].T.astype(LOW)


def swap(v, axis, mask):
    count = lax.axis_size(axis)
    return lax.ppermute(v, axis, [(j, j ^ mask) for j in range(count)])


def groups_of(axis, first):
    top = lax.axis_size(axis).bit_length() - 1
    return [(at, min(2, top - at)) for at in range(first, top, 2)]


def scatter_step(v, axis, at, width):
    parts = 1 << width
    own = (lax.axis_index(axis) >> at) & (parts - 1)
    v = v.reshape(v.shape[0] // parts, parts, *v.shape[1:])
    total = lax.dynamic_index_in_dim(v, own, 1, keepdims=False).astype(WIDE)
    for m in range(1, parts):
        sent = lax.dynamic_index_in_dim(v, own ^ m, 1, keepdims=False)
        total = total + swap(sent, axis, m << at).astype(WIDE)
    return total.astype(LOW)


def core_sum(v):
    return scatter_step(v, "edge", 0, 1)


def group_sum(v):
    own = lax.axis_index("grp")
    total = lax.dynamic_index_in_dim(v, own, 1, keepdims=False).astype(WIDE)
    for m in range(1, v.shape[1]):
        sent = lax.dynamic_index_in_dim(v, own ^ m, 1, keepdims=False)
        total = total + swap(sent, "grp", m).astype(WIDE)
    return total.astype(LOW)


def share_sum(v):
    for at, width in groups_of("edge", 1):
        v = scatter_step(v, "edge", at, width)
    return v[0]


def group_gather(v):
    own = lax.axis_index("grp")
    count = lax.axis_size("grp")
    out = jnp.zeros((count,) + v.shape, LOW)
    out = lax.dynamic_update_index_in_dim(out, v, own, 0)
    for m in range(1, count):
        out = lax.dynamic_update_index_in_dim(out, swap(v, "grp", m), own ^ m, 0)
    return out.astype(WIDE)


def exchange(v, peers):
    parts = v.reshape(peers, v.shape[0] // peers, v.shape[1])
    return lax.all_to_all(parts, "edge", split_axis=0, concat_axis=0, tiled=True).reshape(v.shape)


def by_rows(g, count):
    parts = g.reshape(count, g.shape[0] // count, g.shape[1])
    return jnp.stack([parts[:, :, q : q + 128] for q in range(0, g.shape[1], 128)], axis=1)


def fold(g, count):
    parts = g.reshape(count, 4, g.shape[0] // count // 4, g.shape[1])
    return jnp.pad(parts, ((0, 0), (0, 0), (0, 0), (0, 128 - g.shape[1])))


def wide_rows(g, start, stop):
    return jnp.concatenate([g[q, start:stop] for q in range(g.shape[0])], axis=1)


def unfold(g, start, stop, width):
    return g[:, start:stop, 0:width].reshape(g.shape[0] * (stop - start), width)


def per_device(
    edge_embed, atom_embed, radial_basis, triplet_basis, quadruplet_basis,
    triplet_source_row, triplet_mask, quadruplet_source_row, quadruplet_mask,
    edge_target_atom, borrowed_edges,
    w_source_trip, w_rbf_trip, w_down_trip, w_source_quad, w_rbf_quad, w_down_quad,
    triplet_bilinear_weight, w_up_trip, w_bilinear_quad, w_up_quad, w_skip,
    w_res_first, w_res_second, w_rbf_atom, w_atom, w_concat, w_rbf_out, w_out,
    edge_cotangent, atom_cotangent, output_cotangent,
):
    edges, wide = edge_embed.shape
    atoms, aw = atom_embed.shape
    rbf = radial_basis.shape[1]
    peers = lax.axis_size("edge")
    cap = borrowed_edges.shape[2]
    steps = edges // TILE
    n3, n4 = w_down_trip.shape[1], w_down_quad.shape[1]
    nb = n3 + n4
    k3, k4 = triplet_mask.shape[1], quadruplet_mask.shape[1]
    f3, f4 = triplet_bilinear_weight.shape[0], w_bilinear_quad.shape[0]
    q3, q4 = triplet_basis.shape[1], quadruplet_basis.shape[1]
    ghosts = peers * cap
    ghosts_up = -(-ghosts // TILE) * TILE
    slabs = (edges + ghosts_up) // TILE

    wanted = borrowed_edges[0] - (jnp.arange(peers, dtype=jnp.int32) * edges)[:, None]
    asked = lax.all_to_all(wanted, "edge", split_axis=0, concat_axis=0, tiled=True).reshape(1, ghosts)

    i3 = jnp.where(triplet_mask > 0, triplet_source_row, -1).T
    i4 = jnp.where(quadruplet_mask > 0, quadruplet_source_row, -1).T
    trow = edge_target_atom
    sources = (w_source_trip, w_rbf_trip, w_down_trip, w_source_quad, w_rbf_quad, w_down_quad)
    turned = [pltpu.VMEM((n3, wide), LOW), pltpu.VMEM((n4, wide), LOW)]

    table, down, sent = call(
        source_body, "source_rows", steps, 10, (edge_embed, radial_basis, asked) + sources,
        [rows(wide), rows(rbf), whole(asked)] + [whole(w) for w in sources],
        [((nb, edges), LOW), ((nb, edges), WIDE), ((ghosts, LANES), LOW)],
        [cols(nb), cols(nb), fixed(ghosts, LANES)],
        turned + [pltpu.VMEM((LANES, ghosts), WIDE)],
    )
    ghost = exchange(sent, peers)

    s3, s4, p3, p4 = call(
        gather_body, "gather_sums", steps, 38,
        (table, ghost, i3, i4, triplet_basis, quadruplet_basis, triplet_bilinear_weight, w_bilinear_quad),
        [whole(table), whole(ghost), cols(k3), cols(k4), rows(q3), rows(q4),
         whole(triplet_bilinear_weight), whole(w_bilinear_quad)],
        [((f3, edges), LOW), ((f4, edges), LOW), ((n3, edges), WIDE), ((n4, edges), WIDE)],
        [cols(f3), cols(f4), cols(n3), cols(n4)],
        [
            pltpu.VMEM((slabs * n3, TILE), LOW), pltpu.VMEM((slabs * n4, TILE), LOW),
            pltpu.VMEM((k3, n3, TILE), WIDE), pltpu.VMEM((k4, n4, TILE), WIDE),
            pltpu.VMEM((q3, TILE), WIDE), pltpu.VMEM((q4, TILE), WIDE),
            pltpu.VMEM((n3, f3), LOW), pltpu.VMEM((n4, f4), LOW),
        ],
    )

    act = ((edges, wide), LOW)
    ups = (w_up_trip, w_up_quad, w_skip, w_res_first, w_res_second, w_rbf_atom)
    merged, mixlow, reshid, dsk, du3, du4, dr1, dr2, gath, anew, aslope = call(
        mix_body, "edge_update", steps, 19,
        (edge_embed, radial_basis, p3, p4, trow) + ups + (w_atom, atom_embed),
        [rows(wide), rows(rbf), cols(n3), cols(n4), cols(1)] + [whole(w) for w in ups + (w_atom, atom_embed)],
        [((edges, wide), WIDE), act, act, act, act, act, act, act,
         ((atoms, wide), LOW), ((atoms, aw), LOW), ((atoms, aw), WIDE)],
        [rows(wide)] * 8 + [fixed(atoms, wide), fixed(atoms, aw), fixed(atoms, aw)],
        [pltpu.VMEM((atoms, wide), WIDE)],
    )

    outs = (w_concat, w_rbf_out, w_out, output_cotangent, atom_cotangent, aslope, gath, w_atom)
    enew, gmer, gwc, gro, goa, aout, gatom, gw2 = call(
        out_body, "output_block", steps, 16,
        (merged, radial_basis, trow, anew, edge_cotangent) + outs,
        [rows(wide), rows(rbf), cols(1), whole(anew), rows(wide)] + [whole(w) for w in outs],
        [act, ((edges, wide), WIDE), (w_concat.shape, LOW), (w_rbf_out.shape, LOW),
         ((wide, 2 * aw), LOW), ((atoms, aw), LOW), ((atoms, aw), LOW), ((2 * atoms, wide), LOW)],
        [rows(wide), rows(wide), whole(w_concat), whole(w_rbf_out), fixed(wide, 2 * aw),
         fixed(atoms, aw), fixed(atoms, aw), fixed(2 * atoms, wide)],
        [
            pltpu.VMEM((atoms, wide), WIDE), pltpu.VMEM((atoms, wide), WIDE),
            pltpu.VMEM((2 * atoms, 2 * wide), LOW),
            pltpu.VMEM((w_concat.shape[0] - aw, wide), WIDE), pltpu.VMEM(w_rbf_out.shape, WIDE),
        ],
    )
    first = jnp.concatenate([by_rows(gwc, peers), by_rows(goa, peers), by_rows(gro, peers)], axis=2)
    first = core_sum(first)

    gpart, lb3, lb4, gsk, gr1, gr2, gra, gup, gbil = call(
        back_body, "edge_update_back", steps, 22,
        (edge_embed, radial_basis, trow, s3, s4, merged, gmer, gw2, p3, p4, mixlow, reshid, dsk,
         du3, du4, dr1, dr2) + ups,
        [rows(wide), rows(rbf), cols(1), cols(f3), cols(f4), rows(wide), rows(wide), whole(gw2),
         cols(n3), cols(n4)] + [rows(wide)] * 7 + [whole(w) for w in ups],
        [((edges, wide), WIDE), ((n3, edges), LOW), ((n4, edges), LOW), (w_skip.shape, LOW),
         (w_skip.shape, LOW), (w_skip.shape, LOW), (w_rbf_atom.shape, LOW), ((wide, nb), LOW), ((f3, nb), LOW)],
        [rows(wide), cols(n3), cols(n4), whole(w_skip), whole(w_skip), whole(w_skip),
         whole(w_rbf_atom), fixed(wide, nb), fixed(f3, nb)],
        [pltpu.VMEM(w_skip.shape, WIDE)] * 3
        + [pltpu.VMEM(w_rbf_atom.shape, WIDE), pltpu.VMEM((nb, wide), WIDE), pltpu.VMEM((f3, nb), WIDE)],
    )
    second = jnp.concatenate(
        [by_rows(gsk, peers), by_rows(gr1, peers), by_rows(gr2, peers), by_rows(gra, peers),
         fold(gup, peers), fold(gbil, peers)],
        axis=2,
    )
    lb4, first = lax.optimization_barrier((lb4, first))
    first = group_sum(first)
    second = core_sum(second)

    def scatter(lb, idx, basis, w, beside, name, micros):
        n, slots, q, f = w.shape[1], idx.shape[0], basis.shape[1], w.shape[0]
        ins = (lb, idx, basis, w) + ((beside,) if beside is not None else ())
        far = (n, ghosts_up) if beside is None else (ghosts, LANES)
        far_type = WIDE if beside is None else LOW
        body = functools.partial(scatter_body, edges=edges, other=beside is not None)
        return call(
            body, name, steps, micros, ins,
            [cols(n), cols(slots), rows(q), whole(w)] + [whole(x) for x in ins[4:]],
            [((n, edges), WIDE), (far, far_type)],
            [fixed(n, edges), fixed(*far)],
            [
                pltpu.VMEM((slabs * n, TILE), WIDE), pltpu.VMEM((q, TILE), WIDE), pltpu.VMEM((f, TILE), WIDE),
                pltpu.VMEM((slabs * n, slots * TILE), LOW), pltpu.VMEM((TILE, slots * TILE), LOW),
            ],
        )

    grad4, far4 = scatter(lb4, i4, quadruplet_basis, w_bilinear_quad, None, "scatter_quad", 11)
    lb3, far4, first, second = lax.optimization_barrier((lb3, far4, first, second))
    first = share_sum(first)
    second = group_sum(second)
    grad3, far = scatter(lb3, i3, triplet_basis, triplet_bilinear_weight, far4, "scatter_trip", 20)
    ret = exchange(far, peers)
    ret, first, second = lax.optimization_barrier((ret, first, second))
    first = group_gather(first)
    second = share_sum(second)

    gedge, gs3, gs4, gr3, gr4, gdn = call(
        source_back_body, "source_rows_back", steps, 19,
        (edge_embed, radial_basis, gpart, grad3, grad4, down, ret, asked) + sources,
        [rows(wide), rows(rbf), rows(wide), cols(n3), cols(n4), cols(nb), whole(ret), whole(asked)]
        + [whole(w) for w in sources],
        [act, (w_skip.shape, LOW), (w_skip.shape, LOW), (w_rbf_trip.shape, LOW),
         (w_rbf_trip.shape, LOW), ((wide, nb), LOW)],
        [rows(wide), whole(w_skip), whole(w_skip), whole(w_rbf_trip), whole(w_rbf_trip), fixed(wide, nb)],
        [pltpu.VMEM(w_skip.shape, WIDE)] * 2
        + [pltpu.VMEM(w_rbf_trip.shape, WIDE)] * 2
        + [pltpu.VMEM((nb, wide), WIDE)] + turned + [pltpu.VMEM((LANES, ghosts), LOW)],
    )
    third = jnp.concatenate(
        [by_rows(gs3, peers), by_rows(gs4, peers), by_rows(gr3, peers), by_rows(gr4, peers), fold(gdn, peers)],
        axis=2,
    )
    third, first, second = lax.optimization_barrier((third, first, second))
    third = core_sum(third)
    second = group_gather(second)
    third = group_gather(share_sum(group_sum(third)))

    a = wide // peers
    b = rbf // peers
    c = w_concat.shape[0] // peers
    r_concat = wide_rows(first, 0, c)
    r_oa = wide_rows(first, c, c + a)
    r_out = wide_rows(first, c + a, c + a + b)
    r_sk = wide_rows(second, 0, a)
    r_r1 = wide_rows(second, a, 2 * a)
    r_r2 = wide_rows(second, 2 * a, 3 * a)
    at = 3 * a + b
    r_ra = wide_rows(second, 3 * a, at)
    r_up = unfold(second, at, at + a // 4, nb).T
    r_bil = unfold(second, at + a // 4, second.shape[1], nb)
    r_s3 = wide_rows(third, 0, a)
    r_s4 = wide_rows(third, a, 2 * a)
    r_r3 = wide_rows(third, 2 * a, 2 * a + b)
    r_r4 = wide_rows(third, 2 * a + b, 2 * a + 2 * b)
    r_dn = unfold(third, 2 * a + 2 * b, third.shape[1], nb)
    return (
        enew, anew, aout, gedge, gatom,
        r_s3, r_r3, r_dn[:, 0:n3], r_s4, r_r4, r_dn[:, n3:],
        r_bil[:, 0:n3], r_up[0:n3], r_bil[:, n3:], r_up[n3:],
        r_sk, r_r1, r_r2, r_ra, r_oa[:, aw:], r_concat, r_out, r_oa[:, 0:aw],
    )


def solution(mesh):
    both = P(("grp", "edge"), None)
    placed = (both,) * 10 + (P(("grp", "edge"), None, None),) + (P(),) * 18 + (both,) * 3
    shares = [P("edge", None)] * 18
    shares[7] = P(None, "edge")
    shares[9] = P(None, "edge")
    return jax.shard_map(
        per_device, mesh=mesh, in_specs=placed, out_specs=(both,) * 5 + tuple(shares), check_vma=False
    )
```

time: 298 us -> 274 us (0.919)
  waiting for transfers between devices: 53.9 us -> 29.1 us
  local copies, waits for them, and re-layouts: 38.9 us -> 18.4 us
  starting transfers between devices: 30.2 us -> 48.9 us
  Pallas kernels: 155 us -> 163 us
  other arithmetic: 15.6 us -> 12 us
    ppermute x15 -> x30, waiting for transfers between devices: 49.5 us -> 19.5 us  [swap(): return lax.ppermute(v, axis, [(j, j ^ mask) for j in range(count)])]
    ppermute x15 -> x30, starting transfers between devices: 14.8 us -> 34.8 us  [swap(): return lax.ppermute(v, axis, [(j, j ^ mask) for j in range(count)])]
    pallas_call x7 -> x8, Pallas kernels: 155 us -> 163 us  [call(): pl.pallas_call(body, name=name, out_shape=[jax.ShapeDtypeStruct(s, t) for...]
    slice x13 -> x4, local copies, waits for them, and re-layouts: 8.68 us -> 0.64 us  [the longest x1 0.62 us: per_device(): r_up[0:n3]]
    unnamed x57 -> x42, local copies, waits for them, and re-layouts: 15.4 us -> 8.67 us
    another operation x1 -> x13, local copies, waits for them, and re-layouts: 0.71 us -> 5.37 us  [the longest x11 5.32 us: by_rows(): jnp.stack([parts[:, :, q:q + 128] for q in range(0, g.shape[1], 128)], ax...]
    all_to_all x4 -> x0, other arithmetic: 4.64 us -> none  [the longest x2 3.72 us: per_device(): back = lax.all_to_all(back, 'edge', split_axis=0, concat_axis=0, tiled=True)]
    concatenate x4 -> x7, other arithmetic: 0.07 us -> 4.71 us  [wide_rows(): jnp.concatenate([g[q, start:stop] for q in range(g.shape[0])], axis=1)]
  transfers between devices with their start and end apart: 18 -> 33, of which waited for: 10 -> 13; matrix products, arithmetic and copies ran while one was open for 13% -> 7% of each run, Pallas kernels for 27% -> 20%
where the time goes in v2:
time: 274 us; the launch traced here: 273 us
  Pallas kernels  163 us (59%)
  starting transfers between devices  48.9 us (18%)
  waiting for transfers between devices  29.1 us (11%)
  local copies, waits for them, and re-layouts  18.4 us (7%)
  other arithmetic  12 us (4%)
    pallas_call x8, Pallas kernels, call(): pl.pallas_call(body, name=name, out_shape=[jax.ShapeDtypeStruct(s, t) for...  163 us
    ppermute x30, starting transfers between devices, swap(): return lax.ppermute(v, axis, [(j, j ^ mask) for j in range(count)])  34.8 us
    ppermute x30, waiting for transfers between devices, swap(): return lax.ppermute(v, axis, [(j, j ^ mask) for j in range(count)])  19.5 us
    all_to_all x2, waiting for transfers between devices, exchange(): lax.all_to_all(parts, 'edge', split_axis=0, concat_axis=0, tiled=True)  8.83 us
    unnamed x42, local copies, waits for them, and re-layouts  8.67 us
    all_to_all x2, starting transfers between devices, exchange(): lax.all_to_all(parts, 'edge', split_axis=0, concat_axis=0, tiled=True)  7.7 us
    all_to_all x1, starting transfers between devices, per_device(): lax.all_to_all(wanted, 'edge', split_axis=0, concat_axis=0, tiled=True)  6.35 us
  transfers between devices with their start and end apart: 33, of which 13 were waited for; matrix products, arithmetic and copies ran while one was open for 7% of the time, Pallas kernels for 20%

profile of v2, /device:TPU:0, one launch (start us, length us, event | category | flops | bytes accessed | tf_op | source)
XLA Modules:
  0.0 273.1 jit_solution(15864817292685101069)
XLA Ops:
  0.7 1.4 bitcast_subtract_fusion
  2.0 6.4 %all-to-all-start = ((s32[8,1,16]{2,1,0:T(1,128)}), s32[8,1,16]{2,1,0:T(1,128)S(1)}, u32[]{:S(2)}, u32[]{:S(2)}) async-start(s32[8,1,16]{2,1,0:T(1,128)} %bitcast.1), calls=%async_computation | async-start | bytes 8192 | tf_op jit(solution)/shard_map/all_to_all | solution.py:573
  8.4 1.6 select_bitcast_fusion.i3.idx
  10.0 1.6 copy.116.wd3
  11.6 1.5 copy.117.wd4
  13.1 0.8 all-to-all-done
  15.7 10.6 %source_rows.1 = (bf16[96,2048]{1,0:T(8,128)(2,1)}, f32[96,2048]{1,0:T(8,128)}, bf16[128,128]{1,0:T(8,128)(2,1)}) custom-call(bf16[2048,512]{1,0:T(8,128)(2,1)} %edge.7, bf16[2048,128]{1,0:T(8,128)(2,1)} %radial.9, s32[1,128]{1,0:T(1,128)} %reshape.201.asked, bf16[512,512]{1,0:T(8,128)(2,1)} %ws3.3, bf16[128,512]{1,0:T(8,128)(2,1)} %wr3.3, ...), custom_call_target="tpu_custom_call" | custom-call | flops 11000000512 | bytes 4194304 | tf_op jit(solution)/shard_map/source_rows/pallas_call | solution.py:64
  26.3 4.4 %all-to-all-start.1 = ((bf16[8,16,128]{2,1,0:T(8,128)(2,1)}), bf16[8,16,128]{2,1,0:T(8,128)(2,1)S(1)}, u32[]{:S(2)}, u32[]{:S(2)}) async-start(bf16[8,16,128]{2,1,0:T(8,128)(2,1)} %bitcast.376), calls=%async_computation.1 | async-start | bytes 65536 | tf_op jit(solution)/shard_map/all_to_all | solution.py:527
  31.3 0.8 copy.118.w3.w
  32.2 0.8 copy.119.w4.w
  33.0 3.4 %all-to-all-done.1 = bf16[8,16,128]{2,1,0:T(8,128)(2,1)S(1)} async-done(((bf16[8,16,128]{2,1,0:T(8,128)(2,1)}), bf16[8,16,128]{2,1,0:T(8,128)(2,1)S(1)}, u32[]{:S(2)}, u32[]{:S(2)}) %all-to-all-start.1) | async-done | bytes 32800 | tf_op jit(solution)/shard_map/all_to_all | solution.py:527
  37.0 39.1 %gather_sums.1 = (bf16[1024,2048]{1,0:T(8,128)(2,1)}, bf16[1024,2048]{1,0:T(8,128)(2,1)}, f32[64,2048]{1,0:T(8,128)}, f32[32,2048]{1,0:T(8,128)}) custom-call(bf16[96,2048]{1,0:T(8,128)(2,1)} %get-tuple-element.80.tab, bf16[128,128]{1,0:T(8,128)(2,1)} %bitcast.375, s32[16,2048]{1,0:T(8,128)} %select_bitcast_fusion.i3.idx, ...), custom_call_target="tpu_custom_call" | custom-call | flops 41799999488 | bytes 4194304 | tf_op jit(solution)/shard_map/gather_sums/pallas_call | solution.py:64
  76.2 18.9 %edge_update.1 = (f32[2048,512]{1,0:T(8,128)}, bf16[2048,512]{1,0:T(8,128)(2,1)}, bf16[2048,512]{1,0:T(8,128)(2,1)}, bf16[2048,512]{1,0:T(8,128)(2,1)}, bf16[204...) custom-call(bf16[2048,512]{1,0:T(8,128)(2,1)} %edge.7, ...), custom_call_target="tpu_custom_call" | custom-call | flops 20899999744 | bytes 4194304 | tf_op jit(solution)/shard_map/edge_update/pallas_call | solution.py:64
  95.1 15.8 %output_block.1 = (bf16[2048,512]{1,0:T(8,128)(2,1)}, f32[2048,512]{1,0:T(8,128)}, bf16[768,512]{1,0:T(8,128)(2,1)}, bf16[128,512]{1,0:T(8,128)(2,1)}, bf16[512,...) custom-call(f32[2048,512]{1,0:T(8,128)} %get-tuple-element.84.merged, ...), custom_call_target="tpu_custom_call" | custom-call | flops 17600000000 | bytes 4194304 | tf_op jit(solution)/shard_map/output_block/pallas_call | solution.py:64
  110.9 24.4 %edge_update_back.1 = (f32[2048,512]{1,0:T(8,128)}, bf16[64,2048]{1,0:T(8,128)(2,1)}, bf16[32,2048]{1,0:T(8,128)(2,1)}, bf16[512,512]{1,0:T(8,128)(2,1)}, bf16[5...) custom-call(bf16[2048,512]{1,0:T(8,128)(2,1)} %edge.7, ...), custom_call_target="tpu_custom_call" | custom-call | flops 24199999488 | bytes 4194304 | tf_op jit(solution)/shard_map/edge_update_back/pallas_call | solution.py:64
  135.3 1.2 slice_bitcast_fusion.23
  136.5 1.2 slice_bitcast_fusion.19
  140.1 1.1 dynamic-slice_bitcast_fusion
  141.5 1.6 collective-permute-start.1
  143.0 1.5 collective-permute-start.2
  145.0 13.7 %scatter_quad.1 = (f32[32,2048]{1,0:T(8,128)}, f32[32,256]{1,0:T(8,128)}) custom-call(bf16[32,2048]{1,0:T(8,128)(2,1)} %get-tuple-element.107.lb, s32[8,2048]{1,0:T(8,128)} %select_bitcast_fusion.1.i4.idx, bf16[2048,256]{1,0:T(8,128)(2,1)} %basis.2, bf16[1024,32]{1,0:T(8,128)(2,1)} %copy.119.w4.w), custom_call_target="tpu_custom_call" | custom-call | flops 12099999744 | bytes 4194304 | tf_op jit(solution)/shard_map/scatter_quad/pallas_call | solution.py:64
  158.9 1.5 fusion
  161.2 2.5 collective-permute-start.10
  165.2 3.3 %collective-permute-start.7 = (bf16[1,176,128]{2,1,0:T(8,128)(2,1)S(1)}, bf16[1,176,128]{2,1,0:T(8,128)(2,1)S(1)}, u32[]{:S(2)}, u32[]{:S(2)}) collective-permute-start(bf16[1,176,128]{2,1,0:T(8,128)(2,1)S(1)} %get-tuple-element.227), channel_id=1, source_target_pairs={{0,6},{1,7},{2,4},{3,5},{4,2},{5,3},{6,0},{7,1},{8,14},{9,15},{10,... | collective-permute-start | bytes 135176 | tf_op jit(solution)/shard_map/ppermute | solution.py:477
  168.5 20.6 %scatter_trip.1 = (f32[64,2048]{1,0:T(8,128)}, bf16[128,128]{1,0:T(8,128)(2,1)}) custom-call(bf16[64,2048]{1,0:T(8,128)(2,1)} %get-tuple-element.116.lb, s32[16,2048]{1,0:T(8,128)} %select_bitcast_fusion.i3.idx, bf16[2048,256]{1,0:T(8,128)(2,1)} %basis.3, bf16[1024,64]{1,0:T(8,128)(2,1)} %copy.118.w3.w, f32[32,256]{1,0:T(8,128)} %get-tuple-element.117.rest_0_), custom_call_target="tpu_custom_call" | custom-call | flops 22000001024 | bytes 4194304 | tf_op jit(solution)/shard_map/scatter_trip/pallas_call | solution.py:64
  189.1 3.3 %all-to-all-start.2 = ((bf16[8,16,128]{2,1,0:T(8,128)(2,1)}), bf16[8,16,128]{2,1,0:T(8,128)(2,1)S(1)}, u32[]{:S(2)}, u32[]{:S(2)}) async-start(bf16[8,16,128]{2,1,0:T(8,128)(2,1)} %bitcast.378), calls=%async_computation.2 | async-start | bytes 65536 | tf_op jit(solution)/shard_map/all_to_all | solution.py:527
  192.7 5.4 %all-to-all-done.2 = bf16[8,16,128]{2,1,0:T(8,128)(2,1)S(1)} async-done(((bf16[8,16,128]{2,1,0:T(8,128)(2,1)}), bf16[8,16,128]{2,1,0:T(8,128)(2,1)S(1)}, u32[]{:S(2)}, u32[]{:S(2)}) %all-to-all-start.2) | async-done | bytes 32800 | tf_op jit(solution)/shard_map/all_to_all | solution.py:527
  198.1 1.5 collective-permute-start.11
  199.6 1.5 collective-permute-start.12
  202.9 20.2 %source_rows_back.1 = (bf16[2048,512]{1,0:T(8,128)(2,1)}, bf16[512,512]{1,0:T(8,128)(2,1)}, bf16[512,512]{1,0:T(8,128)(2,1)}, bf16[128,512]{1,0:T(8,128)(2,1)}, ...) custom-call(bf16[2048,512]{1,0:T(8,128)(2,1)} %edge.7, bf16[2048,128]{1,0:T(8,128)(2,1)} %radial.9, ...), custom_call_target="tpu_custom_call" | custom-call | flops 20899999744 | bytes 4194304 | tf_op jit(solution)/shard_map/source_rows_back/pallas_call | solution.py:64
  223.1 1.2 slice_bitcast_fusion.11
  224.3 1.2 slice_bitcast_fusion.7
  225.8 3.4 %collective-permute-start.16 = (bf16[1,256,128]{2,1,0:T(8,128)(2,1)S(1)}, bf16[1,256,128]{2,1,0:T(8,128)(2,1)S(1)}, u32[]{:S(2)}, u32[]{:S(2)}) collective-permute-start(bf16[1,256,128]{2,1,0:T(8,128)(2,1)S(1)} %get-tuple-element.221), channel_id=1, source_target_pairs={{0,6},{1,7},{2,4},{3,5},{4,2},{5,3},{6,0},{7,1},{8,14},{9,15},{10,... | collective-permute-start | bytes 196616 | tf_op jit(solution)/shard_map/ppermute | solution.py:477
  229.3 2.6 collective-permute-done.16
  232.1 1.6 collective-permute-start.27
  233.6 1.5 collective-permute-start.28
  237.9 2.4 collective-permute-done.29
  240.4 0.7 pad_maximum_fusion.3
  242.5 2.4 collective-permute-start.20
  244.9 2.8 %collective-permute-done.18 = bf16[4,176,128]{2,1,0:T(8,128)(2,1)S(1)} collective-permute-done((bf16[4,176,128]{2,1,0:T(8,128)(2,1)S(1)}, bf16[4,176,128]{2,1,0:T(8,128)(2,1)S(1)}, u32[]{:S(2)}, u32[]{:S(2)}) %collective-permute-start.18) | collective-permute-done | bytes 180256 | tf_op jit(solution)/shard_map/ppermute | solution.py:477
  247.8 3.1 %collective-permute-done.19 = bf16[4,176,128]{2,1,0:T(8,128)(2,1)S(1)} collective-permute-done((bf16[4,176,128]{2,1,0:T(8,128)(2,1)S(1)}, bf16[4,176,128]{2,1,0:T(8,128)(2,1)S(1)}, u32[]{:S(2)}, u32[]{:S(2)}) %collective-permute-start.19) | collective-permute-done | bytes 180256 | tf_op jit(solution)/shard_map/ppermute | solution.py:477
  251.1 3.8 %collective-permute-start.22 = (bf16[1,176,128]{2,1,0:T(8,128)(2,1)S(1)}, bf16[1,176,128]{2,1,0:T(8,128)(2,1)S(1)}, u32[]{:S(2)}, u32[]{:S(2)}) collective-permute-start(bf16[1,176,128]{2,1,0:T(8,128)(2,1)S(1)} %get-tuple-element.225), channel_id=1, source_target_pairs={{0,4},{1,5},{2,6},{3,7},{4,0},{5,1},{6,2},{7,3},{8,12},{9,13},{10,... | collective-permute-start | bytes 135176 | tf_op jit(solution)/shard_map/ppermute | solution.py:477
  256.2 1.7 collective-permute-done.22
  257.8 3.0 %collective-permute-done.23 = bf16[1,176,128]{2,1,0:T(8,128)(2,1)S(1)} collective-permute-done((bf16[1,176,128]{2,1,0:T(8,128)(2,1)S(1)}, bf16[1,176,128]{2,1,0:T(8,128)(2,1)S(1)}, u32[]{:S(2)}, u32[]{:S(2)}) %collective-permute-start.23) | collective-permute-done | bytes 45088 | tf_op jit(solution)/shard_map/ppermute | solution.py:477
  260.9 1.6 collective-permute-start.24
  265.9 1.9 collective-permute-start.26
  267.9 2.0 collective-permute-done.25
  269.9 1.0 collective-permute-done.26
  (154 shorter events, 22.1 us)
Async XLA Ops:
  2.0 11.9 %all-to-all-start = ((s32[8,1,16]{2,1,0:T(1,128)}), s32[8,1,16]{2,1,0:T(1,128)S(1)}, u32[]{:S(2)}, u32[]{:S(2)}) async-start(s32[8,1,16]{2,1,0:T(1,128)} %bitcast.1), calls=%async_computation | async-start | bytes 8192 | tf_op jit(solution)/shard_map/all_to_all | solution.py:573
  15.7 15.0 %copy-start.12 = (s32[2048,8]{0,1:T(8,128)S(1)}, s32[2048,8]{0,1:T(8,128)}, u32[]{:S(2)}) copy-start(s32[2048,8]{0,1:T(8,128)} %param.39) | copy-start | bytes 196612
  15.7 15.0 %copy-start.13 = (s32[2048,8]{0,1:T(8,128)S(1)}, s32[2048,8]{0,1:T(8,128)}, u32[]{:S(2)}) copy-start(s32[2048,8]{0,1:T(8,128)} %param.40) | copy-start | bytes 196612
  15.7 15.7 %copy-start.4 = (bf16[1024,64]{0,1:T(8,128)(2,1)S(1)}, bf16[1024,64]{0,1:T(8,128)(2,1)}, u32[]{:S(2)}) copy-start(bf16[1024,64]{0,1:T(8,128)(2,1)} %param.49) | copy-start | bytes 393220
  15.7 16.5 %copy-start.14 = (bf16[1024,32]{0,1:T(8,128)(2,1)S(1)}, bf16[1024,32]{0,1:T(8,128)(2,1)}, u32[]{:S(2)}) copy-start(bf16[1024,32]{0,1:T(8,128)(2,1)} %param.51) | copy-start | bytes 196612
  26.3 10.1 %all-to-all-start.1 = ((bf16[8,16,128]{2,1,0:T(8,128)(2,1)}), bf16[8,16,128]{2,1,0:T(8,128)(2,1)S(1)}, u32[]{:S(2)}, u32[]{:S(2)}) async-start(bf16[8,16,128]{2,1,0:T(8,128)(2,1)} %bitcast.376), calls=%async_computation.1 | async-start | bytes 65536 | tf_op jit(solution)/shard_map/all_to_all | solution.py:527
  135.3 2.5 copy-start.2
  135.3 2.6 copy-start
  136.5 1.5 copy-start.1
  137.7 0.9 copy-start.7
  139.0 0.9 copy-start.5
  139.0 1.0 copy-start.3
  139.0 2.3 collective-permute-start
  141.2 17.7 %collective-permute-start.4 = (bf16[4,4,256,128]{3,2,1,0:T(8,128)(2,1)}, bf16[4,4,256,128]{3,2,1,0:T(8,128)(2,1)}, u32[]{:S(2)}, u32[]{:S(2)}) collective-permute-start(bf16[4,4,256,128]{3,2,1,0:T(8,128)(2,1)} %dynamic-slice_bitcast_fusion), channel_id=1, source_target_pairs={{0,1},{1,0},{2,3},{3,2},{4,5},{5,4},{6,7},{7,6},{8,9},{9,8},{10,11... | collective-permute-start | bytes 3145736 | tf_op jit(solution)/shard_map/ppermute | solution.py:477
  141.5 17.3 %collective-permute-start.1 = (bf16[4,176,128]{2,1,0:T(8,128)(2,1)S(1)}, bf16[4,176,128]{2,1,0:T(8,128)(2,1)S(1)}, u32[]{:S(2)}, u32[]{:S(2)}) collective-permute-start(bf16[4,176,128]{2,1,0:T(8,128)(2,1)S(1)} %get-tuple-element.149), channel_id=1, source_target_pairs={{0,8},{8,0},{16,24},{24,16},{1,9},{9,1},{17,25},{25,17},{2,10},{10... | collective-permute-start | bytes 540680 | tf_op jit(solution)/shard_map/ppermute | solution.py:477
  143.0 15.7 %collective-permute-start.2 = (bf16[4,176,128]{2,1,0:T(8,128)(2,1)S(1)}, bf16[4,176,128]{2,1,0:T(8,128)(2,1)S(1)}, u32[]{:S(2)}, u32[]{:S(2)}) collective-permute-start(bf16[4,176,128]{2,1,0:T(8,128)(2,1)S(1)} %get-tuple-element.151), channel_id=1, source_target_pairs={{0,16},{8,24},{16,0},{24,8},{1,17},{9,25},{17,1},{25,9},{2,18},{10... | collective-permute-start | bytes 540680 | tf_op jit(solution)/shard_map/ppermute | solution.py:477
  144.6 14.2 %collective-permute-start.3 = (bf16[4,176,128]{2,1,0:T(8,128)(2,1)S(1)}, bf16[4,176,128]{2,1,0:T(8,128)(2,1)S(1)}, u32[]{:S(2)}, u32[]{:S(2)}) collective-permute-start(bf16[4,176,128]{2,1,0:T(8,128)(2,1)S(1)} %get-tuple-element.150), channel_id=1, source_target_pairs={{0,24},{8,16},{16,8},{24,0},{1,25},{9,17},{17,9},{25,1},{2,26},{10... | collective-permute-start | bytes 540680 | tf_op jit(solution)/shard_map/ppermute | solution.py:477
  160.4 4.8 %collective-permute-start.5 = (bf16[1,176,128]{2,1,0:T(8,128)(2,1)S(1)}, bf16[1,176,128]{2,1,0:T(8,128)(2,1)S(1)}, u32[]{:S(2)}, u32[]{:S(2)}) collective-permute-start(bf16[1,176,128]{2,1,0:T(8,128)(2,1)S(1)} %get-tuple-element.226), channel_id=1, source_target_pairs={{0,2},{1,3},{2,0},{3,1},{4,6},{5,7},{6,4},{7,5},{8,10},{9,11},{10,... | collective-permute-start | bytes 135176 | tf_op jit(solution)/shard_map/ppermute | solution.py:477
  161.2 31.3 %collective-permute-start.10 = (bf16[4,256,128]{2,1,0:T(8,128)(2,1)S(1)}, bf16[4,256,128]{2,1,0:T(8,128)(2,1)S(1)}, u32[]{:S(2)}, u32[]{:S(2)}) collective-permute-start(bf16[4,256,128]{2,1,0:T(8,128)(2,1)S(1)} %get-tuple-element.140), channel_id=1, source_target_pairs={{0,24},{8,16},{16,8},{24,0},{1,25},{9,17},{17,9},{25,1},{2,26},{10... | collective-permute-start | bytes 786440 | tf_op jit(solution)/shard_map/ppermute | solution.py:477
  163.7 28.8 %collective-permute-start.8 = (bf16[4,256,128]{2,1,0:T(8,128)(2,1)S(1)}, bf16[4,256,128]{2,1,0:T(8,128)(2,1)S(1)}, u32[]{:S(2)}, u32[]{:S(2)}) collective-permute-start(bf16[4,256,128]{2,1,0:T(8,128)(2,1)S(1)} %get-tuple-element.139), channel_id=1, source_target_pairs={{0,8},{8,0},{16,24},{24,16},{1,9},{9,1},{17,25},{25,17},{2,10},{10... | collective-permute-start | bytes 786440 | tf_op jit(solution)/shard_map/ppermute | solution.py:477
  164.2 28.3 %collective-permute-start.9 = (bf16[4,256,128]{2,1,0:T(8,128)(2,1)S(1)}, bf16[4,256,128]{2,1,0:T(8,128)(2,1)S(1)}, u32[]{:S(2)}, u32[]{:S(2)}) collective-permute-start(bf16[4,256,128]{2,1,0:T(8,128)(2,1)S(1)} %get-tuple-element.141), channel_id=1, source_target_pairs={{0,16},{8,24},{16,0},{24,8},{1,17},{9,25},{17,1},{25,9},{2,18},{10... | collective-permute-start | bytes 786440 | tf_op jit(solution)/shard_map/ppermute | solution.py:477
  164.7 27.7 %collective-permute-start.6 = (bf16[1,176,128]{2,1,0:T(8,128)(2,1)S(1)}, bf16[1,176,128]{2,1,0:T(8,128)(2,1)S(1)}, u32[]{:S(2)}, u32[]{:S(2)}) collective-permute-start(bf16[1,176,128]{2,1,0:T(8,128)(2,1)S(1)} %get-tuple-element.228), channel_id=1, source_target_pairs={{0,4},{1,5},{2,6},{3,7},{4,0},{5,1},{6,2},{7,3},{8,12},{9,13},{10,... | collective-permute-start | bytes 135176 | tf_op jit(solution)/shard_map/ppermute | solution.py:477
  165.2 27.2 %collective-permute-start.7 = (bf16[1,176,128]{2,1,0:T(8,128)(2,1)S(1)}, bf16[1,176,128]{2,1,0:T(8,128)(2,1)S(1)}, u32[]{:S(2)}, u32[]{:S(2)}) collective-permute-start(bf16[1,176,128]{2,1,0:T(8,128)(2,1)S(1)} %get-tuple-element.227), channel_id=1, source_target_pairs={{0,6},{1,7},{2,4},{3,5},{4,2},{5,3},{6,0},{7,1},{8,14},{9,15},{10,... | collective-permute-start | bytes 135176 | tf_op jit(solution)/shard_map/ppermute | solution.py:477
  189.1 9.0 %all-to-all-start.2 = ((bf16[8,16,128]{2,1,0:T(8,128)(2,1)}), bf16[8,16,128]{2,1,0:T(8,128)(2,1)S(1)}, u32[]{:S(2)}, u32[]{:S(2)}) async-start(bf16[8,16,128]{2,1,0:T(8,128)(2,1)} %bitcast.378), calls=%async_computation.2 | async-start | bytes 65536 | tf_op jit(solution)/shard_map/all_to_all | solution.py:527
  198.1 4.7 %copy-start.16 = (bf16[8,16,128]{2,1,0:T(8,128)(2,1)}, bf16[8,16,128]{2,1,0:T(8,128)(2,1)S(1)}, u32[]{:S(2)}) copy-start(bf16[8,16,128]{2,1,0:T(8,128)(2,1)S(1)} %all-to-all-done.2) | copy-start | bytes 98308
  198.1 27.7 %collective-permute-start.11 = (bf16[176,128]{1,0:T(8,128)(2,1)S(1)}, bf16[176,128]{1,0:T(8,128)(2,1)S(1)}, u32[]{:S(2)}, u32[]{:S(2)}) collective-permute-start(bf16[176,128]{1,0:T(8,128)(2,1)S(1)} %fusion.13), channel_id=1, source_target_pairs={{0,8},{8,0},{16,24},{24,16},{1,9},{9,1},{17,25},{25,17},{2,10},{10... | collective-permute-start | bytes 135176 | tf_op jit(solution)/shard_map/ppermute | solution.py:477
  199.6 29.6 %collective-permute-start.12 = (bf16[176,128]{1,0:T(8,128)(2,1)S(1)}, bf16[176,128]{1,0:T(8,128)(2,1)S(1)}, u32[]{:S(2)}, u32[]{:S(2)}) collective-permute-start(bf16[176,128]{1,0:T(8,128)(2,1)S(1)} %fusion.13), channel_id=1, source_target_pairs={{0,16},{8,24},{16,0},{24,8},{1,17},{9,25},{17,1},{25,9},{2,18},{10... | collective-permute-start | bytes 135176 | tf_op jit(solution)/shard_map/ppermute | solution.py:477
  201.1 28.1 %collective-permute-start.13 = (bf16[176,128]{1,0:T(8,128)(2,1)S(1)}, bf16[176,128]{1,0:T(8,128)(2,1)S(1)}, u32[]{:S(2)}, u32[]{:S(2)}) collective-permute-start(bf16[176,128]{1,0:T(8,128)(2,1)S(1)} %fusion.13), channel_id=1, source_target_pairs={{0,24},{8,16},{16,8},{24,0},{1,25},{9,17},{17,9},{25,1},{2,26},{10... | collective-permute-start | bytes 135176 | tf_op jit(solution)/shard_map/ppermute | solution.py:477
  201.6 27.7 %collective-permute-start.14 = (bf16[1,256,128]{2,1,0:T(8,128)(2,1)S(1)}, bf16[1,256,128]{2,1,0:T(8,128)(2,1)S(1)}, u32[]{:S(2)}, u32[]{:S(2)}) collective-permute-start(bf16[1,256,128]{2,1,0:T(8,128)(2,1)S(1)} %get-tuple-element.220), channel_id=1, source_target_pairs={{0,2},{1,3},{2,0},{3,1},{4,6},{5,7},{6,4},{7,5},{8,10},{9,11},{10,... | collective-permute-start | bytes 196616 | tf_op jit(solution)/shard_map/ppermute | solution.py:477
  202.3 27.0 %collective-permute-start.15 = (bf16[1,256,128]{2,1,0:T(8,128)(2,1)S(1)}, bf16[1,256,128]{2,1,0:T(8,128)(2,1)S(1)}, u32[]{:S(2)}, u32[]{:S(2)}) collective-permute-start(bf16[1,256,128]{2,1,0:T(8,128)(2,1)S(1)} %get-tuple-element.222), channel_id=1, source_target_pairs={{0,4},{1,5},{2,6},{3,7},{4,0},{5,1},{6,2},{7,3},{8,12},{9,13},{10,... | collective-permute-start | bytes 196616 | tf_op jit(solution)/shard_map/ppermute | solution.py:477
  223.1 2.4 copy-start.10
  223.1 2.4 copy-start.9
  224.3 1.5 copy-start.8
  225.8 6.1 %collective-permute-start.16 = (bf16[1,256,128]{2,1,0:T(8,128)(2,1)S(1)}, bf16[1,256,128]{2,1,0:T(8,128)(2,1)S(1)}, u32[]{:S(2)}, u32[]{:S(2)}) collective-permute-start(bf16[1,256,128]{2,1,0:T(8,128)(2,1)S(1)} %get-tuple-element.221), channel_id=1, source_target_pairs={{0,6},{1,7},{2,4},{3,5},{4,2},{5,3},{6,0},{7,1},{8,14},{9,15},{10,... | collective-permute-start | bytes 196616 | tf_op jit(solution)/shard_map/ppermute | solution.py:477
  232.1 5.1 %collective-permute-start.27 = (bf16[256,128]{1,0:T(8,128)(2,1)S(1)}, bf16[256,128]{1,0:T(8,128)(2,1)S(1)}, u32[]{:S(2)}, u32[]{:S(2)}) collective-permute-start(bf16[256,128]{1,0:T(8,128)(2,1)S(1)} %fusion.12), channel_id=1, source_target_pairs={{0,8},{8,0},{16,24},{24,16},{1,9},{9,1},{17,25},{25,17},{2,10},{10... | collective-permute-start | bytes 196616 | tf_op jit(solution)/shard_map/ppermute | solution.py:477
  233.6 4.3 %collective-permute-start.28 = (bf16[256,128]{1,0:T(8,128)(2,1)S(1)}, bf16[256,128]{1,0:T(8,128)(2,1)S(1)}, u32[]{:S(2)}, u32[]{:S(2)}) collective-permute-start(bf16[256,128]{1,0:T(8,128)(2,1)S(1)} %fusion.12), channel_id=1, source_target_pairs={{0,16},{8,24},{16,0},{24,8},{1,17},{9,25},{17,1},{25,9},{2,18},{10... | collective-permute-start | bytes 196616 | tf_op jit(solution)/shard_map/ppermute | solution.py:477
  235.1 5.2 %collective-permute-start.29 = (bf16[256,128]{1,0:T(8,128)(2,1)S(1)}, bf16[256,128]{1,0:T(8,128)(2,1)S(1)}, u32[]{:S(2)}, u32[]{:S(2)}) collective-permute-start(bf16[256,128]{1,0:T(8,128)(2,1)S(1)} %fusion.12), channel_id=1, source_target_pairs={{0,24},{8,16},{16,8},{24,0},{1,25},{9,17},{17,9},{25,1},{2,26},{10... | collective-permute-start | bytes 196616 | tf_op jit(solution)/shard_map/ppermute | solution.py:477
  235.8 5.4 %collective-permute-start.17 = (bf16[4,4,176,128]{3,2,1,0:T(8,128)(2,1)S(1)}, bf16[4,4,176,128]{3,2,1,0:T(8,128)(2,1)S(1)}, u32[]{:S(2)}, u32[]{:S(2)}) collective-permute-start(bf16[4,4,176,128]{3,2,1,0:T(8,128)(2,1)S(1)} %dynamic-slice_bitcast_fusion.1), channel_id=1, source_target_pairs={{0,1},{1,0},{2,3},{3,2},{4,5},{5,4},{6,7},{7,6},{8,9},{9,8},{10,11... | collective-permute-start | bytes 2162696 | tf_op jit(solution)/shard_map/ppermute | solution.py:477
  241.4 6.4 %collective-permute-start.18 = (bf16[4,176,128]{2,1,0:T(8,128)(2,1)S(1)}, bf16[4,176,128]{2,1,0:T(8,128)(2,1)S(1)}, u32[]{:S(2)}, u32[]{:S(2)}) collective-permute-start(bf16[4,176,128]{2,1,0:T(8,128)(2,1)S(1)} %get-tuple-element.146), channel_id=1, source_target_pairs={{0,8},{8,0},{16,24},{24,16},{1,9},{9,1},{17,25},{25,17},{2,10},{10... | collective-permute-start | bytes 540680 | tf_op jit(solution)/shard_map/ppermute | solution.py:477
  242.0 8.9 %collective-permute-start.19 = (bf16[4,176,128]{2,1,0:T(8,128)(2,1)S(1)}, bf16[4,176,128]{2,1,0:T(8,128)(2,1)S(1)}, u32[]{:S(2)}, u32[]{:S(2)}) collective-permute-start(bf16[4,176,128]{2,1,0:T(8,128)(2,1)S(1)} %get-tuple-element.148), channel_id=1, source_target_pairs={{0,16},{8,24},{16,0},{24,8},{1,17},{9,25},{17,1},{25,9},{2,18},{10... | collective-permute-start | bytes 540680 | tf_op jit(solution)/shard_map/ppermute | solution.py:477
  242.5 8.4 %collective-permute-start.20 = (bf16[4,176,128]{2,1,0:T(8,128)(2,1)S(1)}, bf16[4,176,128]{2,1,0:T(8,128)(2,1)S(1)}, u32[]{:S(2)}, u32[]{:S(2)}) collective-permute-start(bf16[4,176,128]{2,1,0:T(8,128)(2,1)S(1)} %get-tuple-element.147), channel_id=1, source_target_pairs={{0,24},{8,16},{16,8},{24,0},{1,25},{9,17},{17,9},{25,1},{2,26},{10... | collective-permute-start | bytes 540680 | tf_op jit(solution)/shard_map/ppermute | solution.py:477
  251.0 5.1 %collective-permute-start.21 = (bf16[1,176,128]{2,1,0:T(8,128)(2,1)S(1)}, bf16[1,176,128]{2,1,0:T(8,128)(2,1)S(1)}, u32[]{:S(2)}, u32[]{:S(2)}) collective-permute-start(bf16[1,176,128]{2,1,0:T(8,128)(2,1)S(1)} %get-tuple-element.223), channel_id=1, source_target_pairs={{0,2},{1,3},{2,0},{3,1},{4,6},{5,7},{6,4},{7,5},{8,10},{9,11},{10,... | collective-permute-start | bytes 135176 | tf_op jit(solution)/shard_map/ppermute | solution.py:477
  251.1 6.7 %collective-permute-start.22 = (bf16[1,176,128]{2,1,0:T(8,128)(2,1)S(1)}, bf16[1,176,128]{2,1,0:T(8,128)(2,1)S(1)}, u32[]{:S(2)}, u32[]{:S(2)}) collective-permute-start(bf16[1,176,128]{2,1,0:T(8,128)(2,1)S(1)} %get-tuple-element.225), channel_id=1, source_target_pairs={{0,4},{1,5},{2,6},{3,7},{4,0},{5,1},{6,2},{7,3},{8,12},{9,13},{10,... | collective-permute-start | bytes 135176 | tf_op jit(solution)/shard_map/ppermute | solution.py:477
  255.0 5.8 %collective-permute-start.23 = (bf16[1,176,128]{2,1,0:T(8,128)(2,1)S(1)}, bf16[1,176,128]{2,1,0:T(8,128)(2,1)S(1)}, u32[]{:S(2)}, u32[]{:S(2)}) collective-permute-start(bf16[1,176,128]{2,1,0:T(8,128)(2,1)S(1)} %get-tuple-element.224), channel_id=1, source_target_pairs={{0,6},{1,7},{2,4},{3,5},{4,2},{5,3},{6,0},{7,1},{8,14},{9,15},{10,... | collective-permute-start | bytes 135176 | tf_op jit(solution)/shard_map/ppermute | solution.py:477
  260.9 7.0 %collective-permute-start.24 = (bf16[176,128]{1,0:T(8,128)(2,1)S(1)}, bf16[176,128]{1,0:T(8,128)(2,1)S(1)}, u32[]{:S(2)}, u32[]{:S(2)}) collective-permute-start(bf16[176,128]{1,0:T(8,128)(2,1)S(1)} %bitcast.372), channel_id=1, source_target_pairs={{0,8},{8,0},{16,24},{24,16},{1,9},{9,1},{17,25},{25,17},{2,10},{10... | collective-permute-start | bytes 135176 | tf_op jit(solution)/shard_map/ppermute | solution.py:477
  265.9 4.0 %collective-permute-start.25 = (bf16[176,128]{1,0:T(8,128)(2,1)S(1)}, bf16[176,128]{1,0:T(8,128)(2,1)S(1)}, u32[]{:S(2)}, u32[]{:S(2)}) collective-permute-start(bf16[176,128]{1,0:T(8,128)(2,1)S(1)} %bitcast.373), channel_id=1, source_target_pairs={{0,16},{8,24},{16,0},{24,8},{1,17},{9,25},{17,1},{25,9},{2,18},{10... | collective-permute-start | bytes 135176 | tf_op jit(solution)/shard_map/ppermute | solution.py:477
  265.9 4.9 %collective-permute-start.26 = (bf16[176,128]{1,0:T(8,128)(2,1)S(1)}, bf16[176,128]{1,0:T(8,128)(2,1)S(1)}, u32[]{:S(2)}, u32[]{:S(2)}) collective-permute-start(bf16[176,128]{1,0:T(8,128)(2,1)S(1)} %bitcast.374), channel_id=1, source_target_pairs={{0,24},{8,16},{16,8},{24,0},{1,25},{9,17},{17,9},{25,1},{2,26},{10... | collective-permute-start | bytes 135176 | tf_op jit(solution)/shard_map/ppermute | solution.py:477
  271.0 2.1 copy-start.11
  (2 other events, 1.5 us)

commit v3 on v2

--- a/solution.py
+++ b/solution.py
@@ -14,6 +14,7 @@
 WIDE = jnp.float32
 TILE = 256
 LANES = 128
+GROUP = 4
 VMEM_BYTES = 60 * 1024 * 1024
 
 
@@ -128,32 +129,35 @@
         t4[s * n4 : (s + 1) * n4, :] = part[n3 : n3 + n4, :].astype(LOW)
 
 
+def hot_of(low_part):
+    place = lax.broadcasted_iota(jnp.int32, (TILE, TILE), 0).astype(WIDE).astype(LOW)
+    return jnp.where(place == low_part, jnp.ones((), LOW), jnp.zeros((), LOW))
+
+
 def pick(tab, index_row, width):
     slabs = tab.shape[0] // width
-    low_part = index_row & (TILE - 1)
-    slab = index_row >> 8
-    hot = (lax.broadcasted_iota(jnp.int32, (TILE, TILE), 0) == low_part).astype(LOW)
-    found = nn(tab[...], hot)
-    got = jnp.zeros((width, TILE), WIDE)
+    low_part = (index_row & (TILE - 1)).astype(WIDE).astype(LOW)
+    slab = jnp.broadcast_to((index_row >> 8).astype(WIDE), (width, TILE)).astype(LOW)
+    found = nn(tab[...], hot_of(low_part)).astype(LOW)
+    got = jnp.zeros((width, TILE), LOW)
     for s in range(slabs):
         got = jnp.where(slab == s, found[s * width : (s + 1) * width, :], got)
     return got
 
 
-def weigh(coef, picked, out, slots, basis, width):
-    chunk = 32
-    for h in range(width // chunk):
-        for cb in range(basis // 4):
-            acc = [None] * 4
-            for k in range(slots):
-                g = picked[k, h * chunk : (h + 1) * chunk, :]
-                for j in range(4):
-                    row = k * basis + cb * 4 + j
-                    term = coef[row : row + 1, :] * g
-                    acc[j] = term if acc[j] is None else acc[j] + term
+def weigh(coef, picked, out, group, basis, width):
+    for cb in range(basis // 4):
+        acc = [None] * 4
+        for k in range(group * GROUP, (group + 1) * GROUP):
+            g = picked[k]
             for j in range(4):
-                at = (cb * 4 + j) * width + h * chunk
-                out[at : at + chunk, :] = acc[j].astype(LOW)
+                row = k * basis + cb * 4 + j
+                term = jnp.broadcast_to(coef[row : row + 1, :], g.shape).astype(LOW) * g
+                acc[j] = term if acc[j] is None else acc[j] + term
+        for j in range(4):
+            at = (cb * 4 + j) * width
+            before = out[at : at + width, :] + acc[j] if group else acc[j]
+            out[at : at + width, :] = before
 
 
 def gather_body(
@@ -171,19 +175,16 @@
     c3[...] = b3[...].astype(WIDE).T
     c4[...] = b4[...].astype(WIDE).T
 
-    def step3(k, carry):
-        g3[k] = pick(t3, i3[pl.ds(k, 1), :], n3)
-        return carry
-
-    lax.fori_loop(0, k3, step3, 0, unroll=4)
-
-    def step4(k, carry):
-        g4[k] = pick(t4, i4[pl.ds(k, 1), :], n4)
-        return carry
-
-    lax.fori_loop(0, k4, step4, 0, unroll=4)
-    weigh(c3, g3, s3, k3, c3.shape[0] // k3, n3)
-    weigh(c4, g4, s4, k4, c4.shape[0] // k4, n4)
+    work = [(t3, i3, g3, c3, s3, n3, k3, j) for j in range(k3 // GROUP)]
+    work += [(t4, i4, g4, c4, s4, n4, k4, j) for j in range(k4 // GROUP)]
+    for at in range(len(work) + 1):
+        if at < len(work):
+            t, i, g, _, _, n, _, j = work[at]
+            for k in range(j * GROUP, (j + 1) * GROUP):
+                g[k] = pick(t, i[k : k + 1, :], n)
+        if at:
+            _, _, g, c, out, n, count, j = work[at - 1]
+            weigh(c, g, out, j, c.shape[0] // count, n)
     p3[...] = nn(w3t[...], s3[...])
     p4[...] = nn(w4t[...], s4[...])
 
@@ -354,31 +355,25 @@
         gbil[...] = abil[...].astype(LOW)
 
 
-def unweigh(coef, dsum, index, spread, hots, slots, basis, width):
-    chunk = 32
+def unweigh(coef, dsum, index, spread, hots, group, basis, width):
     slabs = spread.shape[0] // width
-    for k in range(slots):
-        low_part = index[k : k + 1, :] & (TILE - 1)
-        hot = (lax.broadcasted_iota(jnp.int32, (TILE, TILE), 0) == low_part).astype(LOW)
-        hots[:, k * TILE : (k + 1) * TILE] = hot
-    for h in range(width // chunk):
-        for kb in range(slots // 4):
-            acc = [None] * 4
-            for c in range(basis):
-                at = c * width + h * chunk
-                d = dsum[at : at + chunk, :]
-                for j in range(4):
-                    row = (kb * 4 + j) * basis + c
-                    term = coef[row : row + 1, :] * d
-                    acc[j] = term if acc[j] is None else acc[j] + term
-            for j in range(4):
-                k = kb * 4 + j
-                slab = index[k : k + 1, :] >> 8
-                for s in range(slabs):
-                    at = s * width + h * chunk
-                    spread[at : at + chunk, k * TILE : (k + 1) * TILE] = jnp.where(
-                        slab == s, acc[j], 0.0
-                    ).astype(LOW)
+    for k in range(group * GROUP, (group + 1) * GROUP):
+        low_part = (index[k : k + 1, :] & (TILE - 1)).astype(WIDE).astype(LOW)
+        hots[:, k * TILE : (k + 1) * TILE] = hot_of(low_part)
+    acc = [None] * GROUP
+    for c in range(basis):
+        d = dsum[c * width : (c + 1) * width, :]
+        for j in range(GROUP):
+            row = (group * GROUP + j) * basis + c
+            term = jnp.broadcast_to(coef[row : row + 1, :], d.shape).astype(LOW) * d
+            acc[j] = term if acc[j] is None else acc[j] + term
+    for j in range(GROUP):
+        k = group * GROUP + j
+        slab = jnp.broadcast_to((index[k : k + 1, :] >> 8).astype(WIDE), (width, TILE)).astype(LOW)
+        for s in range(slabs):
+            spread[s * width : (s + 1) * width, k * TILE : (k + 1) * TILE] = jnp.where(
+                slab == s, acc[j], jnp.zeros((), LOW)
+            )
 
 
 def scatter_body(lb, idx, basis, w, *rest, edges, other):
@@ -395,9 +390,11 @@
         acc[...] = jnp.zeros_like(acc)
 
     coef[...] = basis[...].astype(WIDE).T
-    dsum[...] = nn(w[...], lb[...])
-    unweigh(coef, dsum, idx, spread, hots, slots, coef.shape[0] // slots, n)
-    acc[...] += nt(spread[...], hots[...])
+    dsum[...] = nn(w[...], lb[...]).astype(LOW)
+    for group in range(slots // GROUP):
+        part = slice(group * GROUP * TILE, (group + 1) * GROUP * TILE)
+        unweigh(coef, dsum, idx, spread, hots, group, coef.shape[0] // slots, n)
+        acc[...] += nt(spread[:, part], hots[:, part])
 
     @pl.when(step == pl.num_programs(0) - 1)
     def _():
@@ -596,7 +593,7 @@
         [cols(f3), cols(f4), cols(n3), cols(n4)],
         [
             pltpu.VMEM((slabs * n3, TILE), LOW), pltpu.VMEM((slabs * n4, TILE), LOW),
-            pltpu.VMEM((k3, n3, TILE), WIDE), pltpu.VMEM((k4, n4, TILE), WIDE),
+            pltpu.VMEM((k3, n3, TILE), LOW), pltpu.VMEM((k4, n4, TILE), LOW),
             pltpu.VMEM((q3, TILE), WIDE), pltpu.VMEM((q4, TILE), WIDE),
             pltpu.VMEM((n3, f3), LOW), pltpu.VMEM((n4, f4), LOW),
         ],
@@ -666,7 +663,7 @@
             [((n, edges), WIDE), (far, far_type)],
             [fixed(n, edges), fixed(*far)],
             [
-                pltpu.VMEM((slabs * n, TILE), WIDE), pltpu.VMEM((q, TILE), WIDE), pltpu.VMEM((f, TILE), WIDE),
+                pltpu.VMEM((slabs * n, TILE), WIDE), pltpu.VMEM((q, TILE), WIDE), pltpu.VMEM((f, TILE), LOW),
                 pltpu.VMEM((slabs * n, slots * TILE), LOW), pltpu.VMEM((TILE, slots * TILE), LOW),
             ],
         )

time: 274 us -> 254 us (0.927)
  Pallas kernels: 163 us -> 143 us
    pallas_call x8, Pallas kernels: 163 us -> 143 us  [call(): pl.pallas_call(body, name=name, out_shape=[jax.ShapeDtypeStruct(s, t) for...]
  transfers between devices with their start and end apart: 33 -> 33, of which waited for: 13 -> 13; matrix products, arithmetic and copies ran while one was open for 7% -> 7% of each run, Pallas kernels for 20% -> 19%
where the time goes in v3:
time: 254 us; the launch traced here: 253 us
  Pallas kernels  143 us (56%)
  starting transfers between devices  48.9 us (19%)
  waiting for transfers between devices  29.1 us (11%)
  local copies, waits for them, and re-layouts  18.4 us (7%)
  other arithmetic  12 us (5%)
    pallas_call x8, Pallas kernels, call(): pl.pallas_call(body, name=name, out_shape=[jax.ShapeDtypeStruct(s, t) for...  143 us
    ppermute x30, starting transfers between devices, swap(): return lax.ppermute(v, axis, [(j, j ^ mask) for j in range(count)])  34.8 us
    ppermute x30, waiting for transfers between devices, swap(): return lax.ppermute(v, axis, [(j, j ^ mask) for j in range(count)])  19.5 us
    all_to_all x2, waiting for transfers between devices, exchange(): lax.all_to_all(parts, 'edge', split_axis=0, concat_axis=0, tiled=True)  8.83 us
    unnamed x42, local copies, waits for them, and re-layouts  8.67 us
    all_to_all x2, starting transfers between devices, exchange(): lax.all_to_all(parts, 'edge', split_axis=0, concat_axis=0, tiled=True)  7.7 us
    all_to_all x1, starting transfers between devices, per_device(): lax.all_to_all(wanted, 'edge', split_axis=0, concat_axis=0, tiled=True)  6.35 us
    another operation x11, local copies, waits for them, and re-layouts, by_rows(): jnp.stack([parts[:, :, q:q + 128] for q in range(0, g.shape[1], 128)], ax...  5.32 us
  transfers between devices with their start and end apart: 33, of which 13 were waited for; matrix products, arithmetic and copies ran while one was open for 7% of the time, Pallas kernels for 19%

profile of v3, /device:TPU:0, one launch (start us, length us, event | category | flops | bytes accessed | tf_op | source)
XLA Modules:
  0.0 253.1 jit_solution(17742447366649968018)
XLA Ops:
  0.7 1.4 bitcast_subtract_fusion
  2.0 6.4 %all-to-all-start = ((s32[8,1,16]{2,1,0:T(1,128)}), s32[8,1,16]{2,1,0:T(1,128)S(1)}, u32[]{:S(2)}, u32[]{:S(2)}) async-start(s32[8,1,16]{2,1,0:T(1,128)} %bitcast.1), calls=%async_computation | async-start | bytes 8192 | tf_op jit(solution)/shard_map/all_to_all | solution.py:570
  8.4 1.6 select_bitcast_fusion.i3.idx
  10.0 1.6 copy.116.wd3
  11.6 1.5 copy.117.wd4
  13.1 0.8 all-to-all-done
  15.7 10.6 %source_rows.1 = (bf16[96,2048]{1,0:T(8,128)(2,1)}, f32[96,2048]{1,0:T(8,128)}, bf16[128,128]{1,0:T(8,128)(2,1)}) custom-call(bf16[2048,512]{1,0:T(8,128)(2,1)} %edge.7, bf16[2048,128]{1,0:T(8,128)(2,1)} %radial.9, s32[1,128]{1,0:T(1,128)} %reshape.201.asked, bf16[512,512]{1,0:T(8,128)(2,1)} %ws3.3, bf16[128,512]{1,0:T(8,128)(2,1)} %wr3.3, ...), custom_call_target="tpu_custom_call" | custom-call | flops 11000000512 | bytes 4194304 | tf_op jit(solution)/shard_map/source_rows/pallas_call | solution.py:65
  26.3 4.4 %all-to-all-start.1 = ((bf16[8,16,128]{2,1,0:T(8,128)(2,1)}), bf16[8,16,128]{2,1,0:T(8,128)(2,1)S(1)}, u32[]{:S(2)}, u32[]{:S(2)}) async-start(bf16[8,16,128]{2,1,0:T(8,128)(2,1)} %bitcast.376), calls=%async_computation.1 | async-start | bytes 65536 | tf_op jit(solution)/shard_map/all_to_all | solution.py:524
  31.3 0.8 copy.118.w3.w
  32.2 0.8 copy.119.w4.w
  33.0 3.4 %all-to-all-done.1 = bf16[8,16,128]{2,1,0:T(8,128)(2,1)S(1)} async-done(((bf16[8,16,128]{2,1,0:T(8,128)(2,1)}), bf16[8,16,128]{2,1,0:T(8,128)(2,1)S(1)}, u32[]{:S(2)}, u32[]{:S(2)}) %all-to-all-start.1) | async-done | bytes 32800 | tf_op jit(solution)/shard_map/all_to_all | solution.py:524
  37.0 25.1 %gather_sums.1 = (bf16[1024,2048]{1,0:T(8,128)(2,1)}, bf16[1024,2048]{1,0:T(8,128)(2,1)}, f32[64,2048]{1,0:T(8,128)}, f32[32,2048]{1,0:T(8,128)}) custom-call(bf16[96,2048]{1,0:T(8,128)(2,1)} %get-tuple-element.80.tab, bf16[128,128]{1,0:T(8,128)(2,1)} %bitcast.375, s32[16,2048]{1,0:T(8,128)} %select_bitcast_fusion.i3.idx, ...), custom_call_target="tpu_custom_call" | custom-call | flops 41799999488 | bytes 4194304 | tf_op jit(solution)/shard_map/gather_sums/pallas_call | solution.py:65
  62.1 18.9 %edge_update.1 = (f32[2048,512]{1,0:T(8,128)}, bf16[2048,512]{1,0:T(8,128)(2,1)}, bf16[2048,512]{1,0:T(8,128)(2,1)}, bf16[2048,512]{1,0:T(8,128)(2,1)}, bf16[204...) custom-call(bf16[2048,512]{1,0:T(8,128)(2,1)} %edge.7, ...), custom_call_target="tpu_custom_call" | custom-call | flops 20899999744 | bytes 4194304 | tf_op jit(solution)/shard_map/edge_update/pallas_call | solution.py:65
  81.1 15.8 %output_block.1 = (bf16[2048,512]{1,0:T(8,128)(2,1)}, f32[2048,512]{1,0:T(8,128)}, bf16[768,512]{1,0:T(8,128)(2,1)}, bf16[128,512]{1,0:T(8,128)(2,1)}, bf16[512,...) custom-call(f32[2048,512]{1,0:T(8,128)} %get-tuple-element.84.merged, ...), custom_call_target="tpu_custom_call" | custom-call | flops 17600000000 | bytes 4194304 | tf_op jit(solution)/shard_map/output_block/pallas_call | solution.py:65
  96.9 24.4 %edge_update_back.1 = (f32[2048,512]{1,0:T(8,128)}, bf16[64,2048]{1,0:T(8,128)(2,1)}, bf16[32,2048]{1,0:T(8,128)(2,1)}, bf16[512,512]{1,0:T(8,128)(2,1)}, bf16[5...) custom-call(bf16[2048,512]{1,0:T(8,128)(2,1)} %edge.7, ...), custom_call_target="tpu_custom_call" | custom-call | flops 24199999488 | bytes 4194304 | tf_op jit(solution)/shard_map/edge_update_back/pallas_call | solution.py:65
  121.3 1.2 slice_bitcast_fusion.23
  122.5 1.2 slice_bitcast_fusion.19
  126.1 1.1 dynamic-slice_bitcast_fusion
  127.5 1.6 collective-permute-start.1
  129.0 1.5 collective-permute-start.2
  131.0 10.7 %scatter_quad.1 = (f32[32,2048]{1,0:T(8,128)}, f32[32,256]{1,0:T(8,128)}) custom-call(bf16[32,2048]{1,0:T(8,128)(2,1)} %get-tuple-element.107.lb, s32[8,2048]{1,0:T(8,128)} %select_bitcast_fusion.1.i4.idx, bf16[2048,256]{1,0:T(8,128)(2,1)} %basis.2, bf16[1024,32]{1,0:T(8,128)(2,1)} %copy.119.w4.w), custom_call_target="tpu_custom_call" | custom-call | flops 12099999744 | bytes 4194304 | tf_op jit(solution)/shard_map/scatter_quad/pallas_call | solution.py:65
  141.9 1.5 fusion
  144.2 2.5 collective-permute-start.10
  148.2 3.3 %collective-permute-start.7 = (bf16[1,176,128]{2,1,0:T(8,128)(2,1)S(1)}, bf16[1,176,128]{2,1,0:T(8,128)(2,1)S(1)}, u32[]{:S(2)}, u32[]{:S(2)}) collective-permute-start(bf16[1,176,128]{2,1,0:T(8,128)(2,1)S(1)} %get-tuple-element.227), channel_id=1, source_target_pairs={{0,6},{1,7},{2,4},{3,5},{4,2},{5,3},{6,0},{7,1},{8,14},{9,15},{10,... | collective-permute-start | bytes 135176 | tf_op jit(solution)/shard_map/ppermute | solution.py:474
  151.5 17.6 %scatter_trip.1 = (f32[64,2048]{1,0:T(8,128)}, bf16[128,128]{1,0:T(8,128)(2,1)}) custom-call(bf16[64,2048]{1,0:T(8,128)(2,1)} %get-tuple-element.116.lb, s32[16,2048]{1,0:T(8,128)} %select_bitcast_fusion.i3.idx, bf16[2048,256]{1,0:T(8,128)(2,1)} %basis.3, bf16[1024,64]{1,0:T(8,128)(2,1)} %copy.118.w3.w, f32[32,256]{1,0:T(8,128)} %get-tuple-element.117.rest_0_), custom_call_target="tpu_custom_call" | custom-call | flops 22000001024 | bytes 4194304 | tf_op jit(solution)/shard_map/scatter_trip/pallas_call | solution.py:65
  169.1 3.3 %all-to-all-start.2 = ((bf16[8,16,128]{2,1,0:T(8,128)(2,1)}), bf16[8,16,128]{2,1,0:T(8,128)(2,1)S(1)}, u32[]{:S(2)}, u32[]{:S(2)}) async-start(bf16[8,16,128]{2,1,0:T(8,128)(2,1)} %bitcast.378), calls=%async_computation.2 | async-start | bytes 65536 | tf_op jit(solution)/shard_map/all_to_all | solution.py:524
  172.7 5.4 %all-to-all-done.2 = bf16[8,16,128]{2,1,0:T(8,128)(2,1)S(1)} async-done(((bf16[8,16,128]{2,1,0:T(8,128)(2,1)}), bf16[8,16,128]{2,1,0:T(8,128)(2,1)S(1)}, u32[]{:S(2)}, u32[]{:S(2)}) %all-to-all-start.2) | async-done | bytes 32800 | tf_op jit(solution)/shard_map/all_to_all | solution.py:524
  178.1 1.5 collective-permute-start.11
  179.6 1.5 collective-permute-start.12
  182.9 20.2 %source_rows_back.1 = (bf16[2048,512]{1,0:T(8,128)(2,1)}, bf16[512,512]{1,0:T(8,128)(2,1)}, bf16[512,512]{1,0:T(8,128)(2,1)}, bf16[128,512]{1,0:T(8,128)(2,1)}, ...) custom-call(bf16[2048,512]{1,0:T(8,128)(2,1)} %edge.7, bf16[2048,128]{1,0:T(8,128)(2,1)} %radial.9, ...), custom_call_target="tpu_custom_call" | custom-call | flops 20899999744 | bytes 4194304 | tf_op jit(solution)/shard_map/source_rows_back/pallas_call | solution.py:65
  203.1 1.2 slice_bitcast_fusion.11
  204.3 1.2 slice_bitcast_fusion.7
  205.9 3.3 %collective-permute-start.16 = (bf16[1,256,128]{2,1,0:T(8,128)(2,1)S(1)}, bf16[1,256,128]{2,1,0:T(8,128)(2,1)S(1)}, u32[]{:S(2)}, u32[]{:S(2)}) collective-permute-start(bf16[1,256,128]{2,1,0:T(8,128)(2,1)S(1)} %get-tuple-element.221), channel_id=1, source_target_pairs={{0,6},{1,7},{2,4},{3,5},{4,2},{5,3},{6,0},{7,1},{8,14},{9,15},{10,... | collective-permute-start | bytes 196616 | tf_op jit(solution)/shard_map/ppermute | solution.py:474
  209.3 2.7 %collective-permute-done.16 = bf16[1,256,128]{2,1,0:T(8,128)(2,1)S(1)} collective-permute-done((bf16[1,256,128]{2,1,0:T(8,128)(2,1)S(1)}, bf16[1,256,128]{2,1,0:T(8,128)(2,1)S(1)}, u32[]{:S(2)}, u32[]{:S(2)}) %collective-permute-start.16) | collective-permute-done | bytes 65568 | tf_op jit(solution)/shard_map/ppermute | solution.py:474
  212.1 1.5 collective-permute-start.27
  213.6 1.5 collective-permute-start.28
  217.9 2.4 collective-permute-done.29
  220.4 0.7 pad_maximum_fusion.3
  222.5 2.4 collective-permute-start.20
  224.9 2.8 %collective-permute-done.18 = bf16[4,176,128]{2,1,0:T(8,128)(2,1)S(1)} collective-permute-done((bf16[4,176,128]{2,1,0:T(8,128)(2,1)S(1)}, bf16[4,176,128]{2,1,0:T(8,128)(2,1)S(1)}, u32[]{:S(2)}, u32[]{:S(2)}) %collective-permute-start.18) | collective-permute-done | bytes 180256 | tf_op jit(solution)/shard_map/ppermute | solution.py:474
  227.8 3.1 %collective-permute-done.19 = bf16[4,176,128]{2,1,0:T(8,128)(2,1)S(1)} collective-permute-done((bf16[4,176,128]{2,1,0:T(8,128)(2,1)S(1)}, bf16[4,176,128]{2,1,0:T(8,128)(2,1)S(1)}, u32[]{:S(2)}, u32[]{:S(2)}) %collective-permute-start.19) | collective-permute-done | bytes 180256 | tf_op jit(solution)/shard_map/ppermute | solution.py:474
  231.1 3.8 %collective-permute-start.22 = (bf16[1,176,128]{2,1,0:T(8,128)(2,1)S(1)}, bf16[1,176,128]{2,1,0:T(8,128)(2,1)S(1)}, u32[]{:S(2)}, u32[]{:S(2)}) collective-permute-start(bf16[1,176,128]{2,1,0:T(8,128)(2,1)S(1)} %get-tuple-element.225), channel_id=1, source_target_pairs={{0,4},{1,5},{2,6},{3,7},{4,0},{5,1},{6,2},{7,3},{8,12},{9,13},{10,... | collective-permute-start | bytes 135176 | tf_op jit(solution)/shard_map/ppermute | solution.py:474
  236.2 1.7 collective-permute-done.22
  237.8 3.0 %collective-permute-done.23 = bf16[1,176,128]{2,1,0:T(8,128)(2,1)S(1)} collective-permute-done((bf16[1,176,128]{2,1,0:T(8,128)(2,1)S(1)}, bf16[1,176,128]{2,1,0:T(8,128)(2,1)S(1)}, u32[]{:S(2)}, u32[]{:S(2)}) %collective-permute-start.23) | collective-permute-done | bytes 45088 | tf_op jit(solution)/shard_map/ppermute | solution.py:474
  240.9 1.6 collective-permute-start.24
  245.9 1.9 collective-permute-start.26
  247.9 2.0 collective-permute-done.25
  249.9 0.9 collective-permute-done.26
  (154 shorter events, 22.1 us)
Async XLA Ops:
  2.0 11.9 %all-to-all-start = ((s32[8,1,16]{2,1,0:T(1,128)}), s32[8,1,16]{2,1,0:T(1,128)S(1)}, u32[]{:S(2)}, u32[]{:S(2)}) async-start(s32[8,1,16]{2,1,0:T(1,128)} %bitcast.1), calls=%async_computation | async-start | bytes 8192 | tf_op jit(solution)/shard_map/all_to_all | solution.py:570
  15.7 15.0 %copy-start.12 = (s32[2048,8]{0,1:T(8,128)S(1)}, s32[2048,8]{0,1:T(8,128)}, u32[]{:S(2)}) copy-start(s32[2048,8]{0,1:T(8,128)} %param.39) | copy-start | bytes 196612
  15.7 15.0 %copy-start.13 = (s32[2048,8]{0,1:T(8,128)S(1)}, s32[2048,8]{0,1:T(8,128)}, u32[]{:S(2)}) copy-start(s32[2048,8]{0,1:T(8,128)} %param.40) | copy-start | bytes 196612
  15.7 15.7 %copy-start.4 = (bf16[1024,64]{0,1:T(8,128)(2,1)S(1)}, bf16[1024,64]{0,1:T(8,128)(2,1)}, u32[]{:S(2)}) copy-start(bf16[1024,64]{0,1:T(8,128)(2,1)} %param.49) | copy-start | bytes 393220
  15.7 16.5 %copy-start.14 = (bf16[1024,32]{0,1:T(8,128)(2,1)S(1)}, bf16[1024,32]{0,1:T(8,128)(2,1)}, u32[]{:S(2)}) copy-start(bf16[1024,32]{0,1:T(8,128)(2,1)} %param.51) | copy-start | bytes 196612
  26.3 10.1 %all-to-all-start.1 = ((bf16[8,16,128]{2,1,0:T(8,128)(2,1)}), bf16[8,16,128]{2,1,0:T(8,128)(2,1)S(1)}, u32[]{:S(2)}, u32[]{:S(2)}) async-start(bf16[8,16,128]{2,1,0:T(8,128)(2,1)} %bitcast.376), calls=%async_computation.1 | async-start | bytes 65536 | tf_op jit(solution)/shard_map/all_to_all | solution.py:524
  121.2 2.5 copy-start.2
  121.3 2.6 %copy-start = (bf16[768,512]{1,0:T(8,128)(2,1)S(1)}, bf16[768,512]{1,0:T(8,128)(2,1)}, u32[]{:S(2)}) copy-start(bf16[768,512]{1,0:T(8,128)(2,1)} %get-tuple-element.104) | copy-start | bytes 2359300
  122.5 1.5 copy-start.1
  123.7 0.9 copy-start.7
  124.9 0.9 copy-start.5
  125.0 1.0 copy-start.3
  125.0 2.3 collective-permute-start
  127.1 14.7 %collective-permute-start.4 = (bf16[4,4,256,128]{3,2,1,0:T(8,128)(2,1)}, bf16[4,4,256,128]{3,2,1,0:T(8,128)(2,1)}, u32[]{:S(2)}, u32[]{:S(2)}) collective-permute-start(bf16[4,4,256,128]{3,2,1,0:T(8,128)(2,1)} %dynamic-slice_bitcast_fusion), channel_id=1, source_target_pairs={{0,1},{1,0},{2,3},{3,2},{4,5},{5,4},{6,7},{7,6},{8,9},{9,8},{10,11... | collective-permute-start | bytes 3145736 | tf_op jit(solution)/shard_map/ppermute | solution.py:474
  127.5 14.3 %collective-permute-start.1 = (bf16[4,176,128]{2,1,0:T(8,128)(2,1)S(1)}, bf16[4,176,128]{2,1,0:T(8,128)(2,1)S(1)}, u32[]{:S(2)}, u32[]{:S(2)}) collective-permute-start(bf16[4,176,128]{2,1,0:T(8,128)(2,1)S(1)} %get-tuple-element.149), channel_id=1, source_target_pairs={{0,8},{8,0},{16,24},{24,16},{1,9},{9,1},{17,25},{25,17},{2,10},{10... | collective-permute-start | bytes 540680 | tf_op jit(solution)/shard_map/ppermute | solution.py:474
  129.0 12.7 %collective-permute-start.2 = (bf16[4,176,128]{2,1,0:T(8,128)(2,1)S(1)}, bf16[4,176,128]{2,1,0:T(8,128)(2,1)S(1)}, u32[]{:S(2)}, u32[]{:S(2)}) collective-permute-start(bf16[4,176,128]{2,1,0:T(8,128)(2,1)S(1)} %get-tuple-element.151), channel_id=1, source_target_pairs={{0,16},{8,24},{16,0},{24,8},{1,17},{9,25},{17,1},{25,9},{2,18},{10... | collective-permute-start | bytes 540680 | tf_op jit(solution)/shard_map/ppermute | solution.py:474
  130.5 11.2 %collective-permute-start.3 = (bf16[4,176,128]{2,1,0:T(8,128)(2,1)S(1)}, bf16[4,176,128]{2,1,0:T(8,128)(2,1)S(1)}, u32[]{:S(2)}, u32[]{:S(2)}) collective-permute-start(bf16[4,176,128]{2,1,0:T(8,128)(2,1)S(1)} %get-tuple-element.150), channel_id=1, source_target_pairs={{0,24},{8,16},{16,8},{24,0},{1,25},{9,17},{17,9},{25,1},{2,26},{10... | collective-permute-start | bytes 540680 | tf_op jit(solution)/shard_map/ppermute | solution.py:474
  143.4 4.8 %collective-permute-start.5 = (bf16[1,176,128]{2,1,0:T(8,128)(2,1)S(1)}, bf16[1,176,128]{2,1,0:T(8,128)(2,1)S(1)}, u32[]{:S(2)}, u32[]{:S(2)}) collective-permute-start(bf16[1,176,128]{2,1,0:T(8,128)(2,1)S(1)} %get-tuple-element.226), channel_id=1, source_target_pairs={{0,2},{1,3},{2,0},{3,1},{4,6},{5,7},{6,4},{7,5},{8,10},{9,11},{10,... | collective-permute-start | bytes 135176 | tf_op jit(solution)/shard_map/ppermute | solution.py:474
  144.2 28.3 %collective-permute-start.10 = (bf16[4,256,128]{2,1,0:T(8,128)(2,1)S(1)}, bf16[4,256,128]{2,1,0:T(8,128)(2,1)S(1)}, u32[]{:S(2)}, u32[]{:S(2)}) collective-permute-start(bf16[4,256,128]{2,1,0:T(8,128)(2,1)S(1)} %get-tuple-element.140), channel_id=1, source_target_pairs={{0,24},{8,16},{16,8},{24,0},{1,25},{9,17},{17,9},{25,1},{2,26},{10... | collective-permute-start | bytes 786440 | tf_op jit(solution)/shard_map/ppermute | solution.py:474
  146.7 25.8 %collective-permute-start.8 = (bf16[4,256,128]{2,1,0:T(8,128)(2,1)S(1)}, bf16[4,256,128]{2,1,0:T(8,128)(2,1)S(1)}, u32[]{:S(2)}, u32[]{:S(2)}) collective-permute-start(bf16[4,256,128]{2,1,0:T(8,128)(2,1)S(1)} %get-tuple-element.139), channel_id=1, source_target_pairs={{0,8},{8,0},{16,24},{24,16},{1,9},{9,1},{17,25},{25,17},{2,10},{10... | collective-permute-start | bytes 786440 | tf_op jit(solution)/shard_map/ppermute | solution.py:474
  147.2 25.3 %collective-permute-start.9 = (bf16[4,256,128]{2,1,0:T(8,128)(2,1)S(1)}, bf16[4,256,128]{2,1,0:T(8,128)(2,1)S(1)}, u32[]{:S(2)}, u32[]{:S(2)}) collective-permute-start(bf16[4,256,128]{2,1,0:T(8,128)(2,1)S(1)} %get-tuple-element.141), channel_id=1, source_target_pairs={{0,16},{8,24},{16,0},{24,8},{1,17},{9,25},{17,1},{25,9},{2,18},{10... | collective-permute-start | bytes 786440 | tf_op jit(solution)/shard_map/ppermute | solution.py:474
  147.7 24.7 %collective-permute-start.6 = (bf16[1,176,128]{2,1,0:T(8,128)(2,1)S(1)}, bf16[1,176,128]{2,1,0:T(8,128)(2,1)S(1)}, u32[]{:S(2)}, u32[]{:S(2)}) collective-permute-start(bf16[1,176,128]{2,1,0:T(8,128)(2,1)S(1)} %get-tuple-element.228), channel_id=1, source_target_pairs={{0,4},{1,5},{2,6},{3,7},{4,0},{5,1},{6,2},{7,3},{8,12},{9,13},{10,... | collective-permute-start | bytes 135176 | tf_op jit(solution)/shard_map/ppermute | solution.py:474
  148.2 24.2 %collective-permute-start.7 = (bf16[1,176,128]{2,1,0:T(8,128)(2,1)S(1)}, bf16[1,176,128]{2,1,0:T(8,128)(2,1)S(1)}, u32[]{:S(2)}, u32[]{:S(2)}) collective-permute-start(bf16[1,176,128]{2,1,0:T(8,128)(2,1)S(1)} %get-tuple-element.227), channel_id=1, source_target_pairs={{0,6},{1,7},{2,4},{3,5},{4,2},{5,3},{6,0},{7,1},{8,14},{9,15},{10,... | collective-permute-start | bytes 135176 | tf_op jit(solution)/shard_map/ppermute | solution.py:474
  169.1 9.0 %all-to-all-start.2 = ((bf16[8,16,128]{2,1,0:T(8,128)(2,1)}), bf16[8,16,128]{2,1,0:T(8,128)(2,1)S(1)}, u32[]{:S(2)}, u32[]{:S(2)}) async-start(bf16[8,16,128]{2,1,0:T(8,128)(2,1)} %bitcast.378), calls=%async_computation.2 | async-start | bytes 65536 | tf_op jit(solution)/shard_map/all_to_all | solution.py:524
  178.1 4.7 %copy-start.16 = (bf16[8,16,128]{2,1,0:T(8,128)(2,1)}, bf16[8,16,128]{2,1,0:T(8,128)(2,1)S(1)}, u32[]{:S(2)}) copy-start(bf16[8,16,128]{2,1,0:T(8,128)(2,1)S(1)} %all-to-all-done.2) | copy-start | bytes 98308
  178.1 27.7 %collective-permute-start.11 = (bf16[176,128]{1,0:T(8,128)(2,1)S(1)}, bf16[176,128]{1,0:T(8,128)(2,1)S(1)}, u32[]{:S(2)}, u32[]{:S(2)}) collective-permute-start(bf16[176,128]{1,0:T(8,128)(2,1)S(1)} %fusion.13), channel_id=1, source_target_pairs={{0,8},{8,0},{16,24},{24,16},{1,9},{9,1},{17,25},{25,17},{2,10},{10... | collective-permute-start | bytes 135176 | tf_op jit(solution)/shard_map/ppermute | solution.py:474
  179.6 29.6 %collective-permute-start.12 = (bf16[176,128]{1,0:T(8,128)(2,1)S(1)}, bf16[176,128]{1,0:T(8,128)(2,1)S(1)}, u32[]{:S(2)}, u32[]{:S(2)}) collective-permute-start(bf16[176,128]{1,0:T(8,128)(2,1)S(1)} %fusion.13), channel_id=1, source_target_pairs={{0,16},{8,24},{16,0},{24,8},{1,17},{9,25},{17,1},{25,9},{2,18},{10... | collective-permute-start | bytes 135176 | tf_op jit(solution)/shard_map/ppermute | solution.py:474
  181.1 28.1 %collective-permute-start.13 = (bf16[176,128]{1,0:T(8,128)(2,1)S(1)}, bf16[176,128]{1,0:T(8,128)(2,1)S(1)}, u32[]{:S(2)}, u32[]{:S(2)}) collective-permute-start(bf16[176,128]{1,0:T(8,128)(2,1)S(1)} %fusion.13), channel_id=1, source_target_pairs={{0,24},{8,16},{16,8},{24,0},{1,25},{9,17},{17,9},{25,1},{2,26},{10... | collective-permute-start | bytes 135176 | tf_op jit(solution)/shard_map/ppermute | solution.py:474
  181.6 27.7 %collective-permute-start.14 = (bf16[1,256,128]{2,1,0:T(8,128)(2,1)S(1)}, bf16[1,256,128]{2,1,0:T(8,128)(2,1)S(1)}, u32[]{:S(2)}, u32[]{:S(2)}) collective-permute-start(bf16[1,256,128]{2,1,0:T(8,128)(2,1)S(1)} %get-tuple-element.220), channel_id=1, source_target_pairs={{0,2},{1,3},{2,0},{3,1},{4,6},{5,7},{6,4},{7,5},{8,10},{9,11},{10,... | collective-permute-start | bytes 196616 | tf_op jit(solution)/shard_map/ppermute | solution.py:474
  182.3 27.0 %collective-permute-start.15 = (bf16[1,256,128]{2,1,0:T(8,128)(2,1)S(1)}, bf16[1,256,128]{2,1,0:T(8,128)(2,1)S(1)}, u32[]{:S(2)}, u32[]{:S(2)}) collective-permute-start(bf16[1,256,128]{2,1,0:T(8,128)(2,1)S(1)} %get-tuple-element.222), channel_id=1, source_target_pairs={{0,4},{1,5},{2,6},{3,7},{4,0},{5,1},{6,2},{7,3},{8,12},{9,13},{10,... | collective-permute-start | bytes 196616 | tf_op jit(solution)/shard_map/ppermute | solution.py:474
  203.1 2.4 copy-start.10
  203.1 2.4 copy-start.9
  204.3 1.5 copy-start.8
  205.9 6.1 %collective-permute-start.16 = (bf16[1,256,128]{2,1,0:T(8,128)(2,1)S(1)}, bf16[1,256,128]{2,1,0:T(8,128)(2,1)S(1)}, u32[]{:S(2)}, u32[]{:S(2)}) collective-permute-start(bf16[1,256,128]{2,1,0:T(8,128)(2,1)S(1)} %get-tuple-element.221), channel_id=1, source_target_pairs={{0,6},{1,7},{2,4},{3,5},{4,2},{5,3},{6,0},{7,1},{8,14},{9,15},{10,... | collective-permute-start | bytes 196616 | tf_op jit(solution)/shard_map/ppermute | solution.py:474
  212.1 5.1 %collective-permute-start.27 = (bf16[256,128]{1,0:T(8,128)(2,1)S(1)}, bf16[256,128]{1,0:T(8,128)(2,1)S(1)}, u32[]{:S(2)}, u32[]{:S(2)}) collective-permute-start(bf16[256,128]{1,0:T(8,128)(2,1)S(1)} %fusion.12), channel_id=1, source_target_pairs={{0,8},{8,0},{16,24},{24,16},{1,9},{9,1},{17,25},{25,17},{2,10},{10... | collective-permute-start | bytes 196616 | tf_op jit(solution)/shard_map/ppermute | solution.py:474
  213.6 4.3 %collective-permute-start.28 = (bf16[256,128]{1,0:T(8,128)(2,1)S(1)}, bf16[256,128]{1,0:T(8,128)(2,1)S(1)}, u32[]{:S(2)}, u32[]{:S(2)}) collective-permute-start(bf16[256,128]{1,0:T(8,128)(2,1)S(1)} %fusion.12), channel_id=1, source_target_pairs={{0,16},{8,24},{16,0},{24,8},{1,17},{9,25},{17,1},{25,9},{2,18},{10... | collective-permute-start | bytes 196616 | tf_op jit(solution)/shard_map/ppermute | solution.py:474
  215.1 5.2 %collective-permute-start.29 = (bf16[256,128]{1,0:T(8,128)(2,1)S(1)}, bf16[256,128]{1,0:T(8,128)(2,1)S(1)}, u32[]{:S(2)}, u32[]{:S(2)}) collective-permute-start(bf16[256,128]{1,0:T(8,128)(2,1)S(1)} %fusion.12), channel_id=1, source_target_pairs={{0,24},{8,16},{16,8},{24,0},{1,25},{9,17},{17,9},{25,1},{2,26},{10... | collective-permute-start | bytes 196616 | tf_op jit(solution)/shard_map/ppermute | solution.py:474
  215.8 5.4 %collective-permute-start.17 = (bf16[4,4,176,128]{3,2,1,0:T(8,128)(2,1)S(1)}, bf16[4,4,176,128]{3,2,1,0:T(8,128)(2,1)S(1)}, u32[]{:S(2)}, u32[]{:S(2)}) collective-permute-start(bf16[4,4,176,128]{3,2,1,0:T(8,128)(2,1)S(1)} %dynamic-slice_bitcast_fusion.1), channel_id=1, source_target_pairs={{0,1},{1,0},{2,3},{3,2},{4,5},{5,4},{6,7},{7,6},{8,9},{9,8},{10,11... | collective-permute-start | bytes 2162696 | tf_op jit(solution)/shard_map/ppermute | solution.py:474
  221.4 6.4 %collective-permute-start.18 = (bf16[4,176,128]{2,1,0:T(8,128)(2,1)S(1)}, bf16[4,176,128]{2,1,0:T(8,128)(2,1)S(1)}, u32[]{:S(2)}, u32[]{:S(2)}) collective-permute-start(bf16[4,176,128]{2,1,0:T(8,128)(2,1)S(1)} %get-tuple-element.146), channel_id=1, source_target_pairs={{0,8},{8,0},{16,24},{24,16},{1,9},{9,1},{17,25},{25,17},{2,10},{10... | collective-permute-start | bytes 540680 | tf_op jit(solution)/shard_map/ppermute | solution.py:474
  222.0 8.9 %collective-permute-start.19 = (bf16[4,176,128]{2,1,0:T(8,128)(2,1)S(1)}, bf16[4,176,128]{2,1,0:T(8,128)(2,1)S(1)}, u32[]{:S(2)}, u32[]{:S(2)}) collective-permute-start(bf16[4,176,128]{2,1,0:T(8,128)(2,1)S(1)} %get-tuple-element.148), channel_id=1, source_target_pairs={{0,16},{8,24},{16,0},{24,8},{1,17},{9,25},{17,1},{25,9},{2,18},{10... | collective-permute-start | bytes 540680 | tf_op jit(solution)/shard_map/ppermute | solution.py:474
  222.5 8.4 %collective-permute-start.20 = (bf16[4,176,128]{2,1,0:T(8,128)(2,1)S(1)}, bf16[4,176,128]{2,1,0:T(8,128)(2,1)S(1)}, u32[]{:S(2)}, u32[]{:S(2)}) collective-permute-start(bf16[4,176,128]{2,1,0:T(8,128)(2,1)S(1)} %get-tuple-element.147), channel_id=1, source_target_pairs={{0,24},{8,16},{16,8},{24,0},{1,25},{9,17},{17,9},{25,1},{2,26},{10... | collective-permute-start | bytes 540680 | tf_op jit(solution)/shard_map/ppermute | solution.py:474
  231.1 5.1 %collective-permute-start.21 = (bf16[1,176,128]{2,1,0:T(8,128)(2,1)S(1)}, bf16[1,176,128]{2,1,0:T(8,128)(2,1)S(1)}, u32[]{:S(2)}, u32[]{:S(2)}) collective-permute-start(bf16[1,176,128]{2,1,0:T(8,128)(2,1)S(1)} %get-tuple-element.223), channel_id=1, source_target_pairs={{0,2},{1,3},{2,0},{3,1},{4,6},{5,7},{6,4},{7,5},{8,10},{9,11},{10,... | collective-permute-start | bytes 135176 | tf_op jit(solution)/shard_map/ppermute | solution.py:474
  231.1 6.7 %collective-permute-start.22 = (bf16[1,176,128]{2,1,0:T(8,128)(2,1)S(1)}, bf16[1,176,128]{2,1,0:T(8,128)(2,1)S(1)}, u32[]{:S(2)}, u32[]{:S(2)}) collective-permute-start(bf16[1,176,128]{2,1,0:T(8,128)(2,1)S(1)} %get-tuple-element.225), channel_id=1, source_target_pairs={{0,4},{1,5},{2,6},{3,7},{4,0},{5,1},{6,2},{7,3},{8,12},{9,13},{10,... | collective-permute-start | bytes 135176 | tf_op jit(solution)/shard_map/ppermute | solution.py:474
  235.0 5.8 %collective-permute-start.23 = (bf16[1,176,128]{2,1,0:T(8,128)(2,1)S(1)}, bf16[1,176,128]{2,1,0:T(8,128)(2,1)S(1)}, u32[]{:S(2)}, u32[]{:S(2)}) collective-permute-start(bf16[1,176,128]{2,1,0:T(8,128)(2,1)S(1)} %get-tuple-element.224), channel_id=1, source_target_pairs={{0,6},{1,7},{2,4},{3,5},{4,2},{5,3},{6,0},{7,1},{8,14},{9,15},{10,... | collective-permute-start | bytes 135176 | tf_op jit(solution)/shard_map/ppermute | solution.py:474
  240.9 7.0 %collective-permute-start.24 = (bf16[176,128]{1,0:T(8,128)(2,1)S(1)}, bf16[176,128]{1,0:T(8,128)(2,1)S(1)}, u32[]{:S(2)}, u32[]{:S(2)}) collective-permute-start(bf16[176,128]{1,0:T(8,128)(2,1)S(1)} %bitcast.372), channel_id=1, source_target_pairs={{0,8},{8,0},{16,24},{24,16},{1,9},{9,1},{17,25},{25,17},{2,10},{10... | collective-permute-start | bytes 135176 | tf_op jit(solution)/shard_map/ppermute | solution.py:474
  245.9 4.0 %collective-permute-start.25 = (bf16[176,128]{1,0:T(8,128)(2,1)S(1)}, bf16[176,128]{1,0:T(8,128)(2,1)S(1)}, u32[]{:S(2)}, u32[]{:S(2)}) collective-permute-start(bf16[176,128]{1,0:T(8,128)(2,1)S(1)} %bitcast.373), channel_id=1, source_target_pairs={{0,16},{8,24},{16,0},{24,8},{1,17},{9,25},{17,1},{25,9},{2,18},{10... | collective-permute-start | bytes 135176 | tf_op jit(solution)/shard_map/ppermute | solution.py:474
  245.9 4.9 %collective-permute-start.26 = (bf16[176,128]{1,0:T(8,128)(2,1)S(1)}, bf16[176,128]{1,0:T(8,128)(2,1)S(1)}, u32[]{:S(2)}, u32[]{:S(2)}) collective-permute-start(bf16[176,128]{1,0:T(8,128)(2,1)S(1)} %bitcast.374), channel_id=1, source_target_pairs={{0,24},{8,16},{16,8},{24,0},{1,25},{9,17},{17,9},{25,1},{2,26},{10... | collective-permute-start | bytes 135176 | tf_op jit(solution)/shard_map/ppermute | solution.py:474
  251.0 2.1 copy-start.11
  (2 other events, 1.5 us)

commit v4 on v3

v4 whole, which is shorter than its diff:
```python
import functools
import math

import jax
import jax.numpy as jnp
from jax import lax
from jax.experimental import pallas as pl
from jax.experimental.pallas import tpu as pltpu
from jax.sharding import PartitionSpec as P

HALF_ROOT = 1.0 / math.sqrt(2.0)
THIRD_ROOT = 1.0 / math.sqrt(3.0)
LOW = jnp.bfloat16
WIDE = jnp.float32
TILE = 256
LANES = 128
GROUP = 4
PARTS = 4
VMEM_BYTES = 60 * 1024 * 1024


def sigma(v):
    return 0.5 * jnp.tanh(0.5 * v) + 0.5


def slope_of(v, s):
    return s * (1.0 + v * (1.0 - s))


def nn(a, b):
    return jnp.dot(a, b, preferred_element_type=WIDE)


def nt(a, b):
    return lax.dot_general(a, b, (((1,), (1,)), ((), ())), preferred_element_type=WIDE)


def tn(a, b):
    return lax.dot_general(a, b, (((0,), (0,)), ((), ())), preferred_element_type=WIDE)


def split_pair(v):
    high = v.astype(LOW)
    rest = (v - high.astype(WIDE)).astype(LOW)
    return jnp.concatenate([high, rest], axis=0)


def whole(array):
    rank = len(array.shape)
    return pl.BlockSpec(array.shape, lambda i: (0,) * rank)


def rows(width, tile=TILE):
    return pl.BlockSpec((tile, width), lambda i: (i, 0))


def cols(height):
    return pl.BlockSpec((height, TILE), lambda i: (0, i))


def fixed(*shape):
    return pl.BlockSpec(shape, lambda i: (0,) * len(shape))


def call(body, name, steps, micros, ins, in_specs, outs, out_specs, scratch):
    return pl.pallas_call(
        body,
        name=name,
        out_shape=[jax.ShapeDtypeStruct(s, t) for s, t in outs],
        grid_spec=pltpu.PrefetchScalarGridSpec(
            num_scalar_prefetch=0,
            grid=(steps,),
            in_specs=in_specs,
            out_specs=out_specs,
            scratch_shapes=scratch,
        ),
        compiler_params=pltpu.CompilerParams(
            dimension_semantics=("arbitrary",), vmem_limit_bytes=VMEM_BYTES
        ),
        cost_estimate=pl.CostEstimate(
            flops=int(micros * 1.1e9), transcendentals=0, bytes_accessed=1 << 22
        ),
    )(*ins)


def up16(n):
    return -(-n // 16) * 16


def offsets(parts, peers):
    at, places = 0, []
    for kind, shape in parts:
        places.append(at)
        at += up16(shape[0] // peers if kind == "rows" else shape[0] // PARTS)
    return places, at


def fits(peers, rbf):
    return rbf % (16 * peers) == 0


def grad_outs(parts, peers, inside):
    if inside:
        shapes = [(PARTS, peers // 2, offsets(parts, peers)[1], LANES)] * 2
    else:
        shapes = [shape for _, shape in parts]
    return [(shape, LOW) for shape in shapes], [fixed(*shape) for shape in shapes]


def emit(outs, parts, values, peers, inside, start=0):
    if not inside:
        for out, value in zip(outs, values):
            out[...] = value[...].astype(LOW)
        return
    core = lax.axis_index("edge") & 1
    z = lax.axis_index("edge") >> 1
    grp = lax.axis_index("grp")
    places, _ = offsets(parts, peers)
    for to, side in zip(outs, (1 - core, core)):
        for mz in range(peers // 2):
            for mg in range(PARTS):
                e = ((z ^ mz) << 1) + side
                q = grp ^ mg
                for (kind, shape), place, value in zip(parts, places, values):
                    place += start
                    if kind == "rows":
                        m = shape[0] // peers
                        at = pl.multiple_of(e * m, m)
                        to[mg, mz, place : place + m, :] = value[
                            pl.ds(at, m), pl.ds(pl.multiple_of(q * LANES, LANES), LANES)
                        ].astype(LOW)
                    else:
                        h, w = shape[0] // PARTS, shape[1] // peers
                        at = pl.multiple_of(q * h, 8)
                        if w == LANES:
                            got = value[pl.ds(at, h), pl.ds(pl.multiple_of(e * w, w), w)]
                        else:
                            two = value[pl.ds(at, h), pl.ds(pl.multiple_of((z ^ mz) * LANES, LANES), LANES)]
                            got = jnp.where(side > 0, jnp.concatenate([two[:, w:], two[:, :w]], axis=1), two)
                        if up16(h) > h:
                            got = jnp.concatenate([got, jnp.zeros((up16(h) - h, LANES), WIDE)], axis=0)
                        to[mg, mz, place : place + up16(h), :] = got.astype(LOW)


def pack(parts, grads, peers):
    packed = []
    for (kind, shape), g in zip(parts, grads):
        if kind == "rows":
            g = g.reshape(peers // 2, 2, shape[0] // peers, PARTS, LANES).transpose(1, 3, 0, 2, 4)
        else:
            w = shape[1] // peers
            g = g.reshape(PARTS, shape[0] // PARTS, peers // 2, 2, w).transpose(3, 0, 2, 1, 4)
            g = jnp.pad(g, ((0, 0),) * 4 + ((0, LANES - w),))
        rows_up = up16(g.shape[3])
        packed.append(jnp.pad(g, ((0, 0),) * 3 + ((0, rows_up - g.shape[3]), (0, 0))))
    packed = jnp.concatenate(packed, axis=3)
    place = lax.axis_index("edge")
    own = place & 1
    packed = jnp.take(packed, jnp.arange(PARTS) ^ lax.axis_index("grp"), axis=1)
    packed = jnp.take(packed, jnp.arange(peers // 2) ^ (place >> 1), axis=2)
    return [lax.dynamic_index_in_dim(packed, side, 0, keepdims=False) for side in (1 - own, own)]


def assemble_body(*refs, parts, peers):
    arrived, outs, tmp = refs[:PARTS], refs[PARTS:-1], refs[-1]
    grp = lax.axis_index("grp")
    for (kind, shape), place, out in zip(parts, offsets(parts, peers)[0], outs):
        m = shape[0] // peers
        h, w = shape[0] // PARTS, shape[1] // peers
        for mg in range(PARTS):
            q = grp ^ mg
            if kind == "rows":
                got = arrived[mg][place : place + m, :].astype(WIDE)
                out[:, pl.ds(pl.multiple_of(q * LANES, LANES), LANES)] = got
            else:
                tmp[pl.ds(pl.multiple_of(q * h, 8), h), :] = arrived[mg][place : place + h, :].astype(WIDE)
        if kind == "cols":
            out[...] = tmp[0 : shape[0], 0:w]
        if kind == "turned":
            out[...] = tmp[0 : shape[0], :].T[0:w, :]


def assemble(arrived, parts, peers, name):
    shapes = []
    for kind, (n, w) in parts:
        shapes.append((n // peers, w) if kind == "rows" else (n, w // peers) if kind == "cols" else (w // peers, n))
    return call(
        functools.partial(assemble_body, parts=parts, peers=peers), name, 1, 2, arrived,
        [whole(v) for v in arrived], [(shape, WIDE) for shape in shapes], [fixed(*shape) for shape in shapes],
        [pltpu.VMEM((LANES, LANES), WIDE)],
    )


def source_body(edge, radial, ws3, wr3, wd3, ws4, wr4, wd4, table, down):
    e = edge[...]
    r = radial[...]
    pre3 = nn(e, ws3[...])
    mix3 = (pre3 * sigma(pre3) * nn(r, wr3[...])).astype(LOW)
    down3 = nt(wd3[...], mix3)
    pre4 = nn(e, ws4[...])
    mix4 = (pre4 * sigma(pre4) * nn(r, wr4[...])).astype(LOW)
    down4 = nt(wd4[...], mix4)
    both = jnp.concatenate([down3, down4], axis=0)
    down[...] = both
    table[...] = (both * sigma(both)).astype(LOW)


def sent_body(table, asked, sent, row):
    nb, edges = table.shape
    ghosts = row.shape[1]
    got = jnp.concatenate([asked[p : p + 1, :] for p in range(asked.shape[0])], axis=1) & (edges - 1)
    row[...] = got
    total = jnp.zeros((nb, ghosts), WIDE)
    for s in range(edges // TILE):
        place = lax.broadcasted_iota(jnp.int32, (TILE, ghosts), 0) + s * TILE
        total = total + nn(table[:, s * TILE : (s + 1) * TILE], (place == got).astype(LOW))
    total = jnp.concatenate([total, jnp.zeros((LANES - nb, ghosts), WIDE)], axis=0)
    sent[...] = total.T.astype(LOW)


def fill_slabs(tab, ghost, t3, t4, n3, n4):
    local = tab.shape[1] // TILE
    for s in range(local):
        t3[s * n3 : (s + 1) * n3, :] = tab[0:n3, s * TILE : (s + 1) * TILE]
        t4[s * n4 : (s + 1) * n4, :] = tab[n3 : n3 + n4, s * TILE : (s + 1) * TILE]
    for g in range(0, ghost.shape[0], TILE):
        s = local + g // TILE
        size = min(TILE, ghost.shape[0] - g)
        part = ghost[g : g + size, :].astype(WIDE).T
        if size < TILE:
            part = jnp.concatenate([part, jnp.zeros((LANES, TILE - size), WIDE)], axis=1)
        t3[s * n3 : (s + 1) * n3, :] = part[0:n3, :].astype(LOW)
        t4[s * n4 : (s + 1) * n4, :] = part[n3 : n3 + n4, :].astype(LOW)


def hot_of(low_part):
    place = lax.broadcasted_iota(jnp.int32, (TILE, TILE), 0).astype(WIDE).astype(LOW)
    return jnp.where(place == low_part, jnp.ones((), LOW), jnp.zeros((), LOW))


def pick(tab, index_row, width):
    slabs = tab.shape[0] // width
    low_part = (index_row & (TILE - 1)).astype(WIDE).astype(LOW)
    slab = jnp.broadcast_to((index_row >> 8).astype(WIDE), (width, TILE)).astype(LOW)
    found = nn(tab[...], hot_of(low_part)).astype(LOW)
    got = jnp.zeros((width, TILE), LOW)
    for s in range(slabs):
        got = jnp.where(slab == s, found[s * width : (s + 1) * width, :], got)
    return got


def weigh(coef, picked, out, group, basis, width):
    for cb in range(basis // 4):
        acc = [None] * 4
        for k in range(group * GROUP, (group + 1) * GROUP):
            g = picked[k]
            for j in range(4):
                row = k * basis + cb * 4 + j
                term = jnp.broadcast_to(coef[row : row + 1, :], g.shape).astype(LOW) * g
                acc[j] = term if acc[j] is None else acc[j] + term
        for j in range(4):
            at = (cb * 4 + j) * width
            before = out[at : at + width, :] + acc[j] if group else acc[j]
            out[at : at + width, :] = before


def chosen(index, mask):
    return jnp.where(mask > 0, index, -1)


def gather_body(
    tab, ghost, i3, m3, i4, m4, b3, b4, w3t, w4t, s3, s4, p3, p4, t3, t4, g3, g4, c3, c4
):
    n3, n4 = w3t.shape[0], w4t.shape[0]
    k3, k4 = i3.shape[0], i4.shape[0]

    @pl.when(pl.program_id(0) == 0)
    def _():
        fill_slabs(tab, ghost, t3, t4, n3, n4)

    c3[...] = b3[...].astype(WIDE).T
    c4[...] = b4[...].astype(WIDE).T

    work = [(t3, i3, m3, g3, c3, s3, n3, k3, j) for j in range(k3 // GROUP)]
    work += [(t4, i4, m4, g4, c4, s4, n4, k4, j) for j in range(k4 // GROUP)]
    for at in range(len(work) + 1):
        if at < len(work):
            t, i, m, g, _, _, n, _, j = work[at]
            for k in range(j * GROUP, (j + 1) * GROUP):
                g[k] = pick(t, chosen(i[k : k + 1, :], m[k : k + 1, :]), n)
        if at:
            _, _, _, g, c, out, n, count, j = work[at - 1]
            weigh(c, g, out, j, c.shape[0] // count, n)
    p3[...] = nn(w3t[...], s3[...])
    p4[...] = nn(w4t[...], s4[...])


def mix_body(
    edge, radial, p3, p4, trow, wu3, wu4, wsk, wr1, wr2, wra, wat, atom,
    merged, mixlow, reshid, dsk, du3, du4, dr1, dr2, gath, anew, aslope, acc,
):
    step = pl.program_id(0)
    atoms = acc.shape[0]
    v3 = p3[...]
    v4 = p4[...]
    h3 = (v3 * sigma(v3)).T.astype(LOW)
    h4 = (v4 * sigma(v4)).T.astype(LOW)
    up3 = nn(h3, wu3[...])
    s = sigma(up3)
    du3[...] = slope_of(up3, s).astype(LOW)
    total = up3 * s
    up4 = nn(h4, wu4[...])
    s = sigma(up4)
    du4[...] = slope_of(up4, s).astype(LOW)
    total = total + up4 * s
    skip = nn(edge[...], wsk[...])
    s = sigma(skip)
    dsk[...] = slope_of(skip, s).astype(LOW)
    mixed = (total + skip * s) * THIRD_ROOT
    low_mixed = mixed.astype(LOW)
    mixlow[...] = low_mixed
    res = nn(low_mixed, wr1[...])
    s = sigma(res)
    dr1[...] = slope_of(res, s).astype(LOW)
    hid = (res * s).astype(LOW)
    reshid[...] = hid
    res2 = nn(hid, wr2[...])
    s = sigma(res2)
    dr2[...] = (0.5 * slope_of(res2, s)).astype(LOW)
    out = (edge[...].astype(WIDE) + (mixed + res2 * s) * HALF_ROOT) * HALF_ROOT
    merged[...] = out
    weighted = (out * nn(radial[...], wra[...])).astype(LOW)
    hot_t = (lax.broadcasted_iota(jnp.int32, (atoms, TILE), 0) == trow[...]).astype(LOW)
    part = nn(hot_t, weighted)

    @pl.when(step == 0)
    def _():
        acc[...] = part

    @pl.when(step > 0)
    def _():
        acc[...] += part

    @pl.when(step == pl.num_programs(0) - 1)
    def _():
        g = acc[...].astype(LOW)
        gath[...] = g
        pre = nn(g, wat[...])
        sa = sigma(pre)
        aslope[...] = HALF_ROOT * slope_of(pre, sa)
        anew[...] = ((atom[...].astype(WIDE) + pre * sa) * HALF_ROOT).astype(LOW)


def out_body(
    merged, radial, trow, anew, cot, wc, wro, wout, ocot, acot, aslope, gath, wat,
    enew, gmer, aout, gatom, gw2, *rest, parts, peers, inside,
):
    outs, (ogat, seg, both, awc, aro, aoa) = rest[:-6], rest[-6:]
    step = pl.program_id(0)
    atoms, wide = ogat.shape
    aw = anew.shape[1]

    @pl.when(step == 0)
    def _():
        both[:, 0:wide] = split_pair(nt(ocot[...], wout[...]))
        both[:, wide : 2 * wide] = split_pair(nn(anew[...], wc[0:aw, :]))
        ogat[...] = jnp.zeros_like(ogat)
        seg[...] = jnp.zeros_like(seg)
        awc[...] = jnp.zeros_like(awc)
        aro[...] = jnp.zeros_like(aro)

    hot_t = (lax.broadcasted_iota(jnp.int32, (atoms, TILE), 0) == trow[...]).astype(LOW)
    spread = tn(jnp.concatenate([hot_t, hot_t], axis=0), both[...])
    gow = spread[:, 0:wide]
    m = merged[...]
    ml = m.astype(LOW)
    wcm = wc[aw:, :]
    pre = spread[:, wide:] + nn(ml, wcm)
    s = sigma(pre)
    new = (m + pre * s) * HALF_ROOT
    enew[...] = new.astype(LOW)
    rout = nn(radial[...], wro[...])
    ogat[...] += nn(hot_t, (new * rout).astype(LOW))
    gnew = cot[...].astype(WIDE) + gow * rout
    aro[...] += tn(radial[...], (gow * new).astype(LOW))
    lc = (gnew * (HALF_ROOT * slope_of(pre, s))).astype(LOW)
    awc[aw:, :] += tn(ml, lc)
    seg[...] += nn(hot_t, lc)
    gmer[...] = gnew * HALF_ROOT + nt(lc, wcm)

    @pl.when(step == pl.num_programs(0) - 1)
    def _():
        ol = ogat[...].astype(LOW)
        aout[...] = nn(ol, wout[...]).astype(LOW)
        aoa[:, 0:aw] = tn(ol, ocot[...])
        pair = split_pair(seg[...])
        hi = pair[0:atoms, :]
        lo = pair[atoms:, :]
        awc[0:aw, :] = tn(anew[...], hi) + tn(anew[...], lo)
        wca = wc[0:aw, :]
        ga = acot[...].astype(WIDE) + nt(hi, wca) + nt(lo, wca)
        gatom[...] = (ga * HALF_ROOT).astype(LOW)
        la = (ga * aslope[...]).astype(LOW)
        aoa[:, aw : 2 * aw] = tn(gath[...], la)
        gw2[...] = split_pair(nt(la, wat[...]))
        emit(outs, parts, (awc, aoa, aro), peers, inside)


def back_body(
    edge, radial, trow, s3, s4, merged, gmer, gw2, p3, p4, mixlow, reshid, dsk, du3, du4, dr1, dr2,
    wu3, wu4, wsk, wr1, wr2, wra, *rest, parts, peers, inside,
):
    if inside:
        before, rest = rest[:2], rest[2:]
    (gm_out, ls_out, lb3, lb4), outs = rest[:4], rest[4:-6]
    ask, ar1, ar2, ara, aup, abil = rest[-6:]
    step = pl.program_id(0)
    pair = gw2.shape[0]
    n3 = wu3.shape[0]

    @pl.when(step == 0)
    def _():
        ask[...] = jnp.zeros_like(ask)
        ar1[...] = jnp.zeros_like(ar1)
        ar2[...] = jnp.zeros_like(ar2)
        ara[...] = jnp.zeros_like(ara)
        aup[...] = jnp.zeros_like(aup)
        abil[...] = jnp.zeros_like(abil)

    hot_t = (lax.broadcasted_iota(jnp.int32, (pair // 2, TILE), 0) == trow[...]).astype(LOW)
    gw = tn(jnp.concatenate([hot_t, hot_t], axis=0), gw2[...])
    gm = gmer[...] + gw * nn(radial[...], wra[...])
    ara[...] += tn(radial[...], (gw * merged[...]).astype(LOW))
    l2 = (gm * dr2[...].astype(WIDE)).astype(LOW)
    ar2[...] += tn(reshid[...], l2)
    l1 = (nt(l2, wr2[...]) * dr1[...].astype(WIDE)).astype(LOW)
    ar1[...] += tn(mixlow[...], l1)
    gmix = (gm * 0.5 + nt(l1, wr1[...])) * THIRD_ROOT
    ls = (gmix * dsk[...].astype(WIDE)).astype(LOW)
    l3 = (gmix * du3[...].astype(WIDE)).astype(LOW)
    l4 = (gmix * du4[...].astype(WIDE)).astype(LOW)
    ask[...] += tn(edge[...], ls)
    gm_out[...] = gm * HALF_ROOT
    ls_out[...] = ls
    v3 = p3[...]
    g3 = sigma(v3)
    v4 = p4[...]
    g4 = sigma(v4)
    aup[0:n3, :] += nn((v3 * g3).astype(LOW), l3)
    aup[n3:, :] += nn((v4 * g4).astype(LOW), l4)
    low3 = (nt(wu3[...], l3) * slope_of(v3, g3)).astype(LOW)
    low4 = (nt(wu4[...], l4) * slope_of(v4, g4)).astype(LOW)
    lb3[...] = low3
    lb4[...] = low4
    abil[0:n3, :] += nt(low3, s3[...])
    abil[n3:, :] += nt(low4, s4[...])

    @pl.when(step == pl.num_programs(0) - 1)
    def _():
        values = (ask, ar1, ar2, ara, aup, abil)
        if inside:
            first = before[0].shape[2]
            for out, past in zip(outs, before):
                out[:, :, 0:first, :] = past[...]
            emit(outs, parts, values, peers, inside, first)
        else:
            emit(outs, parts, values, peers, inside)


def unweigh(coef, dsum, index, mask, spread, hots, group, basis, width):
    slabs = spread.shape[0] // width
    for k in range(group * GROUP, (group + 1) * GROUP):
        low_part = (index[k : k + 1, :] & (TILE - 1)).astype(WIDE).astype(LOW)
        hots[:, k * TILE : (k + 1) * TILE] = hot_of(low_part)
    acc = [None] * GROUP
    for c in range(basis):
        d = dsum[c * width : (c + 1) * width, :]
        for j in range(GROUP):
            row = (group * GROUP + j) * basis + c
            term = jnp.broadcast_to(coef[row : row + 1, :], d.shape).astype(LOW) * d
            acc[j] = term if acc[j] is None else acc[j] + term
    for j in range(GROUP):
        k = group * GROUP + j
        got = chosen(index[k : k + 1, :], mask[k : k + 1, :]) >> 8
        slab = jnp.broadcast_to(got.astype(WIDE), (width, TILE)).astype(LOW)
        for s in range(slabs):
            spread[s * width : (s + 1) * width, k * TILE : (k + 1) * TILE] = jnp.where(
                slab == s, acc[j], jnp.zeros((), LOW)
            )


def scatter_body(lb, idx, mask, basis, wt, grad, far, acc, coef, dsum, spread, hots, w, *, edges):
    step = pl.program_id(0)
    n = wt.shape[0]
    slots = idx.shape[0]

    @pl.when(step == 0)
    def _():
        acc[...] = jnp.zeros_like(acc)
        w[...] = wt[...].astype(WIDE).T.astype(LOW)

    coef[...] = basis[...].astype(WIDE).T
    dsum[...] = nn(w[...], lb[...]).astype(LOW)
    for group in range(slots // GROUP):
        part = slice(group * GROUP * TILE, (group + 1) * GROUP * TILE)
        unweigh(coef, dsum, idx, mask, spread, hots, group, coef.shape[0] // slots, n)
        acc[...] += nt(spread[:, part], hots[:, part])

    @pl.when(step == pl.num_programs(0) - 1)
    def _():
        local = edges // TILE
        for s in range(local):
            grad[:, s * TILE : (s + 1) * TILE] = acc[s * n : (s + 1) * n, :]
        for s in range(local, acc.shape[0] // n):
            filler = jnp.zeros((LANES - n, TILE), WIDE)
            part = jnp.concatenate([acc[s * n : (s + 1) * n, :], filler], axis=0).T.astype(LOW)
            at = (s - local) * TILE
            size = min(TILE, far.shape[0] - at)
            far[at : at + size, :] = part[0:size, :]


def source_back_body(edge, radial, grad, down, ret, asked, ws, wr, wd, *rest, low, parts, peers, inside, after):
    if inside and after:
        before, rest = rest[:2], rest[2:]
    low_out, outs, (asum, arad, adn, rt) = rest[0], rest[1:-4], rest[-4:]
    step = pl.program_id(0)
    n = grad.shape[0]

    @pl.when(step == 0)
    def _():
        rt[...] = ret[...].astype(WIDE).T.astype(LOW)
        asum[...] = jnp.zeros_like(asum)
        arad[...] = jnp.zeros_like(arad)
        adn[...] = jnp.zeros_like(adn)

    place = lax.broadcasted_iota(jnp.int32, (TILE, asked.shape[1]), 0) + step * TILE
    back = nt(rt[0:n, :], (place == asked[...]).astype(LOW))
    v = down[low : low + n, :]
    ld = (grad[...] + back) * slope_of(v, sigma(v))
    ldt = ld.astype(LOW)
    low_rows = ld.T.astype(LOW)
    e = edge[...]
    r = radial[...]
    pre = nn(e, ws[...])
    rad = nn(r, wr[...])
    s = sigma(pre)
    act = pre * s
    adn[...] += nn(ldt, (act * rad).astype(LOW))
    gm = nn(low_rows, wd[...])
    lo = (gm * rad * slope_of(pre, s)).astype(LOW)
    low_out[...] = lo
    arad[...] += tn(r, (gm * act).astype(LOW))
    asum[...] += tn(e, lo)

    @pl.when(step == pl.num_programs(0) - 1)
    def _():
        if inside and after:
            first = before[0].shape[2]
            for out, past in zip(outs, before):
                out[:, :, 0:first, :] = past[...]
            emit(outs, parts, (asum, arad, adn), peers, inside, first)
        else:
            emit(outs, parts, (asum, arad, adn), peers, inside)


def edge_grad_body(gm, ls, l3, l4, wsk, ws3, ws4, gedge):
    total = gm[...] + nt(ls[...], wsk[...]) + nt(l3[...], ws3[...]) + nt(l4[...], ws4[...])
    gedge[...] = total.astype(LOW)


def swap(v, axis, mask):
    count = lax.axis_size(axis)
    return lax.ppermute(v, axis, [(j, j ^ mask) for j in range(count)])


def summed(v, axis, shift):
    total = v[0].astype(WIDE)
    for m in range(1, v.shape[0]):
        total = total + swap(v[m], axis, m << shift).astype(WIDE)
    return total.astype(LOW)


def core_sum(send, keep):
    return (keep.astype(WIDE) + swap(send, "edge", 1).astype(WIDE)).astype(LOW)


def group_sum(v):
    return summed(v, "grp", 0)


def share_sum(v):
    at = 1
    while v.shape[0] > 1:
        width = min(4, v.shape[0])
        v = v.reshape(v.shape[0] // width, width, *v.shape[1:])
        v = summed(jnp.moveaxis(v, 1, 0), "edge", at)
        at += width.bit_length() - 1
    return v[0]


def group_gather(v):
    return (v,) + tuple(swap(v, "grp", m) for m in range(1, PARTS))


def exchange(v, peers):
    parts = v.reshape(peers, v.shape[0] // peers, v.shape[1])
    return lax.all_to_all(parts, "edge", split_axis=0, concat_axis=0, tiled=True).reshape(v.shape)


def per_device(
    edge_embed, atom_embed, radial_basis, triplet_basis, quadruplet_basis,
    triplet_source_row, triplet_mask, quadruplet_source_row, quadruplet_mask,
    edge_target_atom, borrowed_edges,
    w_source_trip, w_rbf_trip, w_down_trip, w_source_quad, w_rbf_quad, w_down_quad,
    triplet_bilinear_weight, w_up_trip, w_bilinear_quad, w_up_quad, w_skip,
    w_res_first, w_res_second, w_rbf_atom, w_atom, w_concat, w_rbf_out, w_out,
    edge_cotangent, atom_cotangent, output_cotangent,
):
    edges, wide = edge_embed.shape
    atoms, aw = atom_embed.shape
    rbf = radial_basis.shape[1]
    peers = lax.axis_size("edge")
    cap = borrowed_edges.shape[2]
    steps = edges // TILE
    n3, n4 = w_down_trip.shape[1], w_down_quad.shape[1]
    nb = n3 + n4
    k3, k4 = triplet_mask.shape[1], quadruplet_mask.shape[1]
    f3, f4 = triplet_bilinear_weight.shape[0], w_bilinear_quad.shape[0]
    q3, q4 = triplet_basis.shape[1], quadruplet_basis.shape[1]
    ghosts = peers * cap
    ghosts_up = -(-ghosts // TILE) * TILE
    slabs = (edges + ghosts_up) // TILE

    inside = fits(peers, rbf)
    far_ids = lax.all_to_all(borrowed_edges[0], "edge", split_axis=0, concat_axis=0, tiled=True)

    i3, m3 = triplet_source_row.T, triplet_mask.T
    i4, m4 = quadruplet_source_row.T, quadruplet_mask.T
    wd3, wd4 = w_down_trip.T, w_down_quad.T
    wb3, wb4 = triplet_bilinear_weight.T, w_bilinear_quad.T
    trow = edge_target_atom
    sources = (w_source_trip, w_rbf_trip, wd3, w_source_quad, w_rbf_quad, wd4)

    table, down = call(
        source_body, "source_rows", steps, 10, (edge_embed, radial_basis) + sources,
        [rows(wide), rows(rbf)] + [whole(w) for w in sources],
        [((nb, edges), LOW), ((nb, edges), WIDE)], [cols(nb), cols(nb)], [],
    )
    table, far_ids = lax.optimization_barrier((table, far_ids))
    sent, asked = call(
        sent_body, "sent_rows", 1, 2, (table, far_ids), [whole(table), whole(far_ids)],
        [((ghosts, LANES), LOW), ((1, ghosts), jnp.int32)], [fixed(ghosts, LANES), fixed(1, ghosts)], [],
    )
    ghost = exchange(sent, peers)

    s3, s4, p3, p4 = call(
        gather_body, "gather_sums", steps, 25,
        (table, ghost, i3, m3, i4, m4, triplet_basis, quadruplet_basis, wb3, wb4),
        [whole(table), whole(ghost), cols(k3), cols(k3), cols(k4), cols(k4), rows(q3), rows(q4),
         whole(wb3), whole(wb4)],
        [((f3, edges), LOW), ((f4, edges), LOW), ((n3, edges), WIDE), ((n4, edges), WIDE)],
        [cols(f3), cols(f4), cols(n3), cols(n4)],
        [
            pltpu.VMEM((slabs * n3, TILE), LOW), pltpu.VMEM((slabs * n4, TILE), LOW),
            pltpu.VMEM((k3, n3, TILE), LOW), pltpu.VMEM((k4, n4, TILE), LOW),
            pltpu.VMEM((q3, TILE), WIDE), pltpu.VMEM((q4, TILE), WIDE),
        ],
    )

    act = ((edges, wide), LOW)
    ups = (w_up_trip, w_up_quad, w_skip, w_res_first, w_res_second, w_rbf_atom)
    merged, mixlow, reshid, dsk, du3, du4, dr1, dr2, gath, anew, aslope = call(
        mix_body, "edge_update", steps, 19,
        (edge_embed, radial_basis, p3, p4, trow) + ups + (w_atom, atom_embed),
        [rows(wide), rows(rbf), cols(n3), cols(n4), cols(1)] + [whole(w) for w in ups + (w_atom, atom_embed)],
        [((edges, wide), WIDE), act, act, act, act, act, act, act,
         ((atoms, wide), LOW), ((atoms, aw), LOW), ((atoms, aw), WIDE)],
        [rows(wide)] * 8 + [fixed(atoms, wide), fixed(atoms, aw), fixed(atoms, aw)],
        [pltpu.VMEM((atoms, wide), WIDE)],
    )

    first_parts = (("rows", w_concat.shape), ("rows", (wide, 2 * aw)), ("rows", w_rbf_out.shape))
    outs = (w_concat, w_rbf_out, w_out, output_cotangent, atom_cotangent, aslope, gath, w_atom)
    shapes, specs = grad_outs(first_parts, peers, inside)
    enew, gmer, aout, gatom, gw2, *first = call(
        functools.partial(out_body, parts=first_parts, peers=peers, inside=inside), "output_block", steps, 16,
        (merged, radial_basis, trow, anew, edge_cotangent) + outs,
        [rows(wide), rows(rbf), cols(1), whole(anew), rows(wide)] + [whole(w) for w in outs],
        [act, ((edges, wide), WIDE), ((atoms, aw), LOW), ((atoms, aw), LOW), ((2 * atoms, wide), LOW)] + shapes,
        [rows(wide), rows(wide), fixed(atoms, aw), fixed(atoms, aw), fixed(2 * atoms, wide)] + specs,
        [
            pltpu.VMEM((atoms, wide), WIDE), pltpu.VMEM((atoms, wide), WIDE),
            pltpu.VMEM((2 * atoms, 2 * wide), LOW),
            pltpu.VMEM(w_concat.shape, WIDE), pltpu.VMEM(w_rbf_out.shape, WIDE), pltpu.VMEM((wide, 2 * aw), WIDE),
        ],
    )

    square = w_skip.shape
    second_parts = (
        ("rows", square), ("rows", square), ("rows", square), ("rows", w_rbf_atom.shape),
        ("cols", (nb, wide)), ("cols", (nb, f3)),
    )
    if inside:
        shapes, specs = grad_outs(first_parts + second_parts, peers, inside)
    else:
        shapes, specs = grad_outs(second_parts, peers, inside)
    more = tuple(first) if inside else ()
    gmh, ls, lb3, lb4, *grads = call(
        functools.partial(back_body, parts=second_parts, peers=peers, inside=inside), "edge_update_back", steps, 24,
        (edge_embed, radial_basis, trow, s3, s4, merged, gmer, gw2, p3, p4, mixlow, reshid, dsk,
         du3, du4, dr1, dr2) + ups + more,
        [rows(wide), rows(rbf), cols(1), cols(f3), cols(f4), rows(wide), rows(wide), whole(gw2),
         cols(n3), cols(n4)] + [rows(wide)] * 7 + [whole(w) for w in ups + more],
        [((edges, wide), WIDE), act, ((n3, edges), LOW), ((n4, edges), LOW)] + shapes,
        [rows(wide), rows(wide), cols(n3), cols(n4)] + specs,
        [pltpu.VMEM(square, WIDE)] * 3
        + [pltpu.VMEM(w_rbf_atom.shape, WIDE), pltpu.VMEM((nb, wide), WIDE), pltpu.VMEM((nb, f3), WIDE)],
    )
    early_parts = first_parts + second_parts
    early = core_sum(*(grads if inside else pack(early_parts, tuple(first) + tuple(grads), peers)))

    def scatter(lb, idx, mask, basis, wt, name, micros):
        n, slots, q, f = wt.shape[0], idx.shape[0], basis.shape[1], wt.shape[1]
        return call(
            functools.partial(scatter_body, edges=edges), name, steps, micros, (lb, idx, mask, basis, wt),
            [cols(n), cols(slots), cols(slots), rows(q), whole(wt)],
            [((n, edges), WIDE), ((ghosts, LANES), LOW)],
            [fixed(n, edges), fixed(ghosts, LANES)],
            [
                pltpu.VMEM((slabs * n, TILE), WIDE), pltpu.VMEM((q, TILE), WIDE), pltpu.VMEM((f, TILE), LOW),
                pltpu.VMEM((slabs * n, slots * TILE), LOW), pltpu.VMEM((TILE, slots * TILE), LOW),
                pltpu.VMEM((f, n), LOW),
            ],
        )

    third_parts = (("rows", square), ("rows", w_rbf_trip.shape))
    quad_parts = third_parts + (("cols", (n4, wide)),)
    trip_parts = third_parts + (("cols", (n3, wide)),)

    def source_back(grad, ret, ws, wr, wd, low, parts, before, name):
        n = wd.shape[0]
        whole_parts = (quad_parts if before else ()) + parts
        shapes, specs = grad_outs(whole_parts if inside else parts, peers, inside)
        more = tuple(before) if inside else ()
        body = functools.partial(
            source_back_body, low=low, parts=parts, peers=peers, inside=inside, after=bool(before)
        )
        ins = (ret, asked, ws, wr, wd) + more
        low_rows, *grads = call(
            body, name, steps, 11, (edge_embed, radial_basis, grad, down) + ins,
            [rows(wide), rows(rbf), cols(n), cols(nb)] + [whole(x) for x in ins],
            [act] + shapes, [rows(wide)] + specs,
            [pltpu.VMEM(square, WIDE), pltpu.VMEM(w_rbf_trip.shape, WIDE), pltpu.VMEM((n, wide), WIDE),
             pltpu.VMEM((LANES, ghosts), LOW)],
        )
        return low_rows, grads

    grad4, far4 = scatter(lb4, i4, m4, quadruplet_basis, wb4, "scatter_quad", 11)
    lb3, far4, early = lax.optimization_barrier((lb3, far4, early))
    early = group_sum(early)
    ret4 = exchange(far4, peers)
    grad3, far3 = scatter(lb3, i3, m3, triplet_basis, wb3, "scatter_trip", 18)
    ret4, far3, early = lax.optimization_barrier((ret4, far3, early))
    ret3 = exchange(far3, peers)
    early = share_sum(early)
    l4, quads = source_back(grad4, ret4, w_source_quad, w_rbf_quad, wd4, n3, quad_parts, (), "source_back_quad")
    ret3, quads, early = lax.optimization_barrier((ret3, quads, early))
    early = group_gather(early)
    l3, trips = source_back(grad3, ret3, w_source_trip, w_rbf_trip, wd3, 0, trip_parts, quads, "source_back_trip")
    late_parts = quad_parts + trip_parts
    late = trips if inside else pack(late_parts, tuple(quads) + tuple(trips), peers)
    late, gmh, early = lax.optimization_barrier((late, gmh, early))
    late = core_sum(*late)
    last = (w_skip, w_source_trip, w_source_quad)
    (gedge,) = call(
        edge_grad_body, "edge_grad", steps // 2, 6, (gmh, ls, l3, l4) + last,
        [rows(wide, 2 * TILE)] * 4 + [whole(w) for w in last], [act], [rows(wide, 2 * TILE)], [],
    )
    late, gedge = lax.optimization_barrier((late, gedge))
    late = group_gather(share_sum(group_sum(late)))

    turned = tuple(("turned", shape) if kind == "cols" else (kind, shape) for kind, shape in trip_parts)
    r_concat, r_oa, r_out, r_sk, r_r1, r_r2, r_ra, r_up, r_bil = assemble(early, early_parts, peers, "assemble_early")
    r_s4, r_r4, r_d4, r_s3, r_r3, r_d3 = assemble(late, quad_parts + turned, peers, "assemble_late")
    return (
        enew, anew, aout, gedge, gatom,
        r_s3, r_r3, r_d3, r_s4, r_r4, r_d4.T,
        r_bil[0:n3].T, r_up[0:n3], r_bil[n3:].T, r_up[n3:],
        r_sk, r_r1, r_r2, r_ra, r_oa[:, aw:], r_concat, r_out, r_oa[:, 0:aw],
    )


def solution(mesh):
    both = P(("grp", "edge"), None)
    placed = (both,) * 10 + (P(("grp", "edge"), None, None),) + (P(),) * 18 + (both,) * 3
    shares = [P("edge", None)] * 18
    shares[7] = P(None, "edge")
    shares[9] = P(None, "edge")
    return jax.shard_map(
        per_device, mesh=mesh, in_specs=placed, out_specs=(both,) * 5 + tuple(shares), check_vma=False
    )
```

time: 254 us -> 241 us (0.949)
  Pallas kernels: 143 us -> 160 us
  starting transfers between devices: 48.9 us -> 37.6 us
  local copies, waits for them, and re-layouts: 18.4 us -> 7.24 us
  blocking collectives: 0 us -> 10.9 us
  waiting for transfers between devices: 29.1 us -> 18.3 us
  other arithmetic: 12 us -> 4.2 us
    pallas_call x8 -> x13, Pallas kernels: 143 us -> 160 us  [call(): pl.pallas_call(body, name=name, out_shape=[jax.ShapeDtypeStruct(s, t) for...]
    ppermute x30 -> x20, starting transfers between devices: 34.8 us -> 23.2 us  [swap(): return lax.ppermute(v, axis, [(j, j ^ mask) for j in range(count)])]
    all_to_all x0 -> x1, blocking collectives: none -> 10.9 us  [exchange(): lax.all_to_all(parts, 'edge', split_axis=0, concat_axis=0, tiled=True)]
    all_to_all x2, waiting for transfers between devices: 8.83 us -> 0.01 us  [exchange(): lax.all_to_all(parts, 'edge', split_axis=0, concat_axis=0, tiled=True)]
    unnamed x42 -> x32, local copies, waits for them, and re-layouts: 8.67 us -> 3.18 us
    another operation x13 -> x0, local copies, waits for them, and re-layouts: 5.37 us -> none  [the longest x11 5.32 us: by_rows(): jnp.stack([parts[:, :, q:q + 128] for q in range(0, g.shape[1], 128)], ax...]
    concatenate x8 -> x0, other arithmetic: 4.86 us -> none  [the longest x7 4.71 us: wide_rows(): jnp.concatenate([g[q, start:stop] for q in range(g.shape[0])], axis=1)]
    ppermute x30 -> x20, waiting for transfers between devices: 19.5 us -> 18.3 us  [swap(): return lax.ppermute(v, axis, [(j, j ^ mask) for j in range(count)])]
  transfers between devices with their start and end apart: 33 -> 23, of which waited for: 13 -> 9; matrix products, arithmetic and copies ran while one was open for 7% -> 2% of each run, Pallas kernels for 19% -> 30%
where the time goes in v4:
time: 241 us; the launch traced here: 239 us
  Pallas kernels  160 us (66%)
  starting transfers between devices  37.6 us (16%)
  waiting for transfers between devices  18.3 us (8%)
  blocking collectives  10.9 us (5%)
  local copies, waits for them, and re-layouts  7.24 us (3%)
  other arithmetic  4.2 us (2%)
    pallas_call x13, Pallas kernels, call(): pl.pallas_call(body, name=name, out_shape=[jax.ShapeDtypeStruct(s, t) for...  160 us
    ppermute x20, starting transfers between devices, swap(): return lax.ppermute(v, axis, [(j, j ^ mask) for j in range(count)])  23.2 us
    ppermute x20, waiting for transfers between devices, swap(): return lax.ppermute(v, axis, [(j, j ^ mask) for j in range(count)])  18.3 us
    all_to_all x1, blocking collectives, exchange(): lax.all_to_all(parts, 'edge', split_axis=0, concat_axis=0, tiled=True)  10.9 us
    all_to_all x2, starting transfers between devices, exchange(): lax.all_to_all(parts, 'edge', split_axis=0, concat_axis=0, tiled=True)  8.08 us
    all_to_all x1, starting transfers between devices, per_device(): lax.all_to_all(borrowed_edges[0], 'edge', split_axis=0, concat_axis=0, ti...  6.37 us
  transfers between devices with their start and end apart: 23, of which 9 were waited for; matrix products, arithmetic and copies ran while one was open for 2% of the time, Pallas kernels for 30%

profile of v4, /device:TPU:0, one launch (start us, length us, event | category | flops | bytes accessed | tf_op | source)
XLA Modules:
  0.0 239.3 jit_solution(16927882128457927938)
XLA Ops:
  0.7 6.4 %all-to-all-start = ((s32[8,1,16]{2,1,0:T(1,128)}), s32[8,1,16]{2,1,0:T(1,128)S(1)}, u32[]{:S(2)}, u32[]{:S(2)}) async-start(s32[8,1,16]{2,1,0:T(1,128)} %bitcast.49), calls=%async_computation | async-start | bytes 8192 | tf_op jit(solution)/shard_map/all_to_all | solution.py:635
  7.0 9.8 %source_rows.1 = (bf16[96,2048]{1,0:T(8,128)(2,1)}, f32[96,2048]{1,0:T(8,128)}) custom-call(bf16[2048,512]{1,0:T(8,128)(2,1)} %edge.9, bf16[2048,128]{1,0:T(8,128)(2,1)} %radial.11, bf16[512,512]{1,0:T(8,128)(2,1)} %ws3.3, bf16[128,512]{1,0:T(8,128)(2,1)} %wr.3, bf16[64,512]{1,0:T(8,128)(2,1)} %bitcast.63, bf16[512,512]{1,0:T(8,128)(2,1)} %ws4.3, ...), custom_call_target="tpu_custom_call" | custom-call | flops 11000000512 | bytes 4194304 | tf_op jit(solution)/shard_map/source_rows/pallas_call | solution.py:66
  16.8 0.6 copy-done.9
  17.4 2.0 sent_rows.1
  19.4 10.9 %all_to_all.27 = bf16[8,16,128]{2,1,0:T(8,128)(2,1)} all-to-all(bf16[8,16,128]{2,1,0:T(8,128)(2,1)} %bitcast.48), channel_id=1, replica_groups=mesh['grp'=4,'edge'=8] {'edge'}, dimensions={0} | all-to-all | bytes 65536 | tf_op jit(solution)/shard_map/all_to_all | solution.py:607
  30.4 25.1 %gather_sums.1 = (bf16[1024,2048]{1,0:T(8,128)(2,1)}, bf16[1024,2048]{1,0:T(8,128)(2,1)}, f32[64,2048]{1,0:T(8,128)}, f32[32,2048]{1,0:T(8,128)}) custom-call(bf16[96,2048]{1,0:T(8,128)(2,1)} %get-tuple-element.102.table.tab, bf16[128,128]{1,0:T(8,128)(2,1)} %bitcast.47, s32[16,2048]{1,0:T(8,128)} %bitcast.51, s32[16,2048]{1,0:T(8,128)} %bitcast.53, ...), custom_call_target="tpu_custom_call" | custom-call | flops 27499999232 | bytes 4194304 | tf_op jit(solution)/shard_map/gather_sums/pallas_call | solution.py:66
  55.5 18.9 %edge_update.1 = (f32[2048,512]{1,0:T(8,128)}, bf16[2048,512]{1,0:T(8,128)(2,1)}, bf16[2048,512]{1,0:T(8,128)(2,1)}, bf16[2048,512]{1,0:T(8,128)(2,1)}, bf16[204...) custom-call(bf16[2048,512]{1,0:T(8,128)(2,1)} %edge.9, ...), custom_call_target="tpu_custom_call" | custom-call | flops 20899999744 | bytes 4194304 | tf_op jit(solution)/shard_map/edge_update/pallas_call | solution.py:66
  74.4 16.0 %output_block.1 = (bf16[2048,512]{1,0:T(8,128)(2,1)}, f32[2048,512]{1,0:T(8,128)}, bf16[128,256]{1,0:T(8,128)(2,1)}, bf16[128,256]{1,0:T(8,128)(2,1)}, bf16[256,...) custom-call(f32[2048,512]{1,0:T(8,128)} %get-tuple-element.107.merged, ...), custom_call_target="tpu_custom_call" | custom-call | flops 17600000000 | bytes 4194304 | tf_op jit(solution)/shard_map/output_block/pallas_call | solution.py:66
  90.5 25.1 %edge_update_back.1 = (f32[2048,512]{1,0:T(8,128)}, bf16[2048,512]{1,0:T(8,128)(2,1)}, bf16[64,2048]{1,0:T(8,128)(2,1)}, bf16[32,2048]{1,0:T(8,128)(2,1)}, bf16[...) custom-call(bf16[2048,512]{1,0:T(8,128)(2,1)} %edge.9, bf16[2048,128]{1,0:T(8,128)(2,1)} %radial.11, ...), custom_call_target="tpu_custom_call" | custom-call | flops 26400000000 | bytes 4194304 | tf_op jit(solution)/shard_map/edge_update_back/pallas_call | solution.py:66
  115.7 10.9 %scatter_quad.1 = (f32[32,2048]{1,0:T(8,128)}, bf16[128,128]{1,0:T(8,128)(2,1)}) custom-call(bf16[32,2048]{1,0:T(8,128)(2,1)} %get-tuple-element.127.lb, s32[8,2048]{1,0:T(8,128)} %bitcast.58, s32[8,2048]{1,0:T(8,128)} %bitcast.60, bf16[2048,256]{1,0:T(8,128)(2,1)} %basis.2, bf16[32,1024]{1,0:T(8,128)(2,1)} %bitcast.62), custom_call_target="tpu_custom_call" | custom-call | flops 12099999744 | bytes 4194304 | tf_op jit(solution)/shard_map/scatter_quad/pallas_call | solution.py:66
  126.6 1.2 copy-done
  127.8 2.5 %add_convert_fusion = bf16[4,4,448,128]{3,2,1,0:T(8,128)(2,1)S(1)} fusion(bf16[4,4,448,128]{3,2,1,0:T(8,128)(2,1)} %copy-done, bf16[4,4,448,128]{3,2,1,0:T(8,128)(2,1)} %get-tuple-element.129), kind=kLoop, calls=%fused_computation | loop fusion | flops 3670016 | bytes 5505024 | tf_op jit(solution)/shard_map/convert_element_type | solution.py:584
  130.3 3.5 %all-to-all-start.2 = ((bf16[8,16,128]{2,1,0:T(8,128)(2,1)}), bf16[8,16,128]{2,1,0:T(8,128)(2,1)S(1)}, u32[]{:S(2)}, u32[]{:S(2)}) async-start(bf16[8,16,128]{2,1,0:T(8,128)(2,1)} %bitcast.13), calls=%async_computation.2 | async-start | bytes 65536 | tf_op jit(solution)/shard_map/all_to_all | solution.py:607
  133.9 0.9 slice_bitcast_fusion.2
  134.7 1.5 collective-permute-start.1
  136.2 1.5 collective-permute-start.3
  138.2 17.7 %scatter_trip.1 = (f32[64,2048]{1,0:T(8,128)}, bf16[128,128]{1,0:T(8,128)(2,1)}) custom-call(bf16[64,2048]{1,0:T(8,128)(2,1)} %get-tuple-element.131.lb, s32[16,2048]{1,0:T(8,128)} %bitcast.52, s32[16,2048]{1,0:T(8,128)} %bitcast.54, bf16[2048,256]{1,0:T(8,128)(2,1)} %basis.3, bf16[64,1024]{1,0:T(8,128)(2,1)} %bitcast.56), custom_call_target="tpu_custom_call" | custom-call | flops 19800000512 | bytes 4194304 | tf_op jit(solution)/shard_map/scatter_trip/pallas_call | solution.py:66
  155.9 2.8 %collective-permute-done.3 = bf16[4,448,128]{2,1,0:T(8,128)(2,1)S(1)} collective-permute-done((bf16[4,448,128]{2,1,0:T(8,128)(2,1)S(1)}, bf16[4,448,128]{2,1,0:T(8,128)(2,1)S(1)}, u32[]{:S(2)}, u32[]{:S(2)}) %collective-permute-start.3) | collective-permute-done | bytes 458784 | tf_op jit(solution)/shard_map/ppermute | solution.py:573
  158.7 1.3 collective-permute-done.2
  160.0 1.3 fusion.2
  161.2 4.5 %all-to-all-start.3 = ((bf16[8,16,128]{2,1,0:T(8,128)(2,1)}), bf16[8,16,128]{2,1,0:T(8,128)(2,1)S(1)}, u32[]{:S(2)}, u32[]{:S(2)}) async-start(bf16[8,16,128]{2,1,0:T(8,128)(2,1)} %bitcast.19), calls=%async_computation.3 | async-start | bytes 65536 | tf_op jit(solution)/shard_map/all_to_all | solution.py:607
  165.8 2.1 collective-permute-start.4
  167.9 2.4 collective-permute-start.6
  170.3 10.9 %source_back_quad.1 = (bf16[2048,512]{1,0:T(8,128)(2,1)}, bf16[4,4,96,128]{3,2,1,0:T(8,128)(2,1)}, bf16[4,4,96,128]{3,2,1,0:T(8,128)(2,1)}) custom-call(bf16[2048,512]{1,0:T(8,128)(2,1)} %edge.9, bf16[2048,128]{1,0:T(8,128)(2,1)} %radial.11, f32[32,2048]{1,0:T(8,128)} %get-tuple-element.138.grad, f32[96,2048]{1,0:T(8,128)} %get-tuple-element.133.down, ...), custom_call_target="tpu_custom_call" | custom-call | flops 12099999744 | bytes 4194304 | tf_op jit(solution)/shard_map/source_back_quad/pallas_call | solution.py:66
  181.3 1.5 collective-permute-start.9
  182.8 1.5 collective-permute-start.8
  184.9 11.5 %source_back_trip.1 = (bf16[2048,512]{1,0:T(8,128)(2,1)}, bf16[4,4,192,128]{3,2,1,0:T(8,128)(2,1)}, bf16[4,4,192,128]{3,2,1,0:T(8,128)(2,1)}) custom-call(bf16[2048,512]{1,0:T(8,128)(2,1)} %edge.9, bf16[2048,128]{1,0:T(8,128)(2,1)} %radial.11, f32[64,2048]{1,0:T(8,128)} %get-tuple-element.132.grad, f32[96,2048]{1,0:T(8,128)} %get-tuple-element.133.down, ...), custom_call_target="tpu_custom_call" | custom-call | flops 12099999744 | bytes 4194304 | tf_op jit(solution)/shard_map/source_back_trip/pallas_call | solution.py:66
  197.1 2.0 assemble_early.1
  199.1 8.3 %edge_grad.1 = bf16[2048,512]{1,0:T(8,128)(2,1)} custom-call(f32[2048,512]{1,0:T(8,128)} %get-tuple-element.153.gm, bf16[2048,512]{1,0:T(8,128)(2,1)} %get-tuple-element.154.ls, bf16[2048,512]{1,0:T(8,128)(2,1)} %get-tuple-element.155.l3, bf16[2048,512]{1,0:T(8,128)(2,1)} %get-tuple-element.156.l4, bf16[512,512]{1,0:T(8,128)(2,1)} %wsk.5, ...), custom_call_target="tpu_custom_call" | custom-call | flops 6600000000 | bytes 4194304 | tf_op jit(solution)/shard_map/edge_grad/pallas_call | solution.py:66
  207.8 1.6 collective-permute-start.11
  209.8 1.5 collective-permute-start.12
  211.3 0.7 fusion.10
  212.0 3.6 %collective-permute-done.11 = bf16[4,192,128]{2,1,0:T(8,128)(2,1)S(1)} collective-permute-done((bf16[4,192,128]{2,1,0:T(8,128)(2,1)S(1)}, bf16[4,192,128]{2,1,0:T(8,128)(2,1)S(1)}, u32[]{:S(2)}, u32[]{:S(2)}) %collective-permute-start.11) | collective-permute-done | bytes 196640 | tf_op jit(solution)/shard_map/ppermute | solution.py:573
  215.6 3.2 %collective-permute-done.13 = bf16[4,192,128]{2,1,0:T(8,128)(2,1)S(1)} collective-permute-done((bf16[4,192,128]{2,1,0:T(8,128)(2,1)S(1)}, bf16[4,192,128]{2,1,0:T(8,128)(2,1)S(1)}, u32[]{:S(2)}, u32[]{:S(2)}) %collective-permute-start.13) | collective-permute-done | bytes 196640 | tf_op jit(solution)/shard_map/ppermute | solution.py:573
  218.8 1.4 collective-permute-done.12
  220.3 2.1 collective-permute-start.14
  222.4 2.4 collective-permute-start.16
  224.7 0.6 slice_bitcast_fusion.6
  225.4 2.9 %collective-permute-done.16 = bf16[1,192,128]{2,1,0:T(8,128)(2,1)S(1)} collective-permute-done((bf16[1,192,128]{2,1,0:T(8,128)(2,1)S(1)}, bf16[1,192,128]{2,1,0:T(8,128)(2,1)S(1)}, u32[]{:S(2)}, u32[]{:S(2)}) %collective-permute-start.16) | collective-permute-done | bytes 49184 | tf_op jit(solution)/shard_map/ppermute | solution.py:573
  228.3 1.5 collective-permute-done.15
  229.8 2.5 %collective-permute-start.19 = (bf16[192,128]{1,0:T(8,128)(2,1)S(1)}, bf16[192,128]{1,0:T(8,128)(2,1)S(1)}, u32[]{:S(2)}, u32[]{:S(2)}) collective-permute-start(bf16[192,128]{1,0:T(8,128)(2,1)S(1)} %fusion.7.refs_0_), channel_id=1, source_target_pairs={{0,24},{8,16},{16,8},{24,0},{1,25},{9,17},{17,9},{25,1},{2,26},{10... | collective-permute-start | bytes 147464 | tf_op jit(solution)/shard_map/ppermute | solution.py:573
  232.8 0.5 collective-permute-start.17
  233.3 0.6 slice_bitcast_fusion.7
  233.9 0.6 slice.93
  234.5 0.6 slice.91
  235.2 1.2 collective-permute-done.18.refs_2_
  237.0 0.6 copy-done.15
  237.6 1.6 assemble_late.1
  (59 shorter events, 3.9 us)
Async XLA Ops:
  0.7 16.1 %all-to-all-start = ((s32[8,1,16]{2,1,0:T(1,128)}), s32[8,1,16]{2,1,0:T(1,128)S(1)}, u32[]{:S(2)}, u32[]{:S(2)}) async-start(s32[8,1,16]{2,1,0:T(1,128)} %bitcast.49), calls=%async_computation | async-start | bytes 8192 | tf_op jit(solution)/shard_map/all_to_all | solution.py:635
  16.8 0.6 copy-start.9
  115.6 10.9 %collective-permute-start = (bf16[4,4,448,128]{3,2,1,0:T(8,128)(2,1)}, bf16[4,4,448,128]{3,2,1,0:T(8,128)(2,1)S(1)}, u32[]{:S(2)}, u32[]{:S(2)}) collective-permute-start(bf16[4,4,448,128]{3,2,1,0:T(8,128)(2,1)} %get-tuple-element.130), channel_id=1, source_target_pairs={{0,1},{1,0},{2,3},{3,2},{4,5},{5,4},{6,7},{7,6},{8,9},{9,8},{10,11... | collective-permute-start | bytes 5505032 | tf_op jit(solution)/shard_map/ppermute | solution.py:573
  126.6 1.2 copy-start
  130.3 30.9 %all-to-all-start.2 = ((bf16[8,16,128]{2,1,0:T(8,128)(2,1)}), bf16[8,16,128]{2,1,0:T(8,128)(2,1)S(1)}, u32[]{:S(2)}, u32[]{:S(2)}) async-start(bf16[8,16,128]{2,1,0:T(8,128)(2,1)} %bitcast.13), calls=%async_computation.2 | async-start | bytes 65536 | tf_op jit(solution)/shard_map/all_to_all | solution.py:607
  134.7 21.2 %collective-permute-start.1 = (bf16[4,448,128]{2,1,0:T(8,128)(2,1)}, bf16[4,448,128]{2,1,0:T(8,128)(2,1)S(1)}, u32[]{:S(2)}, u32[]{:S(2)}) collective-permute-start(bf16[4,448,128]{2,1,0:T(8,128)(2,1)} %get-tuple-element.179), channel_id=1, source_target_pairs={{0,8},{8,0},{16,24},{24,16},{1,9},{9,1},{17,25},{25,17},{2,10},{10... | collective-permute-start | bytes 1376264 | tf_op jit(solution)/shard_map/ppermute | solution.py:573
  136.2 22.5 %collective-permute-start.3 = (bf16[4,448,128]{2,1,0:T(8,128)(2,1)S(1)}, bf16[4,448,128]{2,1,0:T(8,128)(2,1)S(1)}, u32[]{:S(2)}, u32[]{:S(2)}) collective-permute-start(bf16[4,448,128]{2,1,0:T(8,128)(2,1)S(1)} %get-tuple-element.180), channel_id=1, source_target_pairs={{0,24},{8,16},{16,8},{24,0},{1,25},{9,17},{17,9},{25,1},{2,26},{10... | collective-permute-start | bytes 1376264 | tf_op jit(solution)/shard_map/ppermute | solution.py:573
  137.7 22.2 %collective-permute-start.2 = (bf16[4,448,128]{2,1,0:T(8,128)(2,1)S(1)}, bf16[4,448,128]{2,1,0:T(8,128)(2,1)}, u32[]{:S(2)}, u32[]{:S(2)}) collective-permute-start(bf16[4,448,128]{2,1,0:T(8,128)(2,1)S(1)} %get-tuple-element.181), channel_id=1, source_target_pairs={{0,16},{8,24},{16,0},{24,8},{1,17},{9,25},{17,1},{25,9},{2,18},{10... | collective-permute-start | bytes 1376264 | tf_op jit(solution)/shard_map/ppermute | solution.py:573
  161.2 9.0 %copy-start.7 = (bf16[8,16,128]{2,1,0:T(8,128)(2,1)}, bf16[8,16,128]{2,1,0:T(8,128)(2,1)S(1)}, u32[]{:S(2)}) copy-start(bf16[8,16,128]{2,1,0:T(8,128)(2,1)S(1)} %all-to-all-done.2) | copy-start | bytes 98308
  161.2 20.0 %all-to-all-start.3 = ((bf16[8,16,128]{2,1,0:T(8,128)(2,1)}), bf16[8,16,128]{2,1,0:T(8,128)(2,1)S(1)}, u32[]{:S(2)}, u32[]{:S(2)}) async-start(bf16[8,16,128]{2,1,0:T(8,128)(2,1)} %bitcast.19), calls=%async_computation.3 | async-start | bytes 65536 | tf_op jit(solution)/shard_map/all_to_all | solution.py:607
  165.8 15.4 %collective-permute-start.4 = (bf16[1,448,128]{2,1,0:T(8,128)(2,1)S(1)}, bf16[1,448,128]{2,1,0:T(8,128)(2,1)S(1)}, u32[]{:S(2)}, u32[]{:S(2)}) collective-permute-start(bf16[1,448,128]{2,1,0:T(8,128)(2,1)S(1)} %get-tuple-element.185), channel_id=1, source_target_pairs={{0,2},{1,3},{2,0},{3,1},{4,6},{5,7},{6,4},{7,5},{8,10},{9,11},{10,... | collective-permute-start | bytes 344072 | tf_op jit(solution)/shard_map/ppermute | solution.py:573
  167.9 13.3 %collective-permute-start.6 = (bf16[1,448,128]{2,1,0:T(8,128)(2,1)S(1)}, bf16[1,448,128]{2,1,0:T(8,128)(2,1)S(1)}, u32[]{:S(2)}, u32[]{:S(2)}) collective-permute-start(bf16[1,448,128]{2,1,0:T(8,128)(2,1)S(1)} %get-tuple-element.186), channel_id=1, source_target_pairs={{0,6},{1,7},{2,4},{3,5},{4,2},{5,3},{6,0},{7,1},{8,14},{9,15},{10,... | collective-permute-start | bytes 344072 | tf_op jit(solution)/shard_map/ppermute | solution.py:573
  170.3 10.9 %collective-permute-start.5 = (bf16[1,448,128]{2,1,0:T(8,128)(2,1)S(1)}, bf16[1,448,128]{2,1,0:T(8,128)(2,1)S(1)}, u32[]{:S(2)}, u32[]{:S(2)}) collective-permute-start(bf16[1,448,128]{2,1,0:T(8,128)(2,1)S(1)} %get-tuple-element.187), channel_id=1, source_target_pairs={{0,4},{1,5},{2,6},{3,7},{4,0},{5,1},{6,2},{7,3},{8,12},{9,13},{10,... | collective-permute-start | bytes 344072 | tf_op jit(solution)/shard_map/ppermute | solution.py:573
  181.3 15.1 %copy-start.3 = (bf16[448,128]{1,0:T(8,128)(2,1)}, bf16[448,128]{1,0:T(8,128)(2,1)S(1)}, u32[]{:S(2)}) copy-start(bf16[448,128]{1,0:T(8,128)(2,1)S(1)} %fusion.6.refs_0_) | copy-start | bytes 344068
  181.3 3.6 %copy-start.8 = (bf16[8,16,128]{2,1,0:T(8,128)(2,1)}, bf16[8,16,128]{2,1,0:T(8,128)(2,1)S(1)}, u32[]{:S(2)}) copy-start(bf16[8,16,128]{2,1,0:T(8,128)(2,1)S(1)} %all-to-all-done.3) | copy-start | bytes 98308
  181.3 15.1 %collective-permute-start.9 = (bf16[448,128]{1,0:T(8,128)(2,1)S(1)}, bf16[448,128]{1,0:T(8,128)(2,1)S(1)}, u32[]{:S(2)}, u32[]{:S(2)}) collective-permute-start(bf16[448,128]{1,0:T(8,128)(2,1)S(1)} %fusion.6.refs_0_), channel_id=1, source_target_pairs={{0,24},{8,16},{16,8},{24,0},{1,25},{9,17},{17,9},{25,1},{2,26},{10... | collective-permute-start | bytes 344072 | tf_op jit(solution)/shard_map/ppermute | solution.py:573
  182.8 13.6 %collective-permute-start.8 = (bf16[448,128]{1,0:T(8,128)(2,1)S(1)}, bf16[448,128]{1,0:T(8,128)(2,1)S(1)}, u32[]{:S(2)}, u32[]{:S(2)}) collective-permute-start(bf16[448,128]{1,0:T(8,128)(2,1)S(1)} %fusion.6.refs_0_), channel_id=1, source_target_pairs={{0,16},{8,24},{16,0},{24,8},{1,17},{9,25},{17,1},{25,9},{2,18},{10... | collective-permute-start | bytes 344072 | tf_op jit(solution)/shard_map/ppermute | solution.py:573
  184.3 12.1 %collective-permute-start.7 = (bf16[448,128]{1,0:T(8,128)(2,1)S(1)}, bf16[448,128]{1,0:T(8,128)(2,1)S(1)}, u32[]{:S(2)}, u32[]{:S(2)}) collective-permute-start(bf16[448,128]{1,0:T(8,128)(2,1)S(1)} %fusion.6.refs_0_), channel_id=1, source_target_pairs={{0,8},{8,0},{16,24},{24,16},{1,9},{9,1},{17,25},{25,17},{2,10},{10... | collective-permute-start | bytes 344072 | tf_op jit(solution)/shard_map/ppermute | solution.py:573
  196.4 0.6 copy-start.10
  196.4 0.7 copy-start.11
  196.5 0.7 copy-start.12
  196.5 11.0 %collective-permute-start.10 = (bf16[4,4,192,128]{3,2,1,0:T(8,128)(2,1)}, bf16[4,4,192,128]{3,2,1,0:T(8,128)(2,1)S(1)}, u32[]{:S(2)}, u32[]{:S(2)}) collective-permute-start(bf16[4,4,192,128]{3,2,1,0:T(8,128)(2,1)} %get-tuple-element.152), channel_id=1, source_target_pairs={{0,1},{1,0},{2,3},{3,2},{4,5},{5,4},{6,7},{7,6},{8,9},{9,8},{10,11... | collective-permute-start | bytes 2359304 | tf_op jit(solution)/shard_map/ppermute | solution.py:573
  199.1 8.3 %copy-start.1 = (bf16[4,4,192,128]{3,2,1,0:T(8,128)(2,1)S(1)}, bf16[4,4,192,128]{3,2,1,0:T(8,128)(2,1)}, u32[]{:S(2)}) copy-start(bf16[4,4,192,128]{3,2,1,0:T(8,128)(2,1)} %get-tuple-element.151) | copy-start | bytes 2359300
  207.4 3.9 %copy-start.2 = (f32[64,512]{1,0:T(8,128)S(1)}, f32[64,512]{1,0:T(8,128)}, u32[]{:S(2)}) copy-start(f32[64,512]{1,0:T(8,128)} %get-tuple-element.176) | copy-start | bytes 393220
  207.5 17.3 %copy-start.5 = (f32[96,128]{1,0:T(8,128)S(1)}, f32[96,128]{1,0:T(8,128)}, u32[]{:S(2)}) copy-start(f32[96,128]{1,0:T(8,128)} %get-tuple-element.170) | copy-start | bytes 147460
  207.7 26.2 %copy-start.4 = (f32[96,64]{1,0:T(8,128)S(1)}, f32[96,64]{1,0:T(8,128)}, u32[]{:S(2)}) copy-start(f32[96,64]{1,0:T(8,128)} %get-tuple-element.171) | copy-start | bytes 73732
  207.8 7.8 %collective-permute-start.11 = (bf16[4,192,128]{2,1,0:T(8,128)(2,1)S(1)}, bf16[4,192,128]{2,1,0:T(8,128)(2,1)S(1)}, u32[]{:S(2)}, u32[]{:S(2)}) collective-permute-start(bf16[4,192,128]{2,1,0:T(8,128)(2,1)S(1)} %get-tuple-element.182), channel_id=1, source_target_pairs={{0,8},{8,0},{16,24},{24,16},{1,9},{9,1},{17,25},{25,17},{2,10},{10... | collective-permute-start | bytes 589832 | tf_op jit(solution)/shard_map/ppermute | solution.py:573
  209.3 9.5 %collective-permute-start.13 = (bf16[4,192,128]{2,1,0:T(8,128)(2,1)S(1)}, bf16[4,192,128]{2,1,0:T(8,128)(2,1)S(1)}, u32[]{:S(2)}, u32[]{:S(2)}) collective-permute-start(bf16[4,192,128]{2,1,0:T(8,128)(2,1)S(1)} %get-tuple-element.183), channel_id=1, source_target_pairs={{0,24},{8,16},{16,8},{24,0},{1,25},{9,17},{17,9},{25,1},{2,26},{10... | collective-permute-start | bytes 589832 | tf_op jit(solution)/shard_map/ppermute | solution.py:573
  209.8 10.4 %collective-permute-start.12 = (bf16[4,192,128]{2,1,0:T(8,128)(2,1)S(1)}, bf16[4,192,128]{2,1,0:T(8,128)(2,1)S(1)}, u32[]{:S(2)}, u32[]{:S(2)}) collective-permute-start(bf16[4,192,128]{2,1,0:T(8,128)(2,1)S(1)} %get-tuple-element.184), channel_id=1, source_target_pairs={{0,16},{8,24},{16,0},{24,8},{1,17},{9,25},{17,1},{25,9},{2,18},{10... | collective-permute-start | bytes 589832 | tf_op jit(solution)/shard_map/ppermute | solution.py:573
  220.3 5.1 %collective-permute-start.14 = (bf16[1,192,128]{2,1,0:T(8,128)(2,1)S(1)}, bf16[1,192,128]{2,1,0:T(8,128)(2,1)S(1)}, u32[]{:S(2)}, u32[]{:S(2)}) collective-permute-start(bf16[1,192,128]{2,1,0:T(8,128)(2,1)S(1)} %get-tuple-element.188), channel_id=1, source_target_pairs={{0,2},{1,3},{2,0},{3,1},{4,6},{5,7},{6,4},{7,5},{8,10},{9,11},{10,... | collective-permute-start | bytes 147464 | tf_op jit(solution)/shard_map/ppermute | solution.py:573
  222.4 5.9 %collective-permute-start.16 = (bf16[1,192,128]{2,1,0:T(8,128)(2,1)S(1)}, bf16[1,192,128]{2,1,0:T(8,128)(2,1)S(1)}, u32[]{:S(2)}, u32[]{:S(2)}) collective-permute-start(bf16[1,192,128]{2,1,0:T(8,128)(2,1)S(1)} %get-tuple-element.189), channel_id=1, source_target_pairs={{0,6},{1,7},{2,4},{3,5},{4,2},{5,3},{6,0},{7,1},{8,14},{9,15},{10,... | collective-permute-start | bytes 147464 | tf_op jit(solution)/shard_map/ppermute | solution.py:573
  224.7 5.0 %collective-permute-start.15 = (bf16[1,192,128]{2,1,0:T(8,128)(2,1)S(1)}, bf16[1,192,128]{2,1,0:T(8,128)(2,1)S(1)}, u32[]{:S(2)}, u32[]{:S(2)}) collective-permute-start(bf16[1,192,128]{2,1,0:T(8,128)(2,1)S(1)} %get-tuple-element.190), channel_id=1, source_target_pairs={{0,4},{1,5},{2,6},{3,7},{4,0},{5,1},{6,2},{7,3},{8,12},{9,13},{10,... | collective-permute-start | bytes 147464 | tf_op jit(solution)/shard_map/ppermute | solution.py:573
  229.8 7.1 %copy-start.6 = (bf16[192,128]{1,0:T(8,128)(2,1)}, bf16[192,128]{1,0:T(8,128)(2,1)S(1)}, u32[]{:S(2)}) copy-start(bf16[192,128]{1,0:T(8,128)(2,1)S(1)} %fusion.7.refs_0_) | copy-start | bytes 147460
  229.8 5.4 %collective-permute-start.19 = (bf16[192,128]{1,0:T(8,128)(2,1)S(1)}, bf16[192,128]{1,0:T(8,128)(2,1)S(1)}, u32[]{:S(2)}, u32[]{:S(2)}) collective-permute-start(bf16[192,128]{1,0:T(8,128)(2,1)S(1)} %fusion.7.refs_0_), channel_id=1, source_target_pairs={{0,24},{8,16},{16,8},{24,0},{1,25},{9,17},{17,9},{25,1},{2,26},{10... | collective-permute-start | bytes 147464 | tf_op jit(solution)/shard_map/ppermute | solution.py:573
  232.3 4.1 %collective-permute-start.18 = (bf16[192,128]{1,0:T(8,128)(2,1)S(1)}, bf16[192,128]{1,0:T(8,128)(2,1)S(1)}, u32[]{:S(2)}, u32[]{:S(2)}) collective-permute-start(bf16[192,128]{1,0:T(8,128)(2,1)S(1)} %fusion.7.refs_0_), channel_id=1, source_target_pairs={{0,16},{8,24},{16,0},{24,8},{1,17},{9,25},{17,1},{25,9},{2,18},{10... | collective-permute-start | bytes 147464 | tf_op jit(solution)/shard_map/ppermute | solution.py:573
  232.8 4.1 %collective-permute-start.17 = (bf16[192,128]{1,0:T(8,128)(2,1)S(1)}, bf16[192,128]{1,0:T(8,128)(2,1)S(1)}, u32[]{:S(2)}, u32[]{:S(2)}) collective-permute-start(bf16[192,128]{1,0:T(8,128)(2,1)S(1)} %fusion.7.refs_0_), channel_id=1, source_target_pairs={{0,8},{8,0},{16,24},{24,16},{1,9},{9,1},{17,25},{25,17},{2,10},{10... | collective-permute-start | bytes 147464 | tf_op jit(solution)/shard_map/ppermute | solution.py:573
  235.2 1.7 copy-start.13
  236.4 0.6 copy-start.14
  237.0 0.6 copy-start.15

commit v5 on v4

--- a/solution.py
+++ b/solution.py
@@ -13,10 +13,15 @@
 LOW = jnp.bfloat16
 WIDE = jnp.float32
 TILE = 256
+BIG = 512
 LANES = 128
 GROUP = 4
 PARTS = 4
-VMEM_BYTES = 60 * 1024 * 1024
+ROOM = {
+    "source_rows": 16, "sent_rows": 8, "gather_sums": 14, "edge_update": 18, "output_block": 20,
+    "edge_update_back": 24, "scatter_quad": 14, "scatter_trip": 16, "source_back_quad": 16,
+    "source_back_trip": 18, "edge_grad": 12, "assemble_early": 8, "assemble_late": 8,
+}
 
 
 def sigma(v):
@@ -54,19 +59,23 @@
     return pl.BlockSpec((tile, width), lambda i: (i, 0))
 
 
-def cols(height):
-    return pl.BlockSpec((height, TILE), lambda i: (0, i))
+def cols(height, tile=TILE):
+    return pl.BlockSpec((height, tile), lambda i: (0, i))
 
 
 def fixed(*shape):
     return pl.BlockSpec(shape, lambda i: (0,) * len(shape))
 
 
-def call(body, name, steps, micros, ins, in_specs, outs, out_specs, scratch):
+def far_array(v):
+    return pltpu.with_memory_space_constraint(v, pltpu.HBM)
+
+
+def call(body, name, steps, micros, ins, in_specs, outs, out_specs, scratch, far=(), alias={}):
     return pl.pallas_call(
         body,
         name=name,
-        out_shape=[jax.ShapeDtypeStruct(s, t) for s, t in outs],
+        out_shape=[(pltpu.HBM if i in far else jax.ShapeDtypeStruct)(s, t) for i, (s, t) in enumerate(outs)],
         grid_spec=pltpu.PrefetchScalarGridSpec(
             num_scalar_prefetch=0,
             grid=(steps,),
@@ -74,8 +83,9 @@
             out_specs=out_specs,
             scratch_shapes=scratch,
         ),
+        input_output_aliases=alias,
         compiler_params=pltpu.CompilerParams(
-            dimension_semantics=("arbitrary",), vmem_limit_bytes=VMEM_BYTES
+            dimension_semantics=("arbitrary",), vmem_limit_bytes=ROOM[name] << 20
         ),
         cost_estimate=pl.CostEstimate(
             flops=int(micros * 1.1e9), transcendentals=0, bytes_accessed=1 << 22
@@ -330,7 +340,7 @@
     out = (edge[...].astype(WIDE) + (mixed + res2 * s) * HALF_ROOT) * HALF_ROOT
     merged[...] = out
     weighted = (out * nn(radial[...], wra[...])).astype(LOW)
-    hot_t = (lax.broadcasted_iota(jnp.int32, (atoms, TILE), 0) == trow[...]).astype(LOW)
+    hot_t = (lax.broadcasted_iota(jnp.int32, (atoms, edge.shape[0]), 0) == trow[...]).astype(LOW)
     part = nn(hot_t, weighted)
 
     @pl.when(step == 0)
@@ -369,7 +379,7 @@
         awc[...] = jnp.zeros_like(awc)
         aro[...] = jnp.zeros_like(aro)
 
-    hot_t = (lax.broadcasted_iota(jnp.int32, (atoms, TILE), 0) == trow[...]).astype(LOW)
+    hot_t = (lax.broadcasted_iota(jnp.int32, (atoms, merged.shape[0]), 0) == trow[...]).astype(LOW)
     spread = tn(jnp.concatenate([hot_t, hot_t], axis=0), both[...])
     gow = spread[:, 0:wide]
     m = merged[...]
@@ -427,7 +437,7 @@
         aup[...] = jnp.zeros_like(aup)
         abil[...] = jnp.zeros_like(abil)
 
-    hot_t = (lax.broadcasted_iota(jnp.int32, (pair // 2, TILE), 0) == trow[...]).astype(LOW)
+    hot_t = (lax.broadcasted_iota(jnp.int32, (pair // 2, edge.shape[0]), 0) == trow[...]).astype(LOW)
     gw = tn(jnp.concatenate([hot_t, hot_t], axis=0), gw2[...])
     gm = gmer[...] + gw * nn(radial[...], wra[...])
     ara[...] += tn(radial[...], (gw * merged[...]).astype(LOW))
@@ -533,7 +543,7 @@
         arad[...] = jnp.zeros_like(arad)
         adn[...] = jnp.zeros_like(adn)
 
-    place = lax.broadcasted_iota(jnp.int32, (TILE, asked.shape[1]), 0) + step * TILE
+    place = lax.broadcasted_iota(jnp.int32, (edge.shape[0], asked.shape[1]), 0) + step * edge.shape[0]
     back = nt(rt[0:n, :], (place == asked[...]).astype(LOW))
     v = down[low : low + n, :]
     ld = (grad[...] + back) * slope_of(v, sigma(v))
@@ -563,7 +573,9 @@
             emit(outs, parts, (asum, arad, adn), peers, inside)
 
 
-def edge_grad_body(gm, ls, l3, l4, wsk, ws3, ws4, gedge):
+def edge_grad_body(*refs):
+    gm, ls, l3, l4, wsk, ws3, ws4 = refs[:7]
+    gedge = refs[-1]
     total = gm[...] + nt(ls[...], wsk[...]) + nt(l3[...], ws3[...]) + nt(l4[...], ws4[...])
     gedge[...] = total.astype(LOW)
 
@@ -632,25 +644,38 @@
     slabs = (edges + ghosts_up) // TILE
 
     inside = fits(peers, rbf)
+    (
+        edge_embed, atom_embed, radial_basis, triplet_basis, quadruplet_basis, edge_cotangent,
+        w_source_trip, w_rbf_trip, w_source_quad, w_rbf_quad, w_skip, w_res_first, w_res_second, w_rbf_atom,
+        w_atom, w_concat, w_rbf_out, w_out, w_up_trip, w_up_quad, atom_cotangent, output_cotangent,
+    ) = map(far_array, (
+        edge_embed, atom_embed, radial_basis, triplet_basis, quadruplet_basis, edge_cotangent,
+        w_source_trip, w_rbf_trip, w_source_quad, w_rbf_quad, w_skip, w_res_first, w_res_second, w_rbf_atom,
+        w_atom, w_concat, w_rbf_out, w_out, w_up_trip, w_up_quad, atom_cotangent, output_cotangent,
+    ))
     far_ids = lax.all_to_all(borrowed_edges[0], "edge", split_axis=0, concat_axis=0, tiled=True)
 
-    i3, m3 = triplet_source_row.T, triplet_mask.T
-    i4, m4 = quadruplet_source_row.T, quadruplet_mask.T
-    wd3, wd4 = w_down_trip.T, w_down_quad.T
-    wb3, wb4 = triplet_bilinear_weight.T, w_bilinear_quad.T
-    trow = edge_target_atom
+    i3, m3, i4, m4, wd3, wd4, wb3, wb4 = [
+        far_array(v.T)
+        for v in (
+            triplet_source_row, triplet_mask, quadruplet_source_row, quadruplet_mask,
+            w_down_trip, w_down_quad, triplet_bilinear_weight, w_bilinear_quad,
+        )
+    ]
+    trow = far_array(edge_target_atom)
     sources = (w_source_trip, w_rbf_trip, wd3, w_source_quad, w_rbf_quad, wd4)
 
     table, down = call(
-        source_body, "source_rows", steps, 10, (edge_embed, radial_basis) + sources,
-        [rows(wide), rows(rbf)] + [whole(w) for w in sources],
-        [((nb, edges), LOW), ((nb, edges), WIDE)], [cols(nb), cols(nb)], [],
+        source_body, "source_rows", edges // BIG, 10, (edge_embed, radial_basis) + sources,
+        [rows(wide, BIG), rows(rbf, BIG)] + [whole(w) for w in sources],
+        [((nb, edges), LOW), ((nb, edges), WIDE)], [cols(nb, BIG), cols(nb, BIG)], [],
     )
     table, far_ids = lax.optimization_barrier((table, far_ids))
     sent, asked = call(
         sent_body, "sent_rows", 1, 2, (table, far_ids), [whole(table), whole(far_ids)],
-        [((ghosts, LANES), LOW), ((1, ghosts), jnp.int32)], [fixed(ghosts, LANES), fixed(1, ghosts)], [],
-    )
+        [((ghosts, LANES), LOW), ((1, ghosts), jnp.int32)], [fixed(ghosts, LANES), fixed(1, ghosts)], [], far=(1,),
+    )
+    asked = far_array(asked)
     ghost = exchange(sent, peers)
 
     s3, s4, p3, p4 = call(
@@ -665,35 +690,40 @@
             pltpu.VMEM((k3, n3, TILE), LOW), pltpu.VMEM((k4, n4, TILE), LOW),
             pltpu.VMEM((q3, TILE), WIDE), pltpu.VMEM((q4, TILE), WIDE),
         ],
+        far=(0, 1),
     )
 
     act = ((edges, wide), LOW)
     ups = (w_up_trip, w_up_quad, w_skip, w_res_first, w_res_second, w_rbf_atom)
     merged, mixlow, reshid, dsk, du3, du4, dr1, dr2, gath, anew, aslope = call(
-        mix_body, "edge_update", steps, 19,
+        mix_body, "edge_update", edges // BIG, 19,
         (edge_embed, radial_basis, p3, p4, trow) + ups + (w_atom, atom_embed),
-        [rows(wide), rows(rbf), cols(n3), cols(n4), cols(1)] + [whole(w) for w in ups + (w_atom, atom_embed)],
+        [rows(wide, BIG), rows(rbf, BIG), cols(n3, BIG), cols(n4, BIG), cols(1, BIG)] + [whole(w) for w in ups + (w_atom, atom_embed)],
         [((edges, wide), WIDE), act, act, act, act, act, act, act,
          ((atoms, wide), LOW), ((atoms, aw), LOW), ((atoms, aw), WIDE)],
-        [rows(wide)] * 8 + [fixed(atoms, wide), fixed(atoms, aw), fixed(atoms, aw)],
+        [rows(wide, BIG)] * 8 + [fixed(atoms, wide), fixed(atoms, aw), fixed(atoms, aw)],
         [pltpu.VMEM((atoms, wide), WIDE)],
-    )
+        far=(9,),
+    )
+    anew = far_array(anew)
 
     first_parts = (("rows", w_concat.shape), ("rows", (wide, 2 * aw)), ("rows", w_rbf_out.shape))
     outs = (w_concat, w_rbf_out, w_out, output_cotangent, atom_cotangent, aslope, gath, w_atom)
     shapes, specs = grad_outs(first_parts, peers, inside)
     enew, gmer, aout, gatom, gw2, *first = call(
-        functools.partial(out_body, parts=first_parts, peers=peers, inside=inside), "output_block", steps, 16,
+        functools.partial(out_body, parts=first_parts, peers=peers, inside=inside), "output_block", edges // BIG, 16,
         (merged, radial_basis, trow, anew, edge_cotangent) + outs,
-        [rows(wide), rows(rbf), cols(1), whole(anew), rows(wide)] + [whole(w) for w in outs],
+        [rows(wide, BIG), rows(rbf, BIG), cols(1, BIG), whole(anew), rows(wide, BIG)] + [whole(w) for w in outs],
         [act, ((edges, wide), WIDE), ((atoms, aw), LOW), ((atoms, aw), LOW), ((2 * atoms, wide), LOW)] + shapes,
-        [rows(wide), rows(wide), fixed(atoms, aw), fixed(atoms, aw), fixed(2 * atoms, wide)] + specs,
+        [rows(wide, BIG), rows(wide, BIG), fixed(atoms, aw), fixed(atoms, aw), fixed(2 * atoms, wide)] + specs,
         [
             pltpu.VMEM((atoms, wide), WIDE), pltpu.VMEM((atoms, wide), WIDE),
             pltpu.VMEM((2 * atoms, 2 * wide), LOW),
             pltpu.VMEM(w_concat.shape, WIDE), pltpu.VMEM(w_rbf_out.shape, WIDE), pltpu.VMEM((wide, 2 * aw), WIDE),
         ],
-    )
+        far=(0, 1, 2, 3),
+    )
+    gmer = far_array(gmer)
 
     square = w_skip.shape
     second_parts = (
@@ -706,15 +736,16 @@
         shapes, specs = grad_outs(second_parts, peers, inside)
     more = tuple(first) if inside else ()
     gmh, ls, lb3, lb4, *grads = call(
-        functools.partial(back_body, parts=second_parts, peers=peers, inside=inside), "edge_update_back", steps, 24,
+        functools.partial(back_body, parts=second_parts, peers=peers, inside=inside), "edge_update_back", edges // BIG, 24,
         (edge_embed, radial_basis, trow, s3, s4, merged, gmer, gw2, p3, p4, mixlow, reshid, dsk,
          du3, du4, dr1, dr2) + ups + more,
-        [rows(wide), rows(rbf), cols(1), cols(f3), cols(f4), rows(wide), rows(wide), whole(gw2),
-         cols(n3), cols(n4)] + [rows(wide)] * 7 + [whole(w) for w in ups + more],
+        [rows(wide, BIG), rows(rbf, BIG), cols(1, BIG), cols(f3, BIG), cols(f4, BIG), rows(wide, BIG), rows(wide, BIG), whole(gw2),
+         cols(n3, BIG), cols(n4, BIG)] + [rows(wide, BIG)] * 7 + [whole(w) for w in ups + more],
         [((edges, wide), WIDE), act, ((n3, edges), LOW), ((n4, edges), LOW)] + shapes,
-        [rows(wide), rows(wide), cols(n3), cols(n4)] + specs,
+        [rows(wide, BIG), rows(wide, BIG), cols(n3, BIG), cols(n4, BIG)] + specs,
         [pltpu.VMEM(square, WIDE)] * 3
         + [pltpu.VMEM(w_rbf_atom.shape, WIDE), pltpu.VMEM((nb, wide), WIDE), pltpu.VMEM((nb, f3), WIDE)],
+        far=(0, 2),
     )
     early_parts = first_parts + second_parts
     early = core_sum(*(grads if inside else pack(early_parts, tuple(first) + tuple(grads), peers)))
@@ -731,6 +762,7 @@
                 pltpu.VMEM((slabs * n, slots * TILE), LOW), pltpu.VMEM((TILE, slots * TILE), LOW),
                 pltpu.VMEM((f, n), LOW),
             ],
+            far=(0,),
         )
 
     third_parts = (("rows", square), ("rows", w_rbf_trip.shape))
@@ -747,37 +779,50 @@
         )
         ins = (ret, asked, ws, wr, wd) + more
         low_rows, *grads = call(
-            body, name, steps, 11, (edge_embed, radial_basis, grad, down) + ins,
-            [rows(wide), rows(rbf), cols(n), cols(nb)] + [whole(x) for x in ins],
-            [act] + shapes, [rows(wide)] + specs,
+            body, name, edges // BIG, 11, (edge_embed, radial_basis, grad, down) + ins,
+            [rows(wide, BIG), rows(rbf, BIG), cols(n, BIG), cols(nb, BIG)] + [whole(x) for x in ins],
+            [act] + shapes, [rows(wide, BIG)] + specs,
             [pltpu.VMEM(square, WIDE), pltpu.VMEM(w_rbf_trip.shape, WIDE), pltpu.VMEM((n, wide), WIDE),
              pltpu.VMEM((LANES, ghosts), LOW)],
+            far=() if before else (0, 1, 2),
         )
         return low_rows, grads
 
     grad4, far4 = scatter(lb4, i4, m4, quadruplet_basis, wb4, "scatter_quad", 11)
     lb3, far4, early = lax.optimization_barrier((lb3, far4, early))
+    lb3 = far_array(lb3)
     early = group_sum(early)
     ret4 = exchange(far4, peers)
     grad3, far3 = scatter(lb3, i3, m3, triplet_basis, wb3, "scatter_trip", 18)
+    grad3, grad4 = far_array(grad3), far_array(grad4)
     ret4, far3, early = lax.optimization_barrier((ret4, far3, early))
     ret3 = exchange(far3, peers)
     early = share_sum(early)
     l4, quads = source_back(grad4, ret4, w_source_quad, w_rbf_quad, wd4, n3, quad_parts, (), "source_back_quad")
     ret3, quads, early = lax.optimization_barrier((ret3, quads, early))
+    quads = [far_array(v) for v in quads] if inside else quads
     early = group_gather(early)
     l3, trips = source_back(grad3, ret3, w_source_trip, w_rbf_trip, wd3, 0, trip_parts, quads, "source_back_trip")
     late_parts = quad_parts + trip_parts
     late = trips if inside else pack(late_parts, tuple(quads) + tuple(trips), peers)
     late, gmh, early = lax.optimization_barrier((late, gmh, early))
     late = core_sum(*late)
+    gmh, l4 = far_array(gmh), far_array(l4)
     last = (w_skip, w_source_trip, w_source_quad)
-    (gedge,) = call(
-        edge_grad_body, "edge_grad", steps // 2, 6, (gmh, ls, l3, l4) + last,
-        [rows(wide, 2 * TILE)] * 4 + [whole(w) for w in last], [act], [rows(wide, 2 * TILE)], [],
-    )
-    late, gedge = lax.optimization_barrier((late, gedge))
-    late = group_gather(share_sum(group_sum(late)))
+    halves = 2
+    for half in range(halves):
+        first = half * edges // BIG // halves
+        block = pl.BlockSpec((BIG, wide), lambda i, first=first: (first + i, 0))
+        ins, extra, alias = (gmh, ls, l3, l4) + last, [], {}
+        if half:
+            ins, extra, alias = ins + (gedge,), [pl.BlockSpec(memory_space=pl.ANY)], {7: 0}
+        (gedge,) = call(
+            edge_grad_body, "edge_grad", edges // BIG // halves, 4, ins,
+            [block] * 4 + [whole(w) for w in last] + extra, [act], [block], [], far=(0,), alias=alias,
+        )
+        late, gedge = lax.optimization_barrier((late, gedge))
+        late = (group_sum, share_sum)[half](late)
+    late = group_gather(late)
 
     turned = tuple(("turned", shape) if kind == "cols" else (kind, shape) for kind, shape in trip_parts)
     r_concat, r_oa, r_out, r_sk, r_r1, r_r2, r_ra, r_up, r_bil = assemble(early, early_parts, peers, "assemble_early")

time: 241 us -> 212 us (0.88)
  Pallas kernels: 160 us -> 139 us
  local copies, waits for them, and re-layouts: 7.24 us -> 4.58 us
    pallas_call x13 -> x14, Pallas kernels: 160 us -> 139 us  [call(): pl.pallas_call(body, name=name, out_shape=[(pltpu.HBM if i in far else ja...]
    unnamed x32 -> x4, local copies, waits for them, and re-layouts: 3.18 us -> 0.01 us
  transfers between devices with their start and end apart: 23 -> 23, of which waited for: 9 -> 10; matrix products, arithmetic and copies ran while one was open for 2% -> 3% of each run, Pallas kernels for 30% -> 30%
where the time goes in v5:
time: 212 us
  Pallas kernels  139 us (66%)
  starting transfers between devices  36.8 us (17%)
  waiting for transfers between devices  16.2 us (8%)
  blocking collectives  10.6 us (5%)
  local copies, waits for them, and re-layouts  4.58 us (2%)
  other arithmetic  3.38 us (2%)
    pallas_call x14, Pallas kernels, call(): pl.pallas_call(body, name=name, out_shape=[(pltpu.HBM if i in far else ja...  139 us
    ppermute x20, starting transfers between devices, swap(): return lax.ppermute(v, axis, [(j, j ^ mask) for j in range(count)])  22.4 us
    ppermute x20, waiting for transfers between devices, swap(): return lax.ppermute(v, axis, [(j, j ^ mask) for j in range(count)])  16.2 us
    all_to_all x1, blocking collectives, exchange(): lax.all_to_all(parts, 'edge', split_axis=0, concat_axis=0, tiled=True)  10.6 us
    all_to_all x2, starting transfers between devices, exchange(): lax.all_to_all(parts, 'edge', split_axis=0, concat_axis=0, tiled=True)  8.08 us
    all_to_all x1, starting transfers between devices, per_device(): lax.all_to_all(borrowed_edges[0], 'edge', split_axis=0, concat_axis=0, ti...  6.37 us
  transfers between devices with their start and end apart: 23, of which 10 were waited for; matrix products, arithmetic and copies ran while one was open for 3% of the time, Pallas kernels for 30%

profile of v5, /device:TPU:0, one launch (start us, length us, event | category | flops | bytes accessed | tf_op | source)
XLA Modules:
  0.0 211.5 jit_solution(14104848122535805370)
XLA Ops:
  0.7 6.4 %all-to-all-start = ((s32[8,1,16]{2,1,0:T(1,128)}), s32[8,1,16]{2,1,0:T(1,128)S(1)}, u32[]{:S(2)}, u32[]{:S(2)}) async-start(s32[8,1,16]{2,1,0:T(1,128)} %bitcast.50), calls=%async_computation | async-start | bytes 8192 | tf_op jit(solution)/shard_map/all_to_all | solution.py:656
  7.0 7.2 %source_rows.1 = (bf16[96,2048]{1,0:T(8,128)(2,1)S(1)}, f32[96,2048]{1,0:T(8,128)S(1)}) custom-call(bf16[2048,512]{1,0:T(8,128)(2,1)} %edge.9, bf16[2048,128]{1,0:T(8,128)(2,1)} %radial.11, bf16[512,512]{1,0:T(8,128)(2,1)} %refs_5_.3, bf16[128,512]{1,0:T(8,128)(2,1)} %wr.3, bf16[64,512]{1,0:T(8,128)(2,1)} %bitcast.63, bf16[512,512]{1,0:T(8,128)(2,1)} %refs_6_.3, ...), custom_call_target="tpu_custom_call" | custom-call | flops 11000000512 | bytes 4194304 | tf_op jit(solution)/shard_map/source_rows/pallas_call | solution.py:75
  14.3 0.7 sent_rows.1
  15.0 10.6 %all_to_all.27 = bf16[8,16,128]{2,1,0:T(8,128)(2,1)S(1)} all-to-all(bf16[8,16,128]{2,1,0:T(8,128)(2,1)S(1)} %bitcast.48), channel_id=1, replica_groups=mesh['grp'=4,'edge'=8] {'edge'}, dimensions={0} | all-to-all | bytes 65536 | tf_op jit(solution)/shard_map/all_to_all | solution.py:619
  25.6 25.0 %gather_sums.1 = (bf16[1024,2048]{1,0:T(8,128)(2,1)}, bf16[1024,2048]{1,0:T(8,128)(2,1)}, f32[64,2048]{1,0:T(8,128)S(1)}, f32[32,2048]{1,0:T(8,128)S(1)}) custom-call(bf16[96,2048]{1,0:T(8,128)(2,1)S(1)} %get-tuple-element.104.table.tab, bf16[128,128]{1,0:T(8,128)(2,1)S(1)} %bitcast.47, s32[16,2048]{1,0:T(8,128)} %bitcast.51, s32[16,2048]{1,0:T(8,128)} %bitcast.53, ...), custom_call_target="tpu_custom_call" | custom-call | flops 27499999232 | bytes 4194304 | tf_op jit(solution)/shard_map/gather_sums/pallas_call | solution.py:75
  50.6 15.4 %edge_update.1 = (f32[2048,512]{1,0:T(8,128)S(1)}, bf16[2048,512]{1,0:T(8,128)(2,1)S(1)}, bf16[2048,512]{1,0:T(8,128)(2,1)S(1)}, bf16[2048,512]{1,0:T(8,128)(2,1...) custom-call(bf16[2048,512]{1,0:T(8,128)(2,1)} %edge.9, ...), custom_call_target="tpu_custom_call" | custom-call | flops 20899999744 | bytes 4194304 | tf_op jit(solution)/shard_map/edge_update/pallas_call | solution.py:75
  66.0 15.3 %output_block.1 = (bf16[2048,512]{1,0:T(8,128)(2,1)}, f32[2048,512]{1,0:T(8,128)}, bf16[128,256]{1,0:T(8,128)(2,1)}, bf16[128,256]{1,0:T(8,128)(2,1)}, bf16[256,...) custom-call(f32[2048,512]{1,0:T(8,128)S(1)} %get-tuple-element.109.merged, ...), custom_call_target="tpu_custom_call" | custom-call | flops 17600000000 | bytes 4194304 | tf_op jit(solution)/shard_map/output_block/pallas_call | solution.py:75
  81.3 18.7 %edge_update_back.1 = (f32[2048,512]{1,0:T(8,128)}, bf16[2048,512]{1,0:T(8,128)(2,1)S(1)}, bf16[64,2048]{1,0:T(8,128)(2,1)}, bf16[32,2048]{1,0:T(8,128)(2,1)S(1)...) custom-call(bf16[2048,512]{1,0:T(8,128)(2,1)} %edge.9, bf16[2048,128]{1,0:T(8,128)(2,1)} %radial.11, ...), custom_call_target="tpu_custom_call" | custom-call | flops 26400000000 | bytes 4194304 | tf_op jit(solution)/shard_map/edge_update_back/pallas_call | solution.py:75
  100.1 10.9 %scatter_quad.1 = (f32[32,2048]{1,0:T(8,128)}, bf16[128,128]{1,0:T(8,128)(2,1)}) custom-call(bf16[32,2048]{1,0:T(8,128)(2,1)S(1)} %get-tuple-element.129.lb, s32[8,2048]{1,0:T(8,128)} %bitcast.58, s32[8,2048]{1,0:T(8,128)} %bitcast.60, bf16[2048,256]{1,0:T(8,128)(2,1)} %basis.2, bf16[32,1024]{1,0:T(8,128)(2,1)} %bitcast.62), custom_call_target="tpu_custom_call" | custom-call | flops 12099999744 | bytes 4194304 | tf_op jit(solution)/shard_map/scatter_quad/pallas_call | solution.py:75
  110.9 1.7 add_convert_fusion
  112.6 3.3 %all-to-all-start.2 = ((bf16[8,16,128]{2,1,0:T(8,128)(2,1)}), bf16[8,16,128]{2,1,0:T(8,128)(2,1)S(1)}, u32[]{:S(2)}, u32[]{:S(2)}) async-start(bf16[8,16,128]{2,1,0:T(8,128)(2,1)} %bitcast.13), calls=%async_computation.2 | async-start | bytes 65536 | tf_op jit(solution)/shard_map/all_to_all | solution.py:619
  116.0 1.4 slice_bitcast_fusion.2
  117.4 1.5 collective-permute-start.1
  118.9 1.5 collective-permute-start.3
  120.9 17.7 %scatter_trip.1 = (f32[64,2048]{1,0:T(8,128)}, bf16[128,128]{1,0:T(8,128)(2,1)}) custom-call(bf16[64,2048]{1,0:T(8,128)(2,1)} %get-tuple-element.133.lb, s32[16,2048]{1,0:T(8,128)} %bitcast.52, s32[16,2048]{1,0:T(8,128)} %bitcast.54, bf16[2048,256]{1,0:T(8,128)(2,1)} %basis.3, bf16[64,1024]{1,0:T(8,128)(2,1)} %bitcast.56), custom_call_target="tpu_custom_call" | custom-call | flops 19800000512 | bytes 4194304 | tf_op jit(solution)/shard_map/scatter_trip/pallas_call | solution.py:75
  138.6 2.5 %collective-permute-done.3 = bf16[4,448,128]{2,1,0:T(8,128)(2,1)S(1)} collective-permute-done((bf16[4,448,128]{2,1,0:T(8,128)(2,1)S(1)}, bf16[4,448,128]{2,1,0:T(8,128)(2,1)S(1)}, u32[]{:S(2)}, u32[]{:S(2)}) %collective-permute-start.3) | collective-permute-done | bytes 458784 | tf_op jit(solution)/shard_map/ppermute | solution.py:585
  141.2 1.4 collective-permute-done.2
  142.5 1.3 fusion.2
  143.8 4.7 %all-to-all-start.3 = ((bf16[8,16,128]{2,1,0:T(8,128)(2,1)}), bf16[8,16,128]{2,1,0:T(8,128)(2,1)S(1)}, u32[]{:S(2)}, u32[]{:S(2)}) async-start(bf16[8,16,128]{2,1,0:T(8,128)(2,1)} %bitcast.19), calls=%async_computation.3 | async-start | bytes 65536 | tf_op jit(solution)/shard_map/all_to_all | solution.py:619
  148.6 2.1 collective-permute-start.4
  150.7 2.4 %collective-permute-start.6 = (bf16[1,448,128]{2,1,0:T(8,128)(2,1)S(1)}, bf16[1,448,128]{2,1,0:T(8,128)(2,1)S(1)}, u32[]{:S(2)}, u32[]{:S(2)}) collective-permute-start(bf16[1,448,128]{2,1,0:T(8,128)(2,1)S(1)} %get-tuple-element.190), channel_id=1, source_target_pairs={{0,6},{1,7},{2,4},{3,5},{4,2},{5,3},{6,0},{7,1},{8,14},{9,15},{10,... | collective-permute-start | bytes 344072 | tf_op jit(solution)/shard_map/ppermute | solution.py:585
  153.0 9.0 %source_back_quad.1 = (bf16[2048,512]{1,0:T(8,128)(2,1)}, bf16[4,4,96,128]{3,2,1,0:T(8,128)(2,1)}, bf16[4,4,96,128]{3,2,1,0:T(8,128)(2,1)}) custom-call(bf16[2048,512]{1,0:T(8,128)(2,1)} %edge.9, bf16[2048,128]{1,0:T(8,128)(2,1)} %radial.11, f32[32,2048]{1,0:T(8,128)} %get-tuple-element.140.grad, f32[96,2048]{1,0:T(8,128)S(1)} %get-tuple-element.135.down, ...), custom_call_target="tpu_custom_call" | custom-call | flops 12099999744 | bytes 4194304 | tf_op jit(solution)/shard_map/source_back_quad/pallas_call | solution.py:75
  162.1 1.7 collective-permute-done.5
  163.9 1.5 collective-permute-start.9
  165.4 1.5 collective-permute-start.8
  166.9 0.5 collective-permute-start.7
  167.4 8.3 %source_back_trip.1 = (bf16[2048,512]{1,0:T(8,128)(2,1)S(1)}, bf16[4,4,192,128]{3,2,1,0:T(8,128)(2,1)S(1)}, bf16[4,4,192,128]{3,2,1,0:T(8,128)(2,1)S(1)}) custom-call(bf16[2048,512]{1,0:T(8,128)(2,1)} %edge.9, bf16[2048,128]{1,0:T(8,128)(2,1)} %radial.11, f32[64,2048]{1,0:T(8,128)} %get-tuple-element.134.grad, f32[96,2048]{1,0:T(8,128)S(1)} %get-tuple-element.135.down, ...), custom_call_target="tpu_custom_call" | custom-call | flops 12099999744 | bytes 4194304 | tf_op jit(solution)/shard_map/source_back_trip/pallas_call | solution.py:75
  175.8 0.9 assemble_early.1
  176.7 0.7 fusion.10
  177.4 4.7 %edge_grad.2.refs_7_ = bf16[2048,512]{1,0:T(8,128)(2,1)} custom-call(f32[2048,512]{1,0:T(8,128)} %get-tuple-element.155.refs_0_, bf16[2048,512]{1,0:T(8,128)(2,1)S(1)} %get-tuple-element.156.refs_1_, bf16[2048,512]{1,0:T(8,128)(2,1)S(1)} %get-tuple-element.157.refs_2_, bf16[2048,512]{1,0:T(8,128)(2,1)} %get-tuple-element.158.refs_3_, ...), custom_call_target="tpu_custom_call" | custom-call | flops 4400000000 | bytes 4194304 | tf_op jit(solution)/shard_map/edge_grad/pallas_call | solution.py:75
  182.3 1.5 collective-permute-start.11
  184.3 1.5 collective-permute-start.12
  185.9 4.7 %edge_grad.3 = bf16[2048,512]{1,0:T(8,128)(2,1)} custom-call(f32[2048,512]{1,0:T(8,128)} %get-tuple-element.155.refs_0_, bf16[2048,512]{1,0:T(8,128)(2,1)S(1)} %get-tuple-element.156.refs_1_, bf16[2048,512]{1,0:T(8,128)(2,1)S(1)} %get-tuple-element.157.refs_2_, bf16[2048,512]{1,0:T(8,128)(2,1)} %get-tuple-element.158.refs_3_, ...), custom_call_target="tpu_custom_call", output_to_operand_aliasing={{}: (7, {})} | custom-call | flops 4400000000 | bytes 4194304 | tf_op jit(solution)/shard_map/edge_grad/pallas_call | solution.py:75
  190.5 3.4 %collective-permute-done.13 = bf16[4,192,128]{2,1,0:T(8,128)(2,1)S(1)} collective-permute-done((bf16[4,192,128]{2,1,0:T(8,128)(2,1)S(1)}, bf16[4,192,128]{2,1,0:T(8,128)(2,1)S(1)}, u32[]{:S(2)}, u32[]{:S(2)}) %collective-permute-start.13) | collective-permute-done | bytes 196640 | tf_op jit(solution)/shard_map/ppermute | solution.py:585
  193.9 1.4 collective-permute-done.12
  195.8 2.3 %collective-permute-start.16 = (bf16[1,192,128]{2,1,0:T(8,128)(2,1)S(1)}, bf16[1,192,128]{2,1,0:T(8,128)(2,1)S(1)}, u32[]{:S(2)}, u32[]{:S(2)}) collective-permute-start(bf16[1,192,128]{2,1,0:T(8,128)(2,1)S(1)} %get-tuple-element.193), channel_id=1, source_target_pairs={{0,6},{1,7},{2,4},{3,5},{4,2},{5,3},{6,0},{7,1},{8,14},{9,15},{10,... | collective-permute-start | bytes 147464 | tf_op jit(solution)/shard_map/ppermute | solution.py:585
  198.1 0.9 collective-permute-start.15
  199.0 0.6 slice_bitcast_fusion.6
  200.1 1.6 collective-permute-done.16
  201.7 2.0 collective-permute-done.15
  203.7 2.5 %collective-permute-start.19 = (bf16[192,128]{1,0:T(8,128)(2,1)S(1)}, bf16[192,128]{1,0:T(8,128)(2,1)S(1)}, u32[]{:S(2)}, u32[]{:S(2)}) collective-permute-start(bf16[192,128]{1,0:T(8,128)(2,1)S(1)} %fusion.7.refs_0_), channel_id=1, source_target_pairs={{0,24},{8,16},{16,8},{24,0},{1,25},{9,17},{17,9},{25,1},{2,26},{10... | collective-permute-start | bytes 147464 | tf_op jit(solution)/shard_map/ppermute | solution.py:585
  206.7 0.5 collective-permute-start.17
  207.2 0.6 slice_bitcast_fusion.7
  207.8 0.6 slice.93
  208.4 0.6 slice.91
  209.0 1.2 collective-permute-done.18.refs_2_
  210.3 0.5 collective-permute-done.17.refs_1_
  210.8 0.8 assemble_late.1
  (32 shorter events, 3.0 us)
Async XLA Ops:
  0.7 13.6 %all-to-all-start = ((s32[8,1,16]{2,1,0:T(1,128)}), s32[8,1,16]{2,1,0:T(1,128)S(1)}, u32[]{:S(2)}, u32[]{:S(2)}) async-start(s32[8,1,16]{2,1,0:T(1,128)} %bitcast.50), calls=%async_computation | async-start | bytes 8192 | tf_op jit(solution)/shard_map/all_to_all | solution.py:656
  66.0 15.3 %copy-start = (f32[2048,512]{1,0:T(8,128)}, f32[2048,512]{1,0:T(8,128)S(1)}, u32[]{:S(2)}) copy-start(f32[2048,512]{1,0:T(8,128)S(1)} %get-tuple-element.109.merged) | copy-start | bytes 12582916
  66.0 15.3 %copy-start.1 = (bf16[1024,2048]{1,0:T(8,128)(2,1)S(1)}, bf16[1024,2048]{1,0:T(8,128)(2,1)}, u32[]{:S(2)}) copy-start(bf16[1024,2048]{1,0:T(8,128)(2,1)} %get-tuple-element.115.s3) | copy-start | bytes 12582916
  100.0 10.9 %collective-permute-start = (bf16[4,4,448,128]{3,2,1,0:T(8,128)(2,1)S(1)}, bf16[4,4,448,128]{3,2,1,0:T(8,128)(2,1)S(1)}, u32[]{:S(2)}, u32[]{:S(2)}) collective-permute-start(bf16[4,4,448,128]{3,2,1,0:T(8,128)(2,1)S(1)} %get-tuple-element.132), channel_id=1, source_target_pairs={{0,1},{1,0},{2,3},{3,2},{4,5},{5,4},{6,7},{7,6},{8,9},{9,8},{10,11... | collective-permute-start | bytes 5505032 | tf_op jit(solution)/shard_map/ppermute | solution.py:585
  112.6 31.2 %all-to-all-start.2 = ((bf16[8,16,128]{2,1,0:T(8,128)(2,1)}), bf16[8,16,128]{2,1,0:T(8,128)(2,1)S(1)}, u32[]{:S(2)}, u32[]{:S(2)}) async-start(bf16[8,16,128]{2,1,0:T(8,128)(2,1)} %bitcast.13), calls=%async_computation.2 | async-start | bytes 65536 | tf_op jit(solution)/shard_map/all_to_all | solution.py:619
  117.4 21.2 %collective-permute-start.1 = (bf16[4,448,128]{2,1,0:T(8,128)(2,1)S(1)}, bf16[4,448,128]{2,1,0:T(8,128)(2,1)S(1)}, u32[]{:S(2)}, u32[]{:S(2)}) collective-permute-start(bf16[4,448,128]{2,1,0:T(8,128)(2,1)S(1)} %get-tuple-element.183), channel_id=1, source_target_pairs={{0,8},{8,0},{16,24},{24,16},{1,9},{9,1},{17,25},{25,17},{2,10},{10... | collective-permute-start | bytes 1376264 | tf_op jit(solution)/shard_map/ppermute | solution.py:585
  118.9 22.3 %collective-permute-start.3 = (bf16[4,448,128]{2,1,0:T(8,128)(2,1)S(1)}, bf16[4,448,128]{2,1,0:T(8,128)(2,1)S(1)}, u32[]{:S(2)}, u32[]{:S(2)}) collective-permute-start(bf16[4,448,128]{2,1,0:T(8,128)(2,1)S(1)} %get-tuple-element.184), channel_id=1, source_target_pairs={{0,24},{8,16},{16,8},{24,0},{1,25},{9,17},{17,9},{25,1},{2,26},{10... | collective-permute-start | bytes 1376264 | tf_op jit(solution)/shard_map/ppermute | solution.py:585
  120.4 22.1 %collective-permute-start.2 = (bf16[4,448,128]{2,1,0:T(8,128)(2,1)S(1)}, bf16[4,448,128]{2,1,0:T(8,128)(2,1)S(1)}, u32[]{:S(2)}, u32[]{:S(2)}) collective-permute-start(bf16[4,448,128]{2,1,0:T(8,128)(2,1)S(1)} %get-tuple-element.185), channel_id=1, source_target_pairs={{0,16},{8,24},{16,0},{24,8},{1,17},{9,25},{17,1},{25,9},{2,18},{10... | collective-permute-start | bytes 1376264 | tf_op jit(solution)/shard_map/ppermute | solution.py:585
  143.8 20.1 %all-to-all-start.3 = ((bf16[8,16,128]{2,1,0:T(8,128)(2,1)}), bf16[8,16,128]{2,1,0:T(8,128)(2,1)S(1)}, u32[]{:S(2)}, u32[]{:S(2)}) async-start(bf16[8,16,128]{2,1,0:T(8,128)(2,1)} %bitcast.19), calls=%async_computation.3 | async-start | bytes 65536 | tf_op jit(solution)/shard_map/all_to_all | solution.py:619
  148.6 13.5 %collective-permute-start.4 = (bf16[1,448,128]{2,1,0:T(8,128)(2,1)S(1)}, bf16[1,448,128]{2,1,0:T(8,128)(2,1)S(1)}, u32[]{:S(2)}, u32[]{:S(2)}) collective-permute-start(bf16[1,448,128]{2,1,0:T(8,128)(2,1)S(1)} %get-tuple-element.189), channel_id=1, source_target_pairs={{0,2},{1,3},{2,0},{3,1},{4,6},{5,7},{6,4},{7,5},{8,10},{9,11},{10,... | collective-permute-start | bytes 344072 | tf_op jit(solution)/shard_map/ppermute | solution.py:585
  150.7 11.4 %collective-permute-start.6 = (bf16[1,448,128]{2,1,0:T(8,128)(2,1)S(1)}, bf16[1,448,128]{2,1,0:T(8,128)(2,1)S(1)}, u32[]{:S(2)}, u32[]{:S(2)}) collective-permute-start(bf16[1,448,128]{2,1,0:T(8,128)(2,1)S(1)} %get-tuple-element.190), channel_id=1, source_target_pairs={{0,6},{1,7},{2,4},{3,5},{4,2},{5,3},{6,0},{7,1},{8,14},{9,15},{10,... | collective-permute-start | bytes 344072 | tf_op jit(solution)/shard_map/ppermute | solution.py:585
  153.0 10.8 %collective-permute-start.5 = (bf16[1,448,128]{2,1,0:T(8,128)(2,1)S(1)}, bf16[1,448,128]{2,1,0:T(8,128)(2,1)S(1)}, u32[]{:S(2)}, u32[]{:S(2)}) collective-permute-start(bf16[1,448,128]{2,1,0:T(8,128)(2,1)S(1)} %get-tuple-element.191), channel_id=1, source_target_pairs={{0,4},{1,5},{2,6},{3,7},{4,0},{5,1},{6,2},{7,3},{8,12},{9,13},{10,... | collective-permute-start | bytes 344072 | tf_op jit(solution)/shard_map/ppermute | solution.py:585
  163.9 11.9 %collective-permute-start.9 = (bf16[448,128]{1,0:T(8,128)(2,1)S(1)}, bf16[448,128]{1,0:T(8,128)(2,1)S(1)}, u32[]{:S(2)}, u32[]{:S(2)}) collective-permute-start(bf16[448,128]{1,0:T(8,128)(2,1)S(1)} %fusion.6.refs_0_), channel_id=1, source_target_pairs={{0,24},{8,16},{16,8},{24,0},{1,25},{9,17},{17,9},{25,1},{2,26},{10... | collective-permute-start | bytes 344072 | tf_op jit(solution)/shard_map/ppermute | solution.py:585
  165.4 10.4 %collective-permute-start.8 = (bf16[448,128]{1,0:T(8,128)(2,1)S(1)}, bf16[448,128]{1,0:T(8,128)(2,1)S(1)}, u32[]{:S(2)}, u32[]{:S(2)}) collective-permute-start(bf16[448,128]{1,0:T(8,128)(2,1)S(1)} %fusion.6.refs_0_), channel_id=1, source_target_pairs={{0,16},{8,24},{16,0},{24,8},{1,17},{9,25},{17,1},{25,9},{2,18},{10... | collective-permute-start | bytes 344072 | tf_op jit(solution)/shard_map/ppermute | solution.py:585
  166.9 8.9 %collective-permute-start.7 = (bf16[448,128]{1,0:T(8,128)(2,1)S(1)}, bf16[448,128]{1,0:T(8,128)(2,1)S(1)}, u32[]{:S(2)}, u32[]{:S(2)}) collective-permute-start(bf16[448,128]{1,0:T(8,128)(2,1)S(1)} %fusion.6.refs_0_), channel_id=1, source_target_pairs={{0,8},{8,0},{16,24},{24,16},{1,9},{9,1},{17,25},{25,17},{2,10},{10... | collective-permute-start | bytes 344072 | tf_op jit(solution)/shard_map/ppermute | solution.py:585
  175.8 6.3 %collective-permute-start.10 = (bf16[4,4,192,128]{3,2,1,0:T(8,128)(2,1)S(1)}, bf16[4,4,192,128]{3,2,1,0:T(8,128)(2,1)S(1)}, u32[]{:S(2)}, u32[]{:S(2)}) collective-permute-start(bf16[4,4,192,128]{3,2,1,0:T(8,128)(2,1)S(1)} %get-tuple-element.154), channel_id=1, source_target_pairs={{0,1},{1,0},{2,3},{3,2},{4,5},{5,4},{6,7},{7,6},{8,9},{9,8},{10,11... | collective-permute-start | bytes 2359304 | tf_op jit(solution)/shard_map/ppermute | solution.py:585
  182.3 8.2 %collective-permute-start.11 = (bf16[4,192,128]{2,1,0:T(8,128)(2,1)S(1)}, bf16[4,192,128]{2,1,0:T(8,128)(2,1)S(1)}, u32[]{:S(2)}, u32[]{:S(2)}) collective-permute-start(bf16[4,192,128]{2,1,0:T(8,128)(2,1)S(1)} %get-tuple-element.186), channel_id=1, source_target_pairs={{0,8},{8,0},{16,24},{24,16},{1,9},{9,1},{17,25},{25,17},{2,10},{10... | collective-permute-start | bytes 589832 | tf_op jit(solution)/shard_map/ppermute | solution.py:585
  183.8 10.1 %collective-permute-start.13 = (bf16[4,192,128]{2,1,0:T(8,128)(2,1)S(1)}, bf16[4,192,128]{2,1,0:T(8,128)(2,1)S(1)}, u32[]{:S(2)}, u32[]{:S(2)}) collective-permute-start(bf16[4,192,128]{2,1,0:T(8,128)(2,1)S(1)} %get-tuple-element.187), channel_id=1, source_target_pairs={{0,24},{8,16},{16,8},{24,0},{1,25},{9,17},{17,9},{25,1},{2,26},{10... | collective-permute-start | bytes 589832 | tf_op jit(solution)/shard_map/ppermute | solution.py:585
  184.3 10.9 %collective-permute-start.12 = (bf16[4,192,128]{2,1,0:T(8,128)(2,1)S(1)}, bf16[4,192,128]{2,1,0:T(8,128)(2,1)S(1)}, u32[]{:S(2)}, u32[]{:S(2)}) collective-permute-start(bf16[4,192,128]{2,1,0:T(8,128)(2,1)S(1)} %get-tuple-element.188), channel_id=1, source_target_pairs={{0,16},{8,24},{16,0},{24,8},{1,17},{9,25},{17,1},{25,9},{2,18},{10... | collective-permute-start | bytes 589832 | tf_op jit(solution)/shard_map/ppermute | solution.py:585
  195.4 4.7 %collective-permute-start.14 = (bf16[1,192,128]{2,1,0:T(8,128)(2,1)S(1)}, bf16[1,192,128]{2,1,0:T(8,128)(2,1)S(1)}, u32[]{:S(2)}, u32[]{:S(2)}) collective-permute-start(bf16[1,192,128]{2,1,0:T(8,128)(2,1)S(1)} %get-tuple-element.192), channel_id=1, source_target_pairs={{0,2},{1,3},{2,0},{3,1},{4,6},{5,7},{6,4},{7,5},{8,10},{9,11},{10,... | collective-permute-start | bytes 147464 | tf_op jit(solution)/shard_map/ppermute | solution.py:585
  195.8 5.9 %collective-permute-start.16 = (bf16[1,192,128]{2,1,0:T(8,128)(2,1)S(1)}, bf16[1,192,128]{2,1,0:T(8,128)(2,1)S(1)}, u32[]{:S(2)}, u32[]{:S(2)}) collective-permute-start(bf16[1,192,128]{2,1,0:T(8,128)(2,1)S(1)} %get-tuple-element.193), channel_id=1, source_target_pairs={{0,6},{1,7},{2,4},{3,5},{4,2},{5,3},{6,0},{7,1},{8,14},{9,15},{10,... | collective-permute-start | bytes 147464 | tf_op jit(solution)/shard_map/ppermute | solution.py:585
  198.1 5.5 %collective-permute-start.15 = (bf16[1,192,128]{2,1,0:T(8,128)(2,1)S(1)}, bf16[1,192,128]{2,1,0:T(8,128)(2,1)S(1)}, u32[]{:S(2)}, u32[]{:S(2)}) collective-permute-start(bf16[1,192,128]{2,1,0:T(8,128)(2,1)S(1)} %get-tuple-element.194), channel_id=1, source_target_pairs={{0,4},{1,5},{2,6},{3,7},{4,0},{5,1},{6,2},{7,3},{8,12},{9,13},{10,... | collective-permute-start | bytes 147464 | tf_op jit(solution)/shard_map/ppermute | solution.py:585
  203.7 5.4 %collective-permute-start.19 = (bf16[192,128]{1,0:T(8,128)(2,1)S(1)}, bf16[192,128]{1,0:T(8,128)(2,1)S(1)}, u32[]{:S(2)}, u32[]{:S(2)}) collective-permute-start(bf16[192,128]{1,0:T(8,128)(2,1)S(1)} %fusion.7.refs_0_), channel_id=1, source_target_pairs={{0,24},{8,16},{16,8},{24,0},{1,25},{9,17},{17,9},{25,1},{2,26},{10... | collective-permute-start | bytes 147464 | tf_op jit(solution)/shard_map/ppermute | solution.py:585
  206.2 4.1 %collective-permute-start.18 = (bf16[192,128]{1,0:T(8,128)(2,1)S(1)}, bf16[192,128]{1,0:T(8,128)(2,1)S(1)}, u32[]{:S(2)}, u32[]{:S(2)}) collective-permute-start(bf16[192,128]{1,0:T(8,128)(2,1)S(1)} %fusion.7.refs_0_), channel_id=1, source_target_pairs={{0,16},{8,24},{16,0},{24,8},{1,17},{9,25},{17,1},{25,9},{2,18},{10... | collective-permute-start | bytes 147464 | tf_op jit(solution)/shard_map/ppermute | solution.py:585
  206.7 4.1 %collective-permute-start.17 = (bf16[192,128]{1,0:T(8,128)(2,1)S(1)}, bf16[192,128]{1,0:T(8,128)(2,1)S(1)}, u32[]{:S(2)}, u32[]{:S(2)}) collective-permute-start(bf16[192,128]{1,0:T(8,128)(2,1)S(1)} %fusion.7.refs_0_), channel_id=1, source_target_pairs={{0,8},{8,0},{16,24},{24,16},{1,9},{9,1},{17,25},{25,17},{2,10},{10... | collective-permute-start | bytes 147464 | tf_op jit(solution)/shard_map/ppermute | solution.py:585

commit v6 on v5

--- a/solution.py
+++ b/solution.py
@@ -18,7 +18,7 @@
 GROUP = 4
 PARTS = 4
 ROOM = {
-    "source_rows": 16, "sent_rows": 8, "gather_sums": 14, "edge_update": 18, "output_block": 20,
+    "source_rows": 16, "sent_rows": 8, "skip_branch": 10, "gather_sums": 14, "edge_update": 18, "output_block": 20,
     "edge_update_back": 24, "scatter_quad": 14, "scatter_trip": 16, "source_back_quad": 16,
     "source_back_trip": 18, "edge_grad": 12, "assemble_early": 8, "assemble_late": 8,
 }
@@ -305,9 +305,16 @@
     p4[...] = nn(w4t[...], s4[...])
 
 
+def skip_body(edge, wsk, skip_out, dsk):
+    skip = nn(edge[...], wsk[...])
+    s = sigma(skip)
+    dsk[...] = slope_of(skip, s).astype(LOW)
+    skip_out[...] = (skip * s).astype(LOW)
+
+
 def mix_body(
-    edge, radial, p3, p4, trow, wu3, wu4, wsk, wr1, wr2, wra, wat, atom,
-    merged, mixlow, reshid, dsk, du3, du4, dr1, dr2, gath, anew, aslope, acc,
+    edge, radial, p3, p4, trow, skip, wu3, wu4, wr1, wr2, wra, wat, atom,
+    merged, mixlow, reshid, du3, du4, dr1, dr2, gath, anew, aslope, acc,
 ):
     step = pl.program_id(0)
     atoms = acc.shape[0]
@@ -322,11 +329,7 @@
     up4 = nn(h4, wu4[...])
     s = sigma(up4)
     du4[...] = slope_of(up4, s).astype(LOW)
-    total = total + up4 * s
-    skip = nn(edge[...], wsk[...])
-    s = sigma(skip)
-    dsk[...] = slope_of(skip, s).astype(LOW)
-    mixed = (total + skip * s) * THIRD_ROOT
+    mixed = (total + up4 * s + skip[...].astype(WIDE)) * THIRD_ROOT
     low_mixed = mixed.astype(LOW)
     mixlow[...] = low_mixed
     res = nn(low_mixed, wr1[...])
@@ -418,7 +421,7 @@
 
 def back_body(
     edge, radial, trow, s3, s4, merged, gmer, gw2, p3, p4, mixlow, reshid, dsk, du3, du4, dr1, dr2,
-    wu3, wu4, wsk, wr1, wr2, wra, *rest, parts, peers, inside,
+    wu3, wu4, wr1, wr2, wra, *rest, parts, peers, inside,
 ):
     if inside:
         before, rest = rest[:2], rest[2:]
@@ -677,6 +680,13 @@
     )
     asked = far_array(asked)
     ghost = exchange(sent, peers)
+    sent, later = lax.optimization_barrier((sent, w_skip))
+    act = ((edges, wide), LOW)
+    skip, dsk = call(
+        skip_body, "skip_branch", edges // BIG, 5, (edge_embed, far_array(later)),
+        [rows(wide, BIG), whole(w_skip)], [act, act], [rows(wide, BIG)] * 2, [], far=(0, 1),
+    )
+    skip, dsk = far_array(skip), far_array(dsk)
 
     s3, s4, p3, p4 = call(
         gather_body, "gather_sums", steps, 25,
@@ -693,17 +703,17 @@
         far=(0, 1),
     )
 
-    act = ((edges, wide), LOW)
-    ups = (w_up_trip, w_up_quad, w_skip, w_res_first, w_res_second, w_rbf_atom)
-    merged, mixlow, reshid, dsk, du3, du4, dr1, dr2, gath, anew, aslope = call(
+    s3, s4 = far_array(s3), far_array(s4)
+    ups = (w_up_trip, w_up_quad, w_res_first, w_res_second, w_rbf_atom)
+    merged, mixlow, reshid, du3, du4, dr1, dr2, gath, anew, aslope = call(
         mix_body, "edge_update", edges // BIG, 19,
-        (edge_embed, radial_basis, p3, p4, trow) + ups + (w_atom, atom_embed),
-        [rows(wide, BIG), rows(rbf, BIG), cols(n3, BIG), cols(n4, BIG), cols(1, BIG)] + [whole(w) for w in ups + (w_atom, atom_embed)],
-        [((edges, wide), WIDE), act, act, act, act, act, act, act,
+        (edge_embed, radial_basis, p3, p4, trow, skip) + ups + (w_atom, atom_embed),
+        [rows(wide, BIG), rows(rbf, BIG), cols(n3, BIG), cols(n4, BIG), cols(1, BIG), rows(wide, BIG)] + [whole(w) for w in ups + (w_atom, atom_embed)],
+        [((edges, wide), WIDE), act, act, act, act, act, act,
          ((atoms, wide), LOW), ((atoms, aw), LOW), ((atoms, aw), WIDE)],
-        [rows(wide, BIG)] * 8 + [fixed(atoms, wide), fixed(atoms, aw), fixed(atoms, aw)],
+        [rows(wide, BIG)] * 7 + [fixed(atoms, wide), fixed(atoms, aw), fixed(atoms, aw)],
         [pltpu.VMEM((atoms, wide), WIDE)],
-        far=(9,),
+        far=(8,),
     )
     anew = far_array(anew)
 

time: 212 us -> 211 us (level)
  blocking collectives: 10.6 us -> 0 us
  starting transfers between devices: 36.8 us -> 43.7 us
    all_to_all x1 -> x0, blocking collectives: 10.6 us -> none  [exchange(): lax.all_to_all(parts, 'edge', split_axis=0, concat_axis=0, tiled=True)]
    all_to_all x2 -> x3, starting transfers between devices: 8.08 us -> 14.5 us  [exchange(): lax.all_to_all(parts, 'edge', split_axis=0, concat_axis=0, tiled=True)]
    pallas_call x14 -> x15, Pallas kernels: 139 us -> 141 us  [call(): pl.pallas_call(body, name=name, out_shape=[(pltpu.HBM if i in far else ja...]
  transfers between devices with their start and end apart: 23 -> 24, of which waited for: 10 -> 11; matrix products, arithmetic and copies ran while one was open for 3% -> 3% of each run, Pallas kernels for 30% -> 33%
where the time goes in v6:
time: 211 us; the launch traced here: 210 us
  Pallas kernels  141 us (67%)
  starting transfers between devices  43.7 us (21%)
  waiting for transfers between devices  16.3 us (8%)
  local copies, waits for them, and re-layouts  4.56 us (2%)
  other arithmetic  3.38 us (2%)
    pallas_call x15, Pallas kernels, call(): pl.pallas_call(body, name=name, out_shape=[(pltpu.HBM if i in far else ja...  141 us
    ppermute x20, starting transfers between devices, swap(): return lax.ppermute(v, axis, [(j, j ^ mask) for j in range(count)])  22.8 us
    ppermute x20, waiting for transfers between devices, swap(): return lax.ppermute(v, axis, [(j, j ^ mask) for j in range(count)])  16.3 us
    all_to_all x3, starting transfers between devices, exchange(): lax.all_to_all(parts, 'edge', split_axis=0, concat_axis=0, tiled=True)  14.5 us
    all_to_all x1, starting transfers between devices, per_device(): lax.all_to_all(borrowed_edges[0], 'edge', split_axis=0, concat_axis=0, ti...  6.37 us
  transfers between devices with their start and end apart: 24, of which 11 were waited for; matrix products, arithmetic and copies ran while one was open for 3% of the time, Pallas kernels for 33%

profile of v6, /device:TPU:0, one launch (start us, length us, event | category | flops | bytes accessed | tf_op | source)
XLA Modules:
  0.0 210.2 jit_solution(1113915966631990641)
XLA Ops:
  0.7 6.4 %all-to-all-start = ((s32[8,1,16]{2,1,0:T(1,128)}), s32[8,1,16]{2,1,0:T(1,128)S(1)}, u32[]{:S(2)}, u32[]{:S(2)}) async-start(s32[8,1,16]{2,1,0:T(1,128)} %bitcast.49), calls=%async_computation | async-start | bytes 8192 | tf_op jit(solution)/shard_map/all_to_all | solution.py:659
  7.0 7.2 %source_rows.1 = (bf16[96,2048]{1,0:T(8,128)(2,1)S(1)}, f32[96,2048]{1,0:T(8,128)S(1)}) custom-call(bf16[2048,512]{1,0:T(8,128)(2,1)} %edge.11, bf16[2048,128]{1,0:T(8,128)(2,1)} %radial.11, bf16[512,512]{1,0:T(8,128)(2,1)} %refs_5_.3, bf16[128,512]{1,0:T(8,128)(2,1)} %wr.3, bf16[64,512]{1,0:T(8,128)(2,1)} %bitcast.62, bf16[512,512]{1,0:T(8,128)(2,1)} %refs_6_.3, ...), custom_call_target="tpu_custom_call" | custom-call | flops 11000000512 | bytes 4194304 | tf_op jit(solution)/shard_map/source_rows/pallas_call | solution.py:75
  14.3 1.0 sent_rows.1
  15.3 5.1 %all-to-all-start.1 = ((bf16[8,16,128]{2,1,0:T(8,128)(2,1)}), bf16[8,16,128]{2,1,0:T(8,128)(2,1)S(1)}, u32[]{:S(2)}, u32[]{:S(2)}) async-start(bf16[8,16,128]{2,1,0:T(8,128)(2,1)} %bitcast.5), calls=%async_computation.1 | async-start | bytes 65536 | tf_op jit(solution)/shard_map/all_to_all | solution.py:622
  20.4 5.7 %skip_branch.1 = (bf16[2048,512]{1,0:T(8,128)(2,1)}, bf16[2048,512]{1,0:T(8,128)(2,1)}) custom-call(bf16[2048,512]{1,0:T(8,128)(2,1)} %edge.11, bf16[512,512]{1,0:T(8,128)(2,1)} %refs_4_.3), custom_call_target="tpu_custom_call" | custom-call | flops 5500000256 | bytes 4194304 | tf_op jit(solution)/shard_map/skip_branch/pallas_call | solution.py:75
  26.2 25.1 %gather_sums.1 = (bf16[1024,2048]{1,0:T(8,128)(2,1)}, bf16[1024,2048]{1,0:T(8,128)(2,1)}, f32[64,2048]{1,0:T(8,128)S(1)}, f32[32,2048]{1,0:T(8,128)S(1)}) custom-call(bf16[96,2048]{1,0:T(8,128)(2,1)S(1)} %get-tuple-element.106.table.tab, bf16[128,128]{1,0:T(8,128)(2,1)S(1)} %bitcast.47, s32[16,2048]{1,0:T(8,128)} %bitcast.50, s32[16,2048]{1,0:T(8,128)} %bitcast.52, ...), custom_call_target="tpu_custom_call" | custom-call | flops 27499999232 | bytes 4194304 | tf_op jit(solution)/shard_map/gather_sums/pallas_call | solution.py:75
  51.2 13.4 %edge_update.1 = (f32[2048,512]{1,0:T(8,128)S(1)}, bf16[2048,512]{1,0:T(8,128)(2,1)S(1)}, bf16[2048,512]{1,0:T(8,128)(2,1)S(1)}, bf16[2048,512]{1,0:T(8,128)(2,1...) custom-call(bf16[2048,512]{1,0:T(8,128)(2,1)} %edge.11, ...), custom_call_target="tpu_custom_call" | custom-call | flops 20899999744 | bytes 4194304 | tf_op jit(solution)/shard_map/edge_update/pallas_call | solution.py:75
  64.7 13.7 %output_block.1 = (bf16[2048,512]{1,0:T(8,128)(2,1)}, f32[2048,512]{1,0:T(8,128)}, bf16[128,256]{1,0:T(8,128)(2,1)}, bf16[128,256]{1,0:T(8,128)(2,1)}, bf16[256,...) custom-call(f32[2048,512]{1,0:T(8,128)S(1)} %get-tuple-element.113.merged, ...), custom_call_target="tpu_custom_call" | custom-call | flops 17600000000 | bytes 4194304 | tf_op jit(solution)/shard_map/output_block/pallas_call | solution.py:75
  78.4 18.5 %edge_update_back.1 = (f32[2048,512]{1,0:T(8,128)}, bf16[2048,512]{1,0:T(8,128)(2,1)S(1)}, bf16[64,2048]{1,0:T(8,128)(2,1)}, bf16[32,2048]{1,0:T(8,128)(2,1)S(1)...) custom-call(bf16[2048,512]{1,0:T(8,128)(2,1)} %edge.11, bf16[2048,128]{1,0:T(8,128)(2,1)} %radial.11, ...), custom_call_target="tpu_custom_call" | custom-call | flops 26400000000 | bytes 4194304 | tf_op jit(solution)/shard_map/edge_update_back/pallas_call | solution.py:75
  97.4 10.8 %scatter_quad.1 = (f32[32,2048]{1,0:T(8,128)}, bf16[128,128]{1,0:T(8,128)(2,1)}) custom-call(bf16[32,2048]{1,0:T(8,128)(2,1)S(1)} %get-tuple-element.133.lb, s32[8,2048]{1,0:T(8,128)} %bitcast.57, s32[8,2048]{1,0:T(8,128)} %bitcast.59, bf16[2048,256]{1,0:T(8,128)(2,1)} %basis.2, bf16[32,1024]{1,0:T(8,128)(2,1)} %bitcast.61), custom_call_target="tpu_custom_call" | custom-call | flops 12099999744 | bytes 4194304 | tf_op jit(solution)/shard_map/scatter_quad/pallas_call | solution.py:75
  108.2 1.7 add_convert_fusion
  109.9 4.7 %all-to-all-start.2 = ((bf16[8,16,128]{2,1,0:T(8,128)(2,1)}), bf16[8,16,128]{2,1,0:T(8,128)(2,1)S(1)}, u32[]{:S(2)}, u32[]{:S(2)}) async-start(bf16[8,16,128]{2,1,0:T(8,128)(2,1)} %bitcast.13), calls=%async_computation.2 | async-start | bytes 65536 | tf_op jit(solution)/shard_map/all_to_all | solution.py:622
  114.6 1.4 slice_bitcast_fusion.2
  116.0 1.5 collective-permute-start.1
  117.5 1.5 collective-permute-start.3
  119.6 17.7 %scatter_trip.1 = (f32[64,2048]{1,0:T(8,128)}, bf16[128,128]{1,0:T(8,128)(2,1)}) custom-call(bf16[64,2048]{1,0:T(8,128)(2,1)} %get-tuple-element.137.lb, s32[16,2048]{1,0:T(8,128)} %bitcast.51, s32[16,2048]{1,0:T(8,128)} %bitcast.53, bf16[2048,256]{1,0:T(8,128)(2,1)} %basis.3, bf16[64,1024]{1,0:T(8,128)(2,1)} %bitcast.55), custom_call_target="tpu_custom_call" | custom-call | flops 19800000512 | bytes 4194304 | tf_op jit(solution)/shard_map/scatter_trip/pallas_call | solution.py:75
  137.2 2.6 %collective-permute-done.3 = bf16[4,448,128]{2,1,0:T(8,128)(2,1)S(1)} collective-permute-done((bf16[4,448,128]{2,1,0:T(8,128)(2,1)S(1)}, bf16[4,448,128]{2,1,0:T(8,128)(2,1)S(1)}, u32[]{:S(2)}, u32[]{:S(2)}) %collective-permute-start.3) | collective-permute-done | bytes 458784 | tf_op jit(solution)/shard_map/ppermute | solution.py:588
  139.9 1.4 collective-permute-done.2
  141.2 1.3 fusion.2
  142.5 4.7 %all-to-all-start.3 = ((bf16[8,16,128]{2,1,0:T(8,128)(2,1)}), bf16[8,16,128]{2,1,0:T(8,128)(2,1)S(1)}, u32[]{:S(2)}, u32[]{:S(2)}) async-start(bf16[8,16,128]{2,1,0:T(8,128)(2,1)} %bitcast.19), calls=%async_computation.3 | async-start | bytes 65536 | tf_op jit(solution)/shard_map/all_to_all | solution.py:622
  147.3 2.1 collective-permute-start.4
  149.4 2.4 %collective-permute-start.6 = (bf16[1,448,128]{2,1,0:T(8,128)(2,1)S(1)}, bf16[1,448,128]{2,1,0:T(8,128)(2,1)S(1)}, u32[]{:S(2)}, u32[]{:S(2)}) collective-permute-start(bf16[1,448,128]{2,1,0:T(8,128)(2,1)S(1)} %get-tuple-element.194), channel_id=1, source_target_pairs={{0,6},{1,7},{2,4},{3,5},{4,2},{5,3},{6,0},{7,1},{8,14},{9,15},{10,... | collective-permute-start | bytes 344072 | tf_op jit(solution)/shard_map/ppermute | solution.py:588
  151.7 9.0 %source_back_quad.1 = (bf16[2048,512]{1,0:T(8,128)(2,1)}, bf16[4,4,96,128]{3,2,1,0:T(8,128)(2,1)}, bf16[4,4,96,128]{3,2,1,0:T(8,128)(2,1)}) custom-call(bf16[2048,512]{1,0:T(8,128)(2,1)} %edge.11, bf16[2048,128]{1,0:T(8,128)(2,1)} %radial.11, f32[32,2048]{1,0:T(8,128)} %get-tuple-element.144.grad, f32[96,2048]{1,0:T(8,128)S(1)} %get-tuple-element.139.down, ...), custom_call_target="tpu_custom_call" | custom-call | flops 12099999744 | bytes 4194304 | tf_op jit(solution)/shard_map/source_back_quad/pallas_call | solution.py:75
  160.8 1.7 collective-permute-done.5
  162.6 1.5 collective-permute-start.9
  164.1 1.5 collective-permute-start.8
  165.6 0.5 collective-permute-start.7
  166.1 8.3 %source_back_trip.1 = (bf16[2048,512]{1,0:T(8,128)(2,1)S(1)}, bf16[4,4,192,128]{3,2,1,0:T(8,128)(2,1)S(1)}, bf16[4,4,192,128]{3,2,1,0:T(8,128)(2,1)S(1)}) custom-call(bf16[2048,512]{1,0:T(8,128)(2,1)} %edge.11, bf16[2048,128]{1,0:T(8,128)(2,1)} %radial.11, f32[64,2048]{1,0:T(8,128)} %get-tuple-element.138.grad, f32[96,2048]{1,0:T(8,128)S(1)} %get-tuple-element.139.down, ...), custom_call_target="tpu_custom_call" | custom-call | flops 12099999744 | bytes 4194304 | tf_op jit(solution)/shard_map/source_back_trip/pallas_call | solution.py:75
  174.5 0.9 assemble_early.1
  175.4 0.7 fusion.10
  176.1 4.7 %edge_grad.2.refs_7_ = bf16[2048,512]{1,0:T(8,128)(2,1)} custom-call(f32[2048,512]{1,0:T(8,128)} %get-tuple-element.159.refs_0_, bf16[2048,512]{1,0:T(8,128)(2,1)S(1)} %get-tuple-element.160.refs_1_, bf16[2048,512]{1,0:T(8,128)(2,1)S(1)} %get-tuple-element.161.refs_2_, bf16[2048,512]{1,0:T(8,128)(2,1)} %get-tuple-element.162.refs_3_, ...), custom_call_target="tpu_custom_call" | custom-call | flops 4400000000 | bytes 4194304 | tf_op jit(solution)/shard_map/edge_grad/pallas_call | solution.py:75
  181.0 1.6 collective-permute-start.11
  183.0 1.5 collective-permute-start.12
  184.6 4.7 %edge_grad.3 = bf16[2048,512]{1,0:T(8,128)(2,1)} custom-call(f32[2048,512]{1,0:T(8,128)} %get-tuple-element.159.refs_0_, bf16[2048,512]{1,0:T(8,128)(2,1)S(1)} %get-tuple-element.160.refs_1_, bf16[2048,512]{1,0:T(8,128)(2,1)S(1)} %get-tuple-element.161.refs_2_, bf16[2048,512]{1,0:T(8,128)(2,1)} %get-tuple-element.162.refs_3_, ...), custom_call_target="tpu_custom_call", output_to_operand_aliasing={{}: (7, {})} | custom-call | flops 4400000000 | bytes 4194304 | tf_op jit(solution)/shard_map/edge_grad/pallas_call | solution.py:75
  189.2 3.4 %collective-permute-done.13 = bf16[4,192,128]{2,1,0:T(8,128)(2,1)S(1)} collective-permute-done((bf16[4,192,128]{2,1,0:T(8,128)(2,1)S(1)}, bf16[4,192,128]{2,1,0:T(8,128)(2,1)S(1)}, u32[]{:S(2)}, u32[]{:S(2)}) %collective-permute-start.13) | collective-permute-done | bytes 196640 | tf_op jit(solution)/shard_map/ppermute | solution.py:588
  192.6 1.4 collective-permute-done.12
  194.4 2.4 %collective-permute-start.16 = (bf16[1,192,128]{2,1,0:T(8,128)(2,1)S(1)}, bf16[1,192,128]{2,1,0:T(8,128)(2,1)S(1)}, u32[]{:S(2)}, u32[]{:S(2)}) collective-permute-start(bf16[1,192,128]{2,1,0:T(8,128)(2,1)S(1)} %get-tuple-element.197), channel_id=1, source_target_pairs={{0,6},{1,7},{2,4},{3,5},{4,2},{5,3},{6,0},{7,1},{8,14},{9,15},{10,... | collective-permute-start | bytes 147464 | tf_op jit(solution)/shard_map/ppermute | solution.py:588
  196.8 0.9 collective-permute-start.15
  197.7 0.6 slice_bitcast_fusion.6
  198.8 1.5 collective-permute-done.16
  200.3 2.0 collective-permute-done.15
  202.4 2.5 %collective-permute-start.19 = (bf16[192,128]{1,0:T(8,128)(2,1)S(1)}, bf16[192,128]{1,0:T(8,128)(2,1)S(1)}, u32[]{:S(2)}, u32[]{:S(2)}) collective-permute-start(bf16[192,128]{1,0:T(8,128)(2,1)S(1)} %fusion.7.refs_0_), channel_id=1, source_target_pairs={{0,24},{8,16},{16,8},{24,0},{1,25},{9,17},{17,9},{25,1},{2,26},{10... | collective-permute-start | bytes 147464 | tf_op jit(solution)/shard_map/ppermute | solution.py:588
  205.4 0.6 collective-permute-start.17
  205.9 0.6 slice_bitcast_fusion.7
  206.5 0.6 slice.93
  207.1 0.6 slice.91
  207.8 1.2 collective-permute-done.18.refs_2_
  209.5 0.8 assemble_late.1
  (30 shorter events, 3.9 us)
Async XLA Ops:
  0.7 13.6 %all-to-all-start = ((s32[8,1,16]{2,1,0:T(1,128)}), s32[8,1,16]{2,1,0:T(1,128)S(1)}, u32[]{:S(2)}, u32[]{:S(2)}) async-start(s32[8,1,16]{2,1,0:T(1,128)} %bitcast.49), calls=%async_computation | async-start | bytes 8192 | tf_op jit(solution)/shard_map/all_to_all | solution.py:659
  15.3 10.8 %all-to-all-start.1 = ((bf16[8,16,128]{2,1,0:T(8,128)(2,1)}), bf16[8,16,128]{2,1,0:T(8,128)(2,1)S(1)}, u32[]{:S(2)}, u32[]{:S(2)}) async-start(bf16[8,16,128]{2,1,0:T(8,128)(2,1)} %bitcast.5), calls=%async_computation.1 | async-start | bytes 65536 | tf_op jit(solution)/shard_map/all_to_all | solution.py:622
  96.9 11.3 %collective-permute-start = (bf16[4,4,448,128]{3,2,1,0:T(8,128)(2,1)S(1)}, bf16[4,4,448,128]{3,2,1,0:T(8,128)(2,1)S(1)}, u32[]{:S(2)}, u32[]{:S(2)}) collective-permute-start(bf16[4,4,448,128]{3,2,1,0:T(8,128)(2,1)S(1)} %get-tuple-element.136), channel_id=1, source_target_pairs={{0,1},{1,0},{2,3},{3,2},{4,5},{5,4},{6,7},{7,6},{8,9},{9,8},{10,11... | collective-permute-start | bytes 5505032 | tf_op jit(solution)/shard_map/ppermute | solution.py:588
  109.9 32.6 %all-to-all-start.2 = ((bf16[8,16,128]{2,1,0:T(8,128)(2,1)}), bf16[8,16,128]{2,1,0:T(8,128)(2,1)S(1)}, u32[]{:S(2)}, u32[]{:S(2)}) async-start(bf16[8,16,128]{2,1,0:T(8,128)(2,1)} %bitcast.13), calls=%async_computation.2 | async-start | bytes 65536 | tf_op jit(solution)/shard_map/all_to_all | solution.py:622
  116.0 21.2 %collective-permute-start.1 = (bf16[4,448,128]{2,1,0:T(8,128)(2,1)S(1)}, bf16[4,448,128]{2,1,0:T(8,128)(2,1)S(1)}, u32[]{:S(2)}, u32[]{:S(2)}) collective-permute-start(bf16[4,448,128]{2,1,0:T(8,128)(2,1)S(1)} %get-tuple-element.187), channel_id=1, source_target_pairs={{0,8},{8,0},{16,24},{24,16},{1,9},{9,1},{17,25},{25,17},{2,10},{10... | collective-permute-start | bytes 1376264 | tf_op jit(solution)/shard_map/ppermute | solution.py:588
  117.5 22.3 %collective-permute-start.3 = (bf16[4,448,128]{2,1,0:T(8,128)(2,1)S(1)}, bf16[4,448,128]{2,1,0:T(8,128)(2,1)S(1)}, u32[]{:S(2)}, u32[]{:S(2)}) collective-permute-start(bf16[4,448,128]{2,1,0:T(8,128)(2,1)S(1)} %get-tuple-element.188), channel_id=1, source_target_pairs={{0,24},{8,16},{16,8},{24,0},{1,25},{9,17},{17,9},{25,1},{2,26},{10... | collective-permute-start | bytes 1376264 | tf_op jit(solution)/shard_map/ppermute | solution.py:588
  119.0 22.2 %collective-permute-start.2 = (bf16[4,448,128]{2,1,0:T(8,128)(2,1)S(1)}, bf16[4,448,128]{2,1,0:T(8,128)(2,1)S(1)}, u32[]{:S(2)}, u32[]{:S(2)}) collective-permute-start(bf16[4,448,128]{2,1,0:T(8,128)(2,1)S(1)} %get-tuple-element.189), channel_id=1, source_target_pairs={{0,16},{8,24},{16,0},{24,8},{1,17},{9,25},{17,1},{25,9},{2,18},{10... | collective-permute-start | bytes 1376264 | tf_op jit(solution)/shard_map/ppermute | solution.py:588
  142.5 20.1 %all-to-all-start.3 = ((bf16[8,16,128]{2,1,0:T(8,128)(2,1)}), bf16[8,16,128]{2,1,0:T(8,128)(2,1)S(1)}, u32[]{:S(2)}, u32[]{:S(2)}) async-start(bf16[8,16,128]{2,1,0:T(8,128)(2,1)} %bitcast.19), calls=%async_computation.3 | async-start | bytes 65536 | tf_op jit(solution)/shard_map/all_to_all | solution.py:622
  147.3 13.5 %collective-permute-start.4 = (bf16[1,448,128]{2,1,0:T(8,128)(2,1)S(1)}, bf16[1,448,128]{2,1,0:T(8,128)(2,1)S(1)}, u32[]{:S(2)}, u32[]{:S(2)}) collective-permute-start(bf16[1,448,128]{2,1,0:T(8,128)(2,1)S(1)} %get-tuple-element.193), channel_id=1, source_target_pairs={{0,2},{1,3},{2,0},{3,1},{4,6},{5,7},{6,4},{7,5},{8,10},{9,11},{10,... | collective-permute-start | bytes 344072 | tf_op jit(solution)/shard_map/ppermute | solution.py:588
  149.4 11.4 %collective-permute-start.6 = (bf16[1,448,128]{2,1,0:T(8,128)(2,1)S(1)}, bf16[1,448,128]{2,1,0:T(8,128)(2,1)S(1)}, u32[]{:S(2)}, u32[]{:S(2)}) collective-permute-start(bf16[1,448,128]{2,1,0:T(8,128)(2,1)S(1)} %get-tuple-element.194), channel_id=1, source_target_pairs={{0,6},{1,7},{2,4},{3,5},{4,2},{5,3},{6,0},{7,1},{8,14},{9,15},{10,... | collective-permute-start | bytes 344072 | tf_op jit(solution)/shard_map/ppermute | solution.py:588
  151.7 10.8 %collective-permute-start.5 = (bf16[1,448,128]{2,1,0:T(8,128)(2,1)S(1)}, bf16[1,448,128]{2,1,0:T(8,128)(2,1)S(1)}, u32[]{:S(2)}, u32[]{:S(2)}) collective-permute-start(bf16[1,448,128]{2,1,0:T(8,128)(2,1)S(1)} %get-tuple-element.195), channel_id=1, source_target_pairs={{0,4},{1,5},{2,6},{3,7},{4,0},{5,1},{6,2},{7,3},{8,12},{9,13},{10,... | collective-permute-start | bytes 344072 | tf_op jit(solution)/shard_map/ppermute | solution.py:588
  162.6 11.9 %collective-permute-start.9 = (bf16[448,128]{1,0:T(8,128)(2,1)S(1)}, bf16[448,128]{1,0:T(8,128)(2,1)S(1)}, u32[]{:S(2)}, u32[]{:S(2)}) collective-permute-start(bf16[448,128]{1,0:T(8,128)(2,1)S(1)} %fusion.6.refs_0_), channel_id=1, source_target_pairs={{0,24},{8,16},{16,8},{24,0},{1,25},{9,17},{17,9},{25,1},{2,26},{10... | collective-permute-start | bytes 344072 | tf_op jit(solution)/shard_map/ppermute | solution.py:588
  164.1 10.4 %collective-permute-start.8 = (bf16[448,128]{1,0:T(8,128)(2,1)S(1)}, bf16[448,128]{1,0:T(8,128)(2,1)S(1)}, u32[]{:S(2)}, u32[]{:S(2)}) collective-permute-start(bf16[448,128]{1,0:T(8,128)(2,1)S(1)} %fusion.6.refs_0_), channel_id=1, source_target_pairs={{0,16},{8,24},{16,0},{24,8},{1,17},{9,25},{17,1},{25,9},{2,18},{10... | collective-permute-start | bytes 344072 | tf_op jit(solution)/shard_map/ppermute | solution.py:588
  165.6 8.9 %collective-permute-start.7 = (bf16[448,128]{1,0:T(8,128)(2,1)S(1)}, bf16[448,128]{1,0:T(8,128)(2,1)S(1)}, u32[]{:S(2)}, u32[]{:S(2)}) collective-permute-start(bf16[448,128]{1,0:T(8,128)(2,1)S(1)} %fusion.6.refs_0_), channel_id=1, source_target_pairs={{0,8},{8,0},{16,24},{24,16},{1,9},{9,1},{17,25},{25,17},{2,10},{10... | collective-permute-start | bytes 344072 | tf_op jit(solution)/shard_map/ppermute | solution.py:588
  174.5 6.3 %collective-permute-start.10 = (bf16[4,4,192,128]{3,2,1,0:T(8,128)(2,1)S(1)}, bf16[4,4,192,128]{3,2,1,0:T(8,128)(2,1)S(1)}, u32[]{:S(2)}, u32[]{:S(2)}) collective-permute-start(bf16[4,4,192,128]{3,2,1,0:T(8,128)(2,1)S(1)} %get-tuple-element.158), channel_id=1, source_target_pairs={{0,1},{1,0},{2,3},{3,2},{4,5},{5,4},{6,7},{7,6},{8,9},{9,8},{10,11... | collective-permute-start | bytes 2359304 | tf_op jit(solution)/shard_map/ppermute | solution.py:588
  181.0 8.2 %collective-permute-start.11 = (bf16[4,192,128]{2,1,0:T(8,128)(2,1)S(1)}, bf16[4,192,128]{2,1,0:T(8,128)(2,1)S(1)}, u32[]{:S(2)}, u32[]{:S(2)}) collective-permute-start(bf16[4,192,128]{2,1,0:T(8,128)(2,1)S(1)} %get-tuple-element.190), channel_id=1, source_target_pairs={{0,8},{8,0},{16,24},{24,16},{1,9},{9,1},{17,25},{25,17},{2,10},{10... | collective-permute-start | bytes 589832 | tf_op jit(solution)/shard_map/ppermute | solution.py:588
  182.6 10.1 %collective-permute-start.13 = (bf16[4,192,128]{2,1,0:T(8,128)(2,1)S(1)}, bf16[4,192,128]{2,1,0:T(8,128)(2,1)S(1)}, u32[]{:S(2)}, u32[]{:S(2)}) collective-permute-start(bf16[4,192,128]{2,1,0:T(8,128)(2,1)S(1)} %get-tuple-element.191), channel_id=1, source_target_pairs={{0,24},{8,16},{16,8},{24,0},{1,25},{9,17},{17,9},{25,1},{2,26},{10... | collective-permute-start | bytes 589832 | tf_op jit(solution)/shard_map/ppermute | solution.py:588
  183.0 11.0 %collective-permute-start.12 = (bf16[4,192,128]{2,1,0:T(8,128)(2,1)S(1)}, bf16[4,192,128]{2,1,0:T(8,128)(2,1)S(1)}, u32[]{:S(2)}, u32[]{:S(2)}) collective-permute-start(bf16[4,192,128]{2,1,0:T(8,128)(2,1)S(1)} %get-tuple-element.192), channel_id=1, source_target_pairs={{0,16},{8,24},{16,0},{24,8},{1,17},{9,25},{17,1},{25,9},{2,18},{10... | collective-permute-start | bytes 589832 | tf_op jit(solution)/shard_map/ppermute | solution.py:588
  194.1 4.7 %collective-permute-start.14 = (bf16[1,192,128]{2,1,0:T(8,128)(2,1)S(1)}, bf16[1,192,128]{2,1,0:T(8,128)(2,1)S(1)}, u32[]{:S(2)}, u32[]{:S(2)}) collective-permute-start(bf16[1,192,128]{2,1,0:T(8,128)(2,1)S(1)} %get-tuple-element.196), channel_id=1, source_target_pairs={{0,2},{1,3},{2,0},{3,1},{4,6},{5,7},{6,4},{7,5},{8,10},{9,11},{10,... | collective-permute-start | bytes 147464 | tf_op jit(solution)/shard_map/ppermute | solution.py:588
  194.4 5.9 %collective-permute-start.16 = (bf16[1,192,128]{2,1,0:T(8,128)(2,1)S(1)}, bf16[1,192,128]{2,1,0:T(8,128)(2,1)S(1)}, u32[]{:S(2)}, u32[]{:S(2)}) collective-permute-start(bf16[1,192,128]{2,1,0:T(8,128)(2,1)S(1)} %get-tuple-element.197), channel_id=1, source_target_pairs={{0,6},{1,7},{2,4},{3,5},{4,2},{5,3},{6,0},{7,1},{8,14},{9,15},{10,... | collective-permute-start | bytes 147464 | tf_op jit(solution)/shard_map/ppermute | solution.py:588
  196.8 5.5 %collective-permute-start.15 = (bf16[1,192,128]{2,1,0:T(8,128)(2,1)S(1)}, bf16[1,192,128]{2,1,0:T(8,128)(2,1)S(1)}, u32[]{:S(2)}, u32[]{:S(2)}) collective-permute-start(bf16[1,192,128]{2,1,0:T(8,128)(2,1)S(1)} %get-tuple-element.198), channel_id=1, source_target_pairs={{0,4},{1,5},{2,6},{3,7},{4,0},{5,1},{6,2},{7,3},{8,12},{9,13},{10,... | collective-permute-start | bytes 147464 | tf_op jit(solution)/shard_map/ppermute | solution.py:588
  202.4 5.4 %collective-permute-start.19 = (bf16[192,128]{1,0:T(8,128)(2,1)S(1)}, bf16[192,128]{1,0:T(8,128)(2,1)S(1)}, u32[]{:S(2)}, u32[]{:S(2)}) collective-permute-start(bf16[192,128]{1,0:T(8,128)(2,1)S(1)} %fusion.7.refs_0_), channel_id=1, source_target_pairs={{0,24},{8,16},{16,8},{24,0},{1,25},{9,17},{17,9},{25,1},{2,26},{10... | collective-permute-start | bytes 147464 | tf_op jit(solution)/shard_map/ppermute | solution.py:588
  204.9 4.1 %collective-permute-start.18 = (bf16[192,128]{1,0:T(8,128)(2,1)S(1)}, bf16[192,128]{1,0:T(8,128)(2,1)S(1)}, u32[]{:S(2)}, u32[]{:S(2)}) collective-permute-start(bf16[192,128]{1,0:T(8,128)(2,1)S(1)} %fusion.7.refs_0_), channel_id=1, source_target_pairs={{0,16},{8,24},{16,0},{24,8},{1,17},{9,25},{17,1},{25,9},{2,18},{10... | collective-permute-start | bytes 147464 | tf_op jit(solution)/shard_map/ppermute | solution.py:588
  205.4 4.1 %collective-permute-start.17 = (bf16[192,128]{1,0:T(8,128)(2,1)S(1)}, bf16[192,128]{1,0:T(8,128)(2,1)S(1)}, u32[]{:S(2)}, u32[]{:S(2)}) collective-permute-start(bf16[192,128]{1,0:T(8,128)(2,1)S(1)} %fusion.7.refs_0_), channel_id=1, source_target_pairs={{0,8},{8,0},{16,24},{24,16},{1,9},{9,1},{17,25},{25,17},{2,10},{10... | collective-permute-start | bytes 147464 | tf_op jit(solution)/shard_map/ppermute | solution.py:588
